TPU v7x, 32 devices: a whole 2x2x4 slice. The times are simulated.
32 devices in a mesh: term: 4 (over y, x), sector: 8 (over z, core).
Axes of the slice: x: 2, y: 2, z: 4, core: 2. Of those that a mesh axis runs over, the one named last changes fastest.
Arguments:
- psi: bfloat16 [8, 8, 128, 128], P('sector'), may hold values from -6 to 6
- left_env: bfloat16 [8, 8, 128, 128], P('term', 'sector'), may hold values from -40 to 40
- right_env: bfloat16 [8, 8, 128, 128], P('term', 'sector'), may hold values from -4 to 4
- precond: bfloat16 [8, 8, 128, 128], P('sector'), may hold values from 0.5 to 4
- block_sizes: int32 [8], replicated, may hold values from 32 to 128, as said below
Outputs:
- state: bfloat16 [8, 8, 128, 128], P('sector')
- energy: float32 [3], replicated
Inputs may be any that keep to these rules, and one draw needn't show every extreme that they name: `block_sizes`: some sector has exactly 128 rows in every draw.
All inputs are finite; a program needn't handle non-finite values.
Results may differ from a plain program's by a relative error of at most 0.022.
Values may be sent and summed in bfloat16 or wider, within the bound.
No kernel may reach another device: no remote copies, remote signals or barrier semaphores. Data moves between devices by JAX's collectives and lax.ppermute only.
A program may use at most 128 MiB of HBM per device.

v0:
```python
import jax
import jax.numpy as jnp
from jax import lax
from jax.sharding import PartitionSpec as P

ITERS = 3


def block_mask(block_sizes, width, own_row):
    rows = jnp.arange(width)
    valid = rows[None, :] < block_sizes[:, None]
    own_valid = lax.dynamic_slice_in_dim(valid, own_row, 1, 0)[0]
    return (own_valid[None, :, None] & valid[:, None, :]).astype(jnp.float32)


def dot_sums(cur_share, img_share, pre_share, count):
    first = lax.psum(
        (jnp.sum(cur_share * cur_share), jnp.sum(cur_share * img_share)), ("term", "sector")
    )
    theta = first[1] / first[0]
    fresh = cur_share - (img_share - theta * cur_share) / pre_share
    squares = lax.psum(jnp.sum(fresh * fresh), ("term", "sector"))
    return (theta, lax.rsqrt(squares / count + 1e-06))


def local(psi, left_env, right_env, precond, block_sizes):
    sectors = block_sizes.shape[0]
    width = psi.shape[-1]
    own_row = lax.axis_index("sector")
    share = sectors // lax.axis_size("term")
    share_start = lax.axis_index("term") * share
    count = float(sectors * sectors * width * width)
    mask = block_mask(block_sizes, width, own_row)
    state = (psi[0].astype(jnp.float32) * mask).astype(jnp.bfloat16)
    scaling = precond[0].astype(jnp.float32)
    left_own = left_env[:, 0]

    def portion(values):
        return lax.dynamic_slice_in_dim(values, share_start, share, 0)

    right_all = lax.all_gather(right_env, "sector", axis=1, tiled=True)
    energies = []
    for step in range(ITERS):
        images = jnp.einsum(
            "jab,kjcb->kjac", state, right_all, preferred_element_type=jnp.float32
        ).astype(jnp.bfloat16)
        partial_value = jnp.einsum(
            "kac,kjcd->jad", left_own, images, preferred_element_type=jnp.float32
        )
        current = state.astype(jnp.float32)
        image = lax.psum(partial_value.astype(jnp.bfloat16), "term").astype(jnp.float32) * mask
        theta, factor = dot_sums(portion(current), portion(image), portion(scaling), count)
        fresh = current - (image - theta * current) / scaling
        state = (fresh * factor).astype(jnp.bfloat16)
        energies.append(theta)
    return (state[None], jnp.stack(energies))


def solution(mesh):
    in_specs = (
        P("sector", None, None, None),
        P("term", "sector", None, None),
        P("term", "sector", None, None),
        P("sector", None, None, None),
        P(),
    )
    out_specs = (P("sector", None, None, None), P())
    return jax.shard_map(local, mesh=mesh, in_specs=in_specs, out_specs=out_specs, check_vma=False)
```

profile of v0, /device:TPU:0, one launch (start us, length us, event | category | flops | bytes accessed | tf_op | source)
XLA Modules:
  0.0 424.9 jit_solution(16946019127858269423)
XLA Ops:
  7.2 0.6 copy-done.6
  7.9 0.1 iota_compare_fusion
  8.0 1.1 copy.7
  9.1 16.6 %all_gather.3 = bf16[2,8,128,128]{3,2,1,0:T(8,128)(2,1)S(1)} all-gather(bf16[2,1,128,128]{3,2,1,0:T(8,128)(2,1)S(1)} %copy-done.5), channel_id=1, replica_groups=mesh['term'=4,'sector'=8] {'sector'}, dimensions={1}, use_global_device_ids=true | all-gather | bytes 589824 | tf_op jit(solution)/shard_map/all_gather | solution.py:41
  25.7 1.2 fusion.8
  27.1 0.9 copy-done.4
  27.9 0.2 copy.8
  28.1 43.0 %all-reduce.7.cloned.1.call-done = bf16[8,128,128]{1,2,0:T(8,128)(2,1)} async-done(((bf16[8,128,128]{1,2,0:T(8,128)(2,1)}), bf16[8,128,128]{1,2,0:T(8,128)(2,1)}) %all-reduce.7.cloned.1.call-update) | async-done | bytes 262160 | tf_op jit(solution)/shard_map/psum | solution.py:51
  71.1 1.2 fusion.34
  72.3 0.6 multiply_reduce_fusion.4
  72.9 39.6 %all-reduce.2 = (f32[]{:T(128)}, f32[]{:T(128)}) all-reduce(f32[]{:T(128)} %get-tuple-element.9, f32[]{:T(128)} %get-tuple-element.8), channel_id=1, replica_groups=mesh['term'=4,'sector'=8] {'term','sector'}, use_global_device_ids=true, to_apply=%region_2.0 | all-reduce | flops 2 | bytes 16 | tf_op jit(solution)/shard_map/psum | solution.py:17
  113.9 0.7 fusion.43
  114.5 41.4 %psum.87 = f32[]{:T(128)} all-reduce(f32[]{:T(128)} %fusion.43), channel_id=1, replica_groups=mesh['term'=4,'sector'=8] {'term','sector'}, use_global_device_ids=true, to_apply=%region_6.0 | all-reduce | flops 1 | bytes 8 | tf_op jit(solution)/shard_map/psum | solution.py:22
  156.6 0.3 fusion.52
  156.9 1.2 fusion.7
  158.1 43.0 %all-reduce.9.cloned.1.call-done = bf16[8,128,128]{1,2,0:T(8,128)(2,1)} async-done(((bf16[8,128,128]{1,2,0:T(8,128)(2,1)}), bf16[8,128,128]{1,2,0:T(8,128)(2,1)}) %all-reduce.9.cloned.1.call-update) | async-done | bytes 262160 | tf_op jit(solution)/shard_map/psum | solution.py:51
  201.2 1.1 and_select_fusion.1
  202.3 0.6 multiply_reduce_fusion.2
  203.0 39.6 %all-reduce.1 = (f32[]{:T(128)}, f32[]{:T(128)}) all-reduce(f32[]{:T(128)} %get-tuple-element.7, f32[]{:T(128)} %get-tuple-element.6), channel_id=1, replica_groups=mesh['term'=4,'sector'=8] {'term','sector'}, use_global_device_ids=true, to_apply=%region_9.0 | all-reduce | flops 2 | bytes 16 | tf_op jit(solution)/shard_map/psum | solution.py:17
  243.9 0.7 fusion.42
  244.5 41.4 %psum.91 = f32[]{:T(128)} all-reduce(f32[]{:T(128)} %fusion.42), channel_id=1, replica_groups=mesh['term'=4,'sector'=8] {'term','sector'}, use_global_device_ids=true, to_apply=%region_13.0 | all-reduce | flops 1 | bytes 8 | tf_op jit(solution)/shard_map/psum | solution.py:22
  286.6 0.3 fusion.50
  286.9 1.2 fusion.6
  288.1 43.1 %all-reduce.11.cloned.1.call-done = bf16[8,128,128]{1,2,0:T(8,128)(2,1)} async-done(((bf16[8,128,128]{1,2,0:T(8,128)(2,1)}), bf16[8,128,128]{1,2,0:T(8,128)(2,1)}) %all-reduce.11.cloned.1.call-update) | async-done | bytes 262160 | tf_op jit(solution)/shard_map/psum | solution.py:51
  331.2 1.1 and_select_fusion
  332.3 0.6 multiply_reduce_fusion
  333.0 39.6 %all-reduce = (f32[]{:T(128)}, f32[]{:T(128)}) all-reduce(f32[]{:T(128)} %get-tuple-element.5, f32[]{:T(128)} %get-tuple-element.4), channel_id=1, replica_groups=mesh['term'=4,'sector'=8] {'term','sector'}, use_global_device_ids=true, to_apply=%region_16.0 | all-reduce | flops 2 | bytes 16 | tf_op jit(solution)/shard_map/psum | solution.py:17
  373.9 0.7 fusion.41
  374.5 41.4 %psum.95 = f32[]{:T(128)} all-reduce(f32[]{:T(128)} %fusion.41), channel_id=1, replica_groups=mesh['term'=4,'sector'=8] {'term','sector'}, use_global_device_ids=true, to_apply=%region_20.0 | all-reduce | flops 1 | bytes 8 | tf_op jit(solution)/shard_map/psum | solution.py:22
  416.6 0.3 fusion.31
  416.9 0.9 copy.9
  417.7 0.6 pad_maximum_fusion
  (20 shorter events, 0.2 us)
Async XLA Ops:
  7.2 18.6 %copy-start = (bf16[2,1,128,128]{3,2,1,0:T(8,128)(2,1)S(1)}, bf16[2,1,128,128]{3,2,1,0:T(8,128)(2,1)}, u32[]{:S(2)}) copy-start(bf16[2,1,128,128]{3,2,1,0:T(8,128)(2,1)} %param.6) | copy-start | bytes 196612
  7.2 64.0 %all-reduce.7.cloned.1.call-start = ((), (), s32[]{:S(2)}) async-start(), calls=%async_computation | async-start | bytes 524288 | tf_op jit(solution)/shard_map/psum | solution.py:51
  7.2 0.7 copy-start.6
  8.0 1.2 copy-start.5
  27.0 0.9 copy-start.4
  27.0 174.2 %all-reduce.9.cloned.1.call-start = ((), (), s32[]{:S(2)}) async-start(), calls=%async_computation.1 | async-start | bytes 524288 | tf_op jit(solution)/shard_map/psum | solution.py:51
  72.9 83.6 %copy-start.1 = (bf16[8,128,128]{1,2,0:T(8,128)(2,1)S(1)}, bf16[8,128,128]{1,2,0:T(8,128)(2,1)}, u32[]{:S(2)}) copy-start(bf16[8,128,128]{1,2,0:T(8,128)(2,1)} %all-reduce.7.cloned.1.call-done) | copy-start | bytes 786436
  158.1 173.1 %all-reduce.11.cloned.1.call-start = ((), (), s32[]{:S(2)}) async-start(), calls=%async_computation.2 | async-start | bytes 524288 | tf_op jit(solution)/shard_map/psum | solution.py:51
  203.0 83.6 %copy-start.3 = (bf16[8,128,128]{1,2,0:T(8,128)(2,1)S(1)}, bf16[8,128,128]{1,2,0:T(8,128)(2,1)}, u32[]{:S(2)}) copy-start(bf16[8,128,128]{1,2,0:T(8,128)(2,1)} %all-reduce.9.cloned.1.call-done) | copy-start | bytes 786436
  333.0 83.6 %copy-start.2 = (bf16[8,128,128]{1,2,0:T(8,128)(2,1)S(1)}, bf16[8,128,128]{1,2,0:T(8,128)(2,1)}, u32[]{:S(2)}) copy-start(bf16[8,128,128]{1,2,0:T(8,128)(2,1)} %all-reduce.11.cloned.1.call-done) | copy-start | bytes 786436
Sparse Core Ops, SparseCore 0:
  27.1 43.9 all-reduce.6
  158.2 42.9 all-reduce.8
  288.2 42.9 all-reduce.10
where the time goes:
time: 426 us; the launch traced here: 425 us
  blocking collectives  259 us (61%)
  waiting for transfers between devices  129 us (30%)
  between operations  20 us (5%)
  other arithmetic  8.96 us (2%)
    psum x3, waiting for transfers between devices, local(): lax.psum(partial_value.astype(jnp.bfloat16), 'term').astype(jnp.float32)  129 us
    psum x3, blocking collectives, dot_sums(): squares = lax.psum(jnp.sum(fresh * fresh), ('term', 'sector'))  124 us
    psum x3, blocking collectives, dot_sums(): lax.psum((jnp.sum(cur_share * cur_share), jnp.sum(cur_share * img_share))...  119 us
    all_gather x1, blocking collectives, local(): right_all = lax.all_gather(right_env, 'sector', axis=1, tiled=True)  16.6 us
  transfers between devices with their start and end apart: 3, of which 3 were waited for; matrix products, arithmetic and copies ran while one was open for 0% of the time, Pallas kernels for 0%

commit v1 on v0

v1 whole, which is shorter than its diff:
```python
import functools

import jax
import jax.numpy as jnp
from jax import lax
from jax.experimental import pallas as pl
from jax.experimental.pallas import tpu as pltpu
from jax.sharding import PartitionSpec as P

EPS = 1e-06
SCALE = 2.0**-12
UNSCALE = 2.0**12
ROWS = 64
LANES = 128

POWERS = ((0, 0), (0, 1), (1, 0), (1, 1))
N0, E0 = 0, 1
N1, E1 = 2, 5
N2, E2 = 8, 17
N3 = 26


def split(x):
    high = x.astype(jnp.bfloat16)
    low = (x - high.astype(jnp.float32)).astype(jnp.bfloat16)
    return jnp.concatenate([high, low], axis=1)


def fold(x):
    return functools.reduce(lambda a, b: a + b, [x[r : r + 8] for r in range(0, x.shape[0], 8)])


def main_kernel(
    where_ref, sizes_ref, psi_ref, pre_ref, got_ref, swap_ref, gram_ref, basis_ref, left_cat, right_cat, sums
):
    groups, depth, width = swap_ref.shape[1], swap_ref.shape[2], swap_ref.shape[-1]
    owners = got_ref.shape[0]
    terms = owners * depth
    term, core, row = where_ref[0], where_ref[1], where_ref[2]
    own_size = sizes_ref[row]
    sums[...] = jnp.zeros_like(sums)
    for k in range(terms):
        left_cat[:, k * width : (k + 1) * width] = got_ref[k // depth, groups, k % depth]

    def apply(vectors):
        columns = []
        for b in range(2):
            stacked = jnp.concatenate(vectors[b], axis=0)
            inner = stacked.shape[1]
            images = lax.dot_general(
                stacked,
                right_cat[b, :, :inner],
                (((1,), (1,)), ((), ())),
                preferred_element_type=jnp.float32,
            ).astype(jnp.bfloat16)
            for n in range(len(vectors[b])):
                rows = images[n * width : (n + 1) * width]
                columns.append(
                    jnp.concatenate([rows[:, k * width : (k + 1) * width] for k in range(terms)], axis=0)
                )
        out = jnp.dot(left_cat[...], jnp.concatenate(columns, axis=1), preferred_element_type=jnp.float32)
        count = len(vectors[0])
        return [
            [out[:, (b * count + n) * width : (b * count + n + 1) * width] for n in range(count)]
            for b in range(2)
        ]

    def add(slot, value):
        sums[slot * 8 : slot * 8 + 8] += value

    def group(g):
        for k in range(terms):
            rows = slice(k * width, (k + 1) * width)
            for half in range(2):
                cols = slice(half * width, (half + 1) * width)
                right_cat[0, rows, cols] = got_ref[k // depth, g, k % depth]
                right_cat[1, rows, cols] = swap_ref[k // depth, g, k % depth]
        row_ids = lax.broadcasted_iota(jnp.int32, (width, width), 0)
        col_ids = lax.broadcasted_iota(jnp.int32, (width, width), 1)
        start, inverse = [], []
        for b in range(2):
            block = (term * groups + g) * 2 + (core if b == 0 else 1 - core)
            valid = (row_ids < own_size) & (col_ids < sizes_ref[block])
            start.append(jnp.where(valid, psi_ref[block].astype(jnp.float32), 0.0))
            inverse.append(jnp.where(valid, 1.0 / pre_ref[block].astype(jnp.float32), 0.0))

        images = apply([[s.astype(jnp.bfloat16)] for s in start])
        first = []
        for b in range(2):
            s, h, inv = start[b], images[b][0], inverse[b]
            add(N0, fold(s * s))
            add(E0, fold(s * h))
            first.append([SCALE * s - (SCALE * inv) * h, inv * s])

        images = apply([[split(x) for x in first[b]] for b in range(2)])
        second = []
        for b in range(2):
            inv = inverse[b]
            for m in range(2):
                for n in range(2):
                    if m <= n:
                        scale = 1.0 if m == n else 2.0
                        add(N1 + m + n, scale * fold(first[b][m] * first[b][n]))
                    add(E1 + m + n, fold(first[b][m] * images[b][n]))
            level = []
            for x, h in zip(first[b], images[b]):
                level += [SCALE * x - (SCALE * inv) * h, inv * x]
            second.append(level)

        images = apply([[split(x) for x in second[b]] for b in range(2)])
        for b in range(2):
            inv = inverse[b]
            third = []
            for x, h in zip(second[b], images[b]):
                third.append((SCALE * x - (SCALE * inv) * h, inv * x))
            for m in range(4):
                for d in range(2):
                    basis_ref[2 * m + d, 2 * g + b] = third[m][d]
            norm = [None] * 9
            energy = [None] * 9
            last = [None] * 27

            def put(table, at, value):
                table[at] = value if table[at] is None else table[at] + value

            for m in range(4):
                for n in range(4):
                    a0, a1 = POWERS[m][0] + POWERS[n][0], POWERS[m][1] + POWERS[n][1]
                    put(energy, 3 * a0 + a1, fold(second[b][m] * images[b][n]))
                    for d in range(2):
                        for e in range(2):
                            if (m, d) <= (n, e):
                                scale = 1.0 if (m, d) == (n, e) else 2.0
                                put(last, 9 * a0 + 3 * a1 + d + e, scale * fold(third[m][d] * third[n][e]))
                    if m <= n:
                        scale = 1.0 if m == n else 2.0
                        put(norm, 3 * a0 + a1, scale * fold(second[b][m] * second[b][n]))
            for at in range(9):
                add(N2 + at, norm[at])
                add(E2 + at, energy[at])
            for at in range(27):
                add(N3 + at, last[at])

    if groups == 1:
        group(0)
    else:

        @pl.loop(0, groups)
        def _(g):
            group(g)

    folded = functools.reduce(lambda a, b: a + b, [sums[pl.ds(s, ROWS, stride=8), :] for s in range(8)])
    totals = jnp.sum(folded, axis=1, keepdims=True)
    row_ids = lax.broadcasted_iota(jnp.int32, (ROWS, LANES), 0)
    col_ids = lax.broadcasted_iota(jnp.int32, (ROWS, LANES), 1)
    line = jnp.sum(jnp.where(row_ids == col_ids, totals, 0.0), axis=0, keepdims=True)
    gram_ref[...] = jnp.broadcast_to(line, gram_ref.shape)


def finish_kernel(count, where_ref, gram_ref, basis_ref, out_ref, energy_ref):
    core = where_ref[1]
    share = basis_ref.shape[1]
    gram = jnp.sum(gram_ref[...], axis=0, keepdims=True)
    lane = lax.broadcasted_iota(jnp.int32, (1, LANES), 1)

    def total(base, size, weight):
        inside = (lane >= base) & (lane < base + size)
        return jnp.sum(jnp.where(inside, gram * weight, 0.0), axis=1, keepdims=True)

    def power(exponent, value):
        return jnp.where(exponent == 0, 1.0, jnp.where(exponent == 1, value, value * value))

    theta0 = total(E0, 1, 1.0) / total(N0, 1, 1.0)
    tau0 = SCALE * theta0
    norm1 = total(N1, 3, power(lane - N1, tau0))
    theta1 = total(E1, 3, power(lane - E1, tau0)) / norm1
    tau1 = SCALE * theta1

    def weight2(base):
        at = lane - base
        return power(at // 3, tau0) * power(at % 3, tau1)

    norm2 = total(N2, 9, weight2(N2))
    theta2 = total(E2, 9, weight2(E2)) / norm2
    tau2 = SCALE * theta2
    at = lane - N3
    norm3 = total(N3, 27, power(at // 9, tau0) * power(at // 3 % 3, tau1) * power(at % 3, tau2))

    def factor(gain, norm):
        return lax.rsqrt(gain * gain * jnp.maximum(norm, 0.0) / count + EPS)

    gain = jnp.full((1, 1), UNSCALE, jnp.float32)
    gain = factor(gain, norm1) * gain * UNSCALE
    gain = factor(gain, norm2) * gain * UNSCALE
    gain = factor(gain, norm3) * gain
    weights = [gain, gain * tau1, gain * tau0, gain * tau0 * tau1]
    for at in range(share):
        even = at % 2 == 0
        value = None
        for m in range(4):
            part = weights[m] * (basis_ref[2 * m, at] + tau2 * basis_ref[2 * m + 1, at])
            value = part if value is None else value + part
        block = (at // 2) * 2 + (core if even else 1 - core)
        for t in range(out_ref.shape[0]):
            out_ref[t, block] = value.astype(jnp.bfloat16)
    energy_ref[...] = jnp.where(lane == 0, theta0, jnp.where(lane == 1, theta1, theta2))


def gather_chips(right_own, sectors):
    chips = sectors // 2
    if chips > 8:
        everything = lax.all_gather(right_own, "sector")
        everything = everything.reshape((chips, 2) + right_own.shape)
        return lax.dynamic_index_in_dim(everything, lax.axis_index("sector") % 2, 1, keepdims=False)
    pieces = [right_own]
    for shift in range(1, chips):
        moves = [(i, (i + 2 * shift) % sectors) for i in range(sectors)]
        pieces.append(lax.ppermute(right_own, "sector", moves))
    mine = lax.axis_index("sector") // 2
    stacked = jnp.stack(pieces[::-1] + pieces[:0:-1])
    return lax.dynamic_slice_in_dim(stacked, chips - 1 - mine, chips, 0)


def local(sectors, psi, left_env, right_env, precond, block_sizes):
    owners = lax.axis_size("term")
    devices = owners * sectors
    depth, width = right_env.shape[0], right_env.shape[-1]
    groups = sectors // 2 // owners
    share = 2 * groups
    own = lax.axis_index("sector")
    where = jnp.stack([lax.axis_index("term"), own % 2, own]).astype(jnp.int32)

    by_chip = gather_chips(right_env[:, 0], sectors)
    by_chip = by_chip.reshape(owners, groups, depth, width, width)
    left = jnp.broadcast_to(left_env[:, 0], (owners, 1, depth, width, width))
    got = lax.all_to_all(jnp.concatenate([by_chip, left], axis=1), "term", 0, 0)
    swap = lax.ppermute(got[:, :groups], "sector", [(i, i ^ 1) for i in range(sectors)])

    smem = pl.BlockSpec(memory_space=pltpu.SMEM)
    vmem = pl.BlockSpec(memory_space=pltpu.VMEM)
    terms = owners * depth
    gram, basis = pl.pallas_call(
        main_kernel,
        out_shape=(
            jax.ShapeDtypeStruct((devices, LANES), jnp.float32),
            jax.ShapeDtypeStruct((8, share, width, width), jnp.float32),
        ),
        in_specs=[smem, smem, vmem, vmem, vmem, vmem],
        out_specs=(vmem, vmem),
        scratch_shapes=[
            pltpu.VMEM((width, terms * width), jnp.bfloat16),
            pltpu.VMEM((2, terms * width, 2 * width), jnp.bfloat16),
            pltpu.VMEM((ROWS * 8, LANES), jnp.float32),
        ],
        compiler_params=pltpu.CompilerParams(vmem_limit_bytes=48 << 20),
        name="levels",
    )(where, block_sizes, psi[0], precond[0], got, swap)
    gram = lax.all_to_all(gram, ("term", "sector"), 0, 0, tiled=True)
    count = float(sectors * sectors * width * width)
    blocks, energy = pl.pallas_call(
        functools.partial(finish_kernel, count),
        out_shape=(
            jax.ShapeDtypeStruct((owners, share, width, width), jnp.bfloat16),
            jax.ShapeDtypeStruct((1, LANES), jnp.float32),
        ),
        in_specs=[smem, vmem, vmem],
        out_specs=(vmem, vmem),
        compiler_params=pltpu.CompilerParams(vmem_limit_bytes=48 << 20),
        name="finish",
    )(where, gram, basis)
    state = lax.all_to_all(blocks, "term", 0, 0)
    return (state.reshape((1, sectors, width, width)), energy[0, :3])


def solution(mesh):
    in_specs = (
        P("sector", None, None, None),
        P("term", "sector", None, None),
        P("term", "sector", None, None),
        P("sector", None, None, None),
        P(),
    )
    out_specs = (P("sector", None, None, None), P())
    return jax.shard_map(
        functools.partial(local, mesh.shape["sector"]),
        mesh=mesh,
        in_specs=in_specs,
        out_specs=out_specs,
        check_vma=False,
    )
```

time: 426 us -> 52.4 us (0.12)
  blocking collectives: 259 us -> 20 us
  waiting for transfers between devices: 129 us -> 13.2 us
  between operations: 20 us -> 0.74 us
  starting transfers between devices: 0.12 us -> 9.59 us
  other arithmetic: 8.96 us -> 0.13 us
  Pallas kernels: 0 us -> 4.71 us
    psum x6 -> x0, blocking collectives: 243 us -> none  [the longest x3 124 us: dot_sums(): squares = lax.psum(jnp.sum(fresh * fresh), ('term', 'sector'))]
    psum x3 -> x0, waiting for transfers between devices: 129 us -> none  [local(): lax.psum(partial_value.astype(jnp.bfloat16), 'term').astype(jnp.float32)]
    all_to_all x0 -> x2, blocking collectives: none -> 20 us  [the longest x1 10.6 us: local(): got = lax.all_to_all(jnp.concatenate([by_chip, left], axis=1), 'term', 0, 0)]
    all_gather x1 -> x0, blocking collectives: 16.6 us -> none  [local(): right_all = lax.all_gather(right_env, 'sector', axis=1, tiled=True)]
    ppermute x0 -> x4, waiting for transfers between devices: none -> 8.08 us  [the longest x3 6.65 us: gather_chips(): pieces.append(lax.ppermute(right_own, 'sector', moves))]
    ppermute x0 -> x4, starting transfers between devices: none -> 6.19 us  [the longest x3 6.11 us: gather_chips(): pieces.append(lax.ppermute(right_own, 'sector', moves))]
    all_to_all x0 -> x1, waiting for transfers between devices: none -> 5.14 us  [local(): state = lax.all_to_all(blocks, 'term', 0, 0)]
    pallas_call x0 -> x2, Pallas kernels: none -> 4.71 us  [the longest x1 3.07 us: local(): pl.pallas_call(main_kernel, out_shape=(jax.ShapeDtypeStruct((devices, LAN...]
  transfers between devices with their start and end apart: 3 -> 5, of which waited for: 3 -> 4; matrix products, arithmetic and copies ran while one was open for 0% -> 1% of each run, Pallas kernels for 0% -> 0%
where the time goes in v1:
time: 52.4 us; the launch traced here: 52 us
  blocking collectives  20 us (38%)
  waiting for transfers between devices  13.2 us (25%)
  starting transfers between devices  9.59 us (18%)
  Pallas kernels  4.71 us (9%)
  local copies, waits for them, and re-layouts  3.65 us (7%)
  between operations  0.74 us (1%)
    all_to_all x1, blocking collectives, local(): got = lax.all_to_all(jnp.concatenate([by_chip, left], axis=1), 'term', 0, 0)  10.6 us
    all_to_all x1, blocking collectives, local(): gram = lax.all_to_all(gram, ('term', 'sector'), 0, 0, tiled=True)  9.35 us
    ppermute x3, waiting for transfers between devices, gather_chips(): pieces.append(lax.ppermute(right_own, 'sector', moves))  6.65 us
    ppermute x3, starting transfers between devices, gather_chips(): pieces.append(lax.ppermute(right_own, 'sector', moves))  6.11 us
    all_to_all x1, waiting for transfers between devices, local(): state = lax.all_to_all(blocks, 'term', 0, 0)  5.14 us
    all_to_all x1, starting transfers between devices, local(): state = lax.all_to_all(blocks, 'term', 0, 0)  3.41 us
    pallas_call x1, Pallas kernels, local(): pl.pallas_call(main_kernel, out_shape=(jax.ShapeDtypeStruct((devices, LAN...  3.07 us
    unnamed x17, local copies, waits for them, and re-layouts  3.04 us
  transfers between devices with their start and end apart: 5, of which 4 were waited for; matrix products, arithmetic and copies ran while one was open for 1% of the time, Pallas kernels for 0%

profile of v1, /device:TPU:0, one launch (start us, length us, event | category | flops | bytes accessed | tf_op | source)
XLA Modules:
  0.0 52.0 jit_solution(12640453578062846519)
XLA Ops:
  0.6 5.1 %collective-permute-start = (bf16[2,128,128]{2,1,0:T(8,128)(2,1)}, bf16[2,128,128]{2,1,0:T(8,128)(2,1)S(1)}, u32[]{:S(2)}, u32[]{:S(2)}) collective-permute-start(bf16[2,128,128]{2,1,0:T(8,128)(2,1)} %bitcast.33), channel_id=1, source_target_pairs={{0,6},{1,7},{2,0},{3,1},{4,2},{5,3},{6,4},{7,5},{8,14},{9,15},{10,... | collective-permute-start | bytes 196616 | tf_op jit(solution)/shard_map/ppermute | solution.py:218
  5.7 0.0 collective-permute-start.2
  5.7 1.0 %collective-permute-start.1 = (bf16[2,128,128]{2,1,0:T(8,128)(2,1)}, bf16[2,128,128]{2,1,0:T(8,128)(2,1)S(1)}, u32[]{:S(2)}, u32[]{:S(2)}) collective-permute-start(bf16[2,128,128]{2,1,0:T(8,128)(2,1)} %bitcast.35), channel_id=1, source_target_pairs={{0,4},{1,5},{2,6},{3,7},{4,0},{5,1},{6,2},{7,3},{8,12},{9,13},{10,... | collective-permute-start | bytes 196616 | tf_op jit(solution)/shard_map/ppermute | solution.py:218
  6.7 1.8 %collective-permute-done = bf16[2,128,128]{2,1,0:T(8,128)(2,1)S(1)} collective-permute-done((bf16[2,128,128]{2,1,0:T(8,128)(2,1)}, bf16[2,128,128]{2,1,0:T(8,128)(2,1)S(1)}, u32[]{:S(2)}, u32[]{:S(2)}) %collective-permute-start) | collective-permute-done | bytes 65568 | tf_op jit(solution)/shard_map/ppermute | solution.py:218
  8.6 4.8 %collective-permute-done.1 = bf16[2,128,128]{2,1,0:T(8,128)(2,1)S(1)} collective-permute-done((bf16[2,128,128]{2,1,0:T(8,128)(2,1)}, bf16[2,128,128]{2,1,0:T(8,128)(2,1)S(1)}, u32[]{:S(2)}, u32[]{:S(2)}) %collective-permute-start.1) | collective-permute-done | bytes 65568 | tf_op jit(solution)/shard_map/ppermute | solution.py:218
  13.4 0.0 copy-start.4
  13.4 0.0 collective-permute-done.2
  13.5 0.8 %copy-done.4 = bf16[2,1,128,128]{3,2,1,0:T(8,128)(2,1)S(1)} copy-done((bf16[2,1,128,128]{3,2,1,0:T(8,128)(2,1)S(1)}, bf16[2,1,128,128]{3,2,1,0:T(8,128)(2,1)}, u32[]{:S(2)}) %copy-start.4) | copy-done | bytes 65560
  14.3 0.0 copy-start.3
  14.4 0.8 %copy-done.3 = bf16[2,1,128,128]{3,2,1,0:T(8,128)(2,1)S(1)} copy-done((bf16[2,1,128,128]{3,2,1,0:T(8,128)(2,1)S(1)}, bf16[2,1,128,128]{3,2,1,0:T(8,128)(2,1)}, u32[]{:S(2)}) %copy-start.3) | copy-done | bytes 65560
  15.2 0.1 pad_maximum_fusion
  15.3 10.6 %all_to_all.21.got_ref = bf16[4,2,2,128,128]{4,3,2,1,0:T(8,128)(2,1)S(1)} all-to-all(bf16[4,2,2,128,128]{4,3,2,1,0:T(8,128)(2,1)S(1)} %pad_maximum_fusion), channel_id=1, replica_groups=mesh['term'=4,'sector'=8] {'term'}, dimensions={0} | all-to-all | bytes 1048576 | tf_op jit(solution)/shard_map/all_to_all | solution.py:236
  25.9 0.0 copy-start
  25.9 0.0 copy-start.1
  25.9 0.1 collective-permute-start.3
  26.0 0.1 pad_add_fusion.where_ref
  26.1 1.4 %collective-permute-done.3.swap_ref = bf16[4,1,2,128,128]{4,3,2,1,0:T(8,128)(2,1)S(1)} collective-permute-done((bf16[4,1,2,128,128]{4,3,2,1,0:T(8,128)(2,1)S(1)}, bf16[4,1,2,128,128]{4,3,2,1,0:T(8,128)(2,1)S(1)}, u32[]{:S(2)}, u32[]{:S(2)}) %collective-permute-start.3) | collective-permute-done | bytes 262176 | tf_op jit(solution)/shard_map/ppermute | solution.py:237
  27.5 0.0 copy-start.2
  27.5 0.0 copy-done
  27.5 0.0 copy-done.1
  27.5 0.6 %copy-done.2 = s32[8]{0:T(128)S(1)} copy-done((s32[8]{0:T(128)S(1)}, s32[8]{0:T(128)}, u32[]{:S(2)}) %copy-start.2) | copy-done | bytes 56
  28.2 3.1 %levels.1 = (f32[32,128]{1,0:T(8,128)S(1)}, f32[8,2,128,128]{3,2,1,0:T(8,128)S(1)}) custom-call(s32[3]{0:T(128)S(1)} %pad_add_fusion.where_ref, s32[8]{0:T(128)S(1)} %copy-done.2, bf16[8,128,128]{2,1,0:T(8,128)(2,1)S(1)} %bitcast.27, bf16[8,128,128]{2,1,0:T(8,128)(2,1)S(1)} %bitcast.28, bf16[4,2,2,128,128]{4,3,2,1,0:T(8,128)(2,1)S(1)} %all_to_all.21.got_ref, ...), custom_call_target="tpu_custom_call" | custom-call | tf_op jit(solution)/shard_map/levels/pallas_call | solution.py:242
  31.3 9.3 %all_to_all.22 = f32[32,1,128]{2,1,0:T(1,128)S(1)} all-to-all(f32[32,1,128]{2,1,0:T(1,128)S(1)} %bitcast.30), channel_id=1, replica_groups=mesh['term'=4,'sector'=8] {'term','sector'}, dimensions={0} | all-to-all | bytes 32768 | tf_op jit(solution)/shard_map/all_to_all | solution.py:258
  40.6 1.6 %finish.1 = (bf16[4,2,128,128]{3,2,1,0:T(8,128)(2,1)}, f32[1,128]{1,0:T(1,128)S(1)}) custom-call(s32[3]{0:T(128)S(1)} %pad_add_fusion.where_ref, f32[32,128]{1,0:T(8,128)S(1)} %bitcast.29, f32[8,2,128,128]{3,2,1,0:T(8,128)S(1)} %get-tuple-element.7.basis_ref), custom_call_target="tpu_custom_call" | custom-call | tf_op jit(solution)/shard_map/finish/pallas_call | solution.py:260
  42.3 3.4 %all-to-all-start.2 = ((bf16[4,2,128,128]{3,2,1,0:T(8,128)(2,1)}), bf16[4,2,128,128]{3,2,1,0:T(8,128)(2,1)S(1)}, u32[]{:S(2)}, u32[]{:S(2)}) async-start(bf16[4,2,128,128]{3,2,1,0:T(8,128)(2,1)} %get-tuple-element.8), calls=%async_computation.2 | async-start | bytes 524288 | tf_op jit(solution)/shard_map/all_to_all | solution.py:271
  45.7 0.5 slice_bitcast_fusion
  46.2 5.1 %all-to-all-done.2 = bf16[4,2,128,128]{3,2,1,0:T(8,128)(2,1)S(1)} async-done(((bf16[4,2,128,128]{3,2,1,0:T(8,128)(2,1)}), bf16[4,2,128,128]{3,2,1,0:T(8,128)(2,1)S(1)}, u32[]{:S(2)}, u32[]{:S(2)}) %all-to-all-start.2) | async-done | bytes 262176 | tf_op jit(solution)/shard_map/all_to_all | solution.py:271
  51.3 0.7 %copy.15 = bf16[1,8,128,128]{3,2,1,0:T(8,128)(2,1)} copy(bf16[1,8,128,128]{3,2,1,0:T(8,128)(2,1)S(1)} %bitcast.31) | data formatting | bytes 524288
  (10 shorter events, 0.2 us)
Async XLA Ops:
  0.6 7.9 %collective-permute-start = (bf16[2,128,128]{2,1,0:T(8,128)(2,1)}, bf16[2,128,128]{2,1,0:T(8,128)(2,1)S(1)}, u32[]{:S(2)}, u32[]{:S(2)}) collective-permute-start(bf16[2,128,128]{2,1,0:T(8,128)(2,1)} %bitcast.33), channel_id=1, source_target_pairs={{0,6},{1,7},{2,0},{3,1},{4,2},{5,3},{6,4},{7,5},{8,14},{9,15},{10,... | collective-permute-start | bytes 196616 | tf_op jit(solution)/shard_map/ppermute | solution.py:218
  5.7 7.7 %collective-permute-start.2 = (bf16[2,128,128]{2,1,0:T(8,128)(2,1)}, bf16[2,128,128]{2,1,0:T(8,128)(2,1)S(1)}, u32[]{:S(2)}, u32[]{:S(2)}) collective-permute-start(bf16[2,128,128]{2,1,0:T(8,128)(2,1)} %bitcast.34), channel_id=1, source_target_pairs={{0,2},{1,3},{2,4},{3,5},{4,6},{5,7},{6,0},{7,1},{8,10},{9,11},{10,... | collective-permute-start | bytes 196616 | tf_op jit(solution)/shard_map/ppermute | solution.py:218
  5.7 7.7 %collective-permute-start.1 = (bf16[2,128,128]{2,1,0:T(8,128)(2,1)}, bf16[2,128,128]{2,1,0:T(8,128)(2,1)S(1)}, u32[]{:S(2)}, u32[]{:S(2)}) collective-permute-start(bf16[2,128,128]{2,1,0:T(8,128)(2,1)} %bitcast.35), channel_id=1, source_target_pairs={{0,4},{1,5},{2,6},{3,7},{4,0},{5,1},{6,2},{7,3},{8,12},{9,13},{10,... | collective-permute-start | bytes 196616 | tf_op jit(solution)/shard_map/ppermute | solution.py:218
  13.4 0.8 %copy-start.4 = (bf16[2,1,128,128]{3,2,1,0:T(8,128)(2,1)S(1)}, bf16[2,1,128,128]{3,2,1,0:T(8,128)(2,1)}, u32[]{:S(2)}) copy-start(bf16[2,1,128,128]{3,2,1,0:T(8,128)(2,1)} %param.7) | copy-start | bytes 196612
  14.3 0.8 %copy-start.3 = (bf16[2,1,128,128]{3,2,1,0:T(8,128)(2,1)S(1)}, bf16[2,1,128,128]{3,2,1,0:T(8,128)(2,1)}, u32[]{:S(2)}) copy-start(bf16[2,1,128,128]{3,2,1,0:T(8,128)(2,1)} %param.6) | copy-start | bytes 196612
  25.9 1.6 %copy-start = (bf16[1,8,128,128]{3,2,1,0:T(8,128)(2,1)S(1)}, bf16[1,8,128,128]{3,2,1,0:T(8,128)(2,1)}, u32[]{:S(2)}) copy-start(bf16[1,8,128,128]{3,2,1,0:T(8,128)(2,1)} %param.5) | copy-start | bytes 786436
  25.9 1.6 %copy-start.1 = (bf16[1,8,128,128]{3,2,1,0:T(8,128)(2,1)S(1)}, bf16[1,8,128,128]{3,2,1,0:T(8,128)(2,1)}, u32[]{:S(2)}) copy-start(bf16[1,8,128,128]{3,2,1,0:T(8,128)(2,1)} %param.8) | copy-start | bytes 786436
  25.9 1.6 %collective-permute-start.3 = (bf16[4,1,2,128,128]{4,3,2,1,0:T(8,128)(2,1)S(1)}, bf16[4,1,2,128,128]{4,3,2,1,0:T(8,128)(2,1)S(1)}, u32[]{:S(2)}, u32[]{:S(2)}) collective-permute-start(bf16[4,1,2,128,128]{4,3,2,1,0:T(8,128)(2,1)S(1)} %slice.8), channel_id=1, source_target_pairs={{0,1},{1,0},{2,3},{3,2},{4,5},{5,4},{6,7},{7,6},{8,9},{9,8},{10,11... | collective-permute-start | bytes 786440 | tf_op jit(solution)/shard_map/ppermute | solution.py:237
  27.5 0.7 %copy-start.2 = (s32[8]{0:T(128)S(1)}, s32[8]{0:T(128)}, u32[]{:S(2)}) copy-start(s32[8]{0:T(128)} %sizes_ref.1) | copy-start | bytes 100
  42.3 9.1 %all-to-all-start.2 = ((bf16[4,2,128,128]{3,2,1,0:T(8,128)(2,1)}), bf16[4,2,128,128]{3,2,1,0:T(8,128)(2,1)S(1)}, u32[]{:S(2)}, u32[]{:S(2)}) async-start(bf16[4,2,128,128]{3,2,1,0:T(8,128)(2,1)} %get-tuple-element.8), calls=%async_computation.2 | async-start | bytes 524288 | tf_op jit(solution)/shard_map/all_to_all | solution.py:271

commit v2 on v1

--- a/solution.py
+++ b/solution.py
@@ -30,17 +30,19 @@
     return functools.reduce(lambda a, b: a + b, [x[r : r + 8] for r in range(0, x.shape[0], 8)])
 
 
-def main_kernel(
-    where_ref, sizes_ref, psi_ref, pre_ref, got_ref, swap_ref, gram_ref, basis_ref, left_cat, right_cat, sums
-):
-    groups, depth, width = swap_ref.shape[1], swap_ref.shape[2], swap_ref.shape[-1]
-    owners = got_ref.shape[0]
+def main_kernel(plan, sizes_ref, psi_ref, pre_ref, *refs):
+    owners = plan.owners
+    left_refs, own_refs, swap_refs = refs[:owners], refs[owners : 2 * owners], refs[2 * owners : 3 * owners]
+    gram_ref, basis_ref, left_cat, right_cat, sums = refs[3 * owners :]
+    groups, depth, width = own_refs[0].shape[0], own_refs[0].shape[1], own_refs[0].shape[-1]
     terms = owners * depth
-    term, core, row = where_ref[0], where_ref[1], where_ref[2]
+    row = lax.axis_index("sector")
+    core = row % 2
+    chip = plan.first_chip(lax.axis_index("term"), row // 2)
     own_size = sizes_ref[row]
     sums[...] = jnp.zeros_like(sums)
     for k in range(terms):
-        left_cat[:, k * width : (k + 1) * width] = got_ref[k // depth, groups, k % depth]
+        left_cat[:, k * width : (k + 1) * width] = left_refs[k // depth][k % depth]
 
     def apply(vectors):
         columns = []
@@ -73,13 +75,13 @@
             rows = slice(k * width, (k + 1) * width)
             for half in range(2):
                 cols = slice(half * width, (half + 1) * width)
-                right_cat[0, rows, cols] = got_ref[k // depth, g, k % depth]
-                right_cat[1, rows, cols] = swap_ref[k // depth, g, k % depth]
+                right_cat[0, rows, cols] = own_refs[k // depth][g, k % depth]
+                right_cat[1, rows, cols] = swap_refs[k // depth][g, k % depth]
         row_ids = lax.broadcasted_iota(jnp.int32, (width, width), 0)
         col_ids = lax.broadcasted_iota(jnp.int32, (width, width), 1)
         start, inverse = [], []
         for b in range(2):
-            block = (term * groups + g) * 2 + (core if b == 0 else 1 - core)
+            block = (chip + g) * 2 + (core if b == 0 else 1 - core)
             valid = (row_ids < own_size) & (col_ids < sizes_ref[block])
             start.append(jnp.where(valid, psi_ref[block].astype(jnp.float32), 0.0))
             inverse.append(jnp.where(valid, 1.0 / pre_ref[block].astype(jnp.float32), 0.0))
@@ -157,8 +159,8 @@
     gram_ref[...] = jnp.broadcast_to(line, gram_ref.shape)
 
 
-def finish_kernel(count, where_ref, gram_ref, basis_ref, out_ref, energy_ref):
-    core = where_ref[1]
+def finish_kernel(count, gram_ref, basis_ref, out_ref, energy_ref):
+    core = lax.axis_index("sector") % 2
     share = basis_ref.shape[1]
     gram = jnp.sum(gram_ref[...], axis=0, keepdims=True)
     lane = lax.broadcasted_iota(jnp.int32, (1, LANES), 1)
@@ -201,51 +203,104 @@
             part = weights[m] * (basis_ref[2 * m, at] + tau2 * basis_ref[2 * m + 1, at])
             value = part if value is None else value + part
         block = (at // 2) * 2 + (core if even else 1 - core)
-        for t in range(out_ref.shape[0]):
-            out_ref[t, block] = value.astype(jnp.bfloat16)
+        out_ref[block] = value.astype(jnp.bfloat16)
     energy_ref[...] = jnp.where(lane == 0, theta0, jnp.where(lane == 1, theta1, theta2))
 
 
-def gather_chips(right_own, sectors):
-    chips = sectors // 2
-    if chips > 8:
-        everything = lax.all_gather(right_own, "sector")
-        everything = everything.reshape((chips, 2) + right_own.shape)
-        return lax.dynamic_index_in_dim(everything, lax.axis_index("sector") % 2, 1, keepdims=False)
-    pieces = [right_own]
-    for shift in range(1, chips):
-        moves = [(i, (i + 2 * shift) % sectors) for i in range(sectors)]
-        pieces.append(lax.ppermute(right_own, "sector", moves))
-    mine = lax.axis_index("sector") // 2
-    stacked = jnp.stack(pieces[::-1] + pieces[:0:-1])
-    return lax.dynamic_slice_in_dim(stacked, chips - 1 - mine, chips, 0)
-
-
-def local(sectors, psi, left_env, right_env, precond, block_sizes):
-    owners = lax.axis_size("term")
+def assemble_kernel(plan, *refs):
+    pieces, out_ref, sems = refs[: plan.owners], refs[plan.owners], refs[plan.owners + 1]
+    share = pieces[0].shape[0]
+    term, chip = lax.axis_index("term"), lax.axis_index("sector") // 2
+    copies = []
+    for m in range(plan.owners):
+        first = plan.first_chip(plan.hop(term, m), chip) * 2
+        copies.append(pltpu.make_async_copy(pieces[m], out_ref.at[pl.ds(first, share)], sems.at[m]))
+        copies[-1].start()
+    for copy in copies:
+        copy.wait()
+
+
+class Plan:
+    def __init__(self, owners, sectors):
+        self.owners, self.sectors, self.chips = owners, sectors, sectors // 2
+        self.groups = self.chips // owners
+        self.direct = self.groups == 1
+        if owners == 4:
+            self.spread = ((0, 2, 1, 3), (1, 3, 0, 2), (2, 0, 3, 1), (3, 1, 2, 0))
+        else:
+            self.spread = tuple(tuple((q + t) % owners for q in range(owners)) for t in range(owners))
+
+    def hop(self, term, offset):
+        if self.owners & (self.owners - 1) == 0:
+            return term ^ offset
+        return (term + offset) % self.owners
+
+    def back(self, offset):
+        if self.owners & (self.owners - 1) == 0:
+            return offset
+        return (self.owners - offset) % self.owners
+
+    def first_chip(self, term, chip):
+        if not self.direct:
+            return term * self.groups
+        found = jnp.int32(0)
+        for t in range(self.owners):
+            for q in range(self.owners):
+                hit = (term == t) & (chip == self.spread[t][q])
+                found = jnp.where(hit, q, found)
+        return found
+
+
+def from_owner(plan, value, offset):
+    if offset == 0:
+        return value
+    moves = [(plan.hop(t, offset), t) for t in range(plan.owners)]
+    return lax.ppermute(value, "term", moves)
+
+
+def inputs(plan, left, right):
+    sectors, owners, groups = plan.sectors, plan.owners, plan.groups
+    cores = [(i, i ^ 1) for i in range(sectors)]
+    if plan.direct:
+        lefts = [from_owner(plan, left, m) for m in range(owners)]
+        own = []
+        for m in range(owners):
+            moves = []
+            for t in range(owners):
+                for q in range(plan.chips):
+                    for c in range(2):
+                        source = plan.hop(t, m) * sectors + 2 * q + c
+                        moves.append((source, t * sectors + 2 * plan.spread[t][q] + c))
+            own.append(lax.ppermute(right, ("term", "sector"), moves)[None])
+        swapped = [lax.ppermute(x, "sector", cores) for x in own]
+        return lefts, own, swapped
+    everything = lax.all_gather(right, "sector").reshape((owners, groups, 2) + right.shape)
+    by_chip = lax.dynamic_index_in_dim(everything, lax.axis_index("sector") % 2, 2, keepdims=False)
+    spread_left = jnp.broadcast_to(left, (owners, 1) + left.shape)
+    got = lax.all_to_all(jnp.concatenate([by_chip, spread_left], axis=1), "term", 0, 0)
+    swapped = lax.ppermute(got[:, :groups], "sector", cores)
+    lefts = [got[t, groups] for t in range(owners)]
+    own = [got[t, :groups] for t in range(owners)]
+    return lefts, own, [swapped[t] for t in range(owners)]
+
+
+def local(plan, psi, left_env, right_env, precond, block_sizes):
+    owners, sectors = plan.owners, plan.sectors
     devices = owners * sectors
     depth, width = right_env.shape[0], right_env.shape[-1]
-    groups = sectors // 2 // owners
-    share = 2 * groups
-    own = lax.axis_index("sector")
-    where = jnp.stack([lax.axis_index("term"), own % 2, own]).astype(jnp.int32)
-
-    by_chip = gather_chips(right_env[:, 0], sectors)
-    by_chip = by_chip.reshape(owners, groups, depth, width, width)
-    left = jnp.broadcast_to(left_env[:, 0], (owners, 1, depth, width, width))
-    got = lax.all_to_all(jnp.concatenate([by_chip, left], axis=1), "term", 0, 0)
-    swap = lax.ppermute(got[:, :groups], "sector", [(i, i ^ 1) for i in range(sectors)])
+    share = 2 * plan.groups
+    lefts, own, swapped = inputs(plan, left_env[:, 0], right_env[:, 0])
 
     smem = pl.BlockSpec(memory_space=pltpu.SMEM)
     vmem = pl.BlockSpec(memory_space=pltpu.VMEM)
     terms = owners * depth
     gram, basis = pl.pallas_call(
-        main_kernel,
+        functools.partial(main_kernel, plan),
         out_shape=(
             jax.ShapeDtypeStruct((devices, LANES), jnp.float32),
             jax.ShapeDtypeStruct((8, share, width, width), jnp.float32),
         ),
-        in_specs=[smem, smem, vmem, vmem, vmem, vmem],
+        in_specs=[smem] + [vmem] * (2 + 3 * owners),
         out_specs=(vmem, vmem),
         scratch_shapes=[
             pltpu.VMEM((width, terms * width), jnp.bfloat16),
@@ -254,22 +309,30 @@
         ],
         compiler_params=pltpu.CompilerParams(vmem_limit_bytes=48 << 20),
         name="levels",
-    )(where, block_sizes, psi[0], precond[0], got, swap)
+    )(block_sizes, psi[0], precond[0], *lefts, *own, *swapped)
     gram = lax.all_to_all(gram, ("term", "sector"), 0, 0, tiled=True)
     count = float(sectors * sectors * width * width)
     blocks, energy = pl.pallas_call(
         functools.partial(finish_kernel, count),
         out_shape=(
-            jax.ShapeDtypeStruct((owners, share, width, width), jnp.bfloat16),
+            jax.ShapeDtypeStruct((share, width, width), jnp.bfloat16),
             jax.ShapeDtypeStruct((1, LANES), jnp.float32),
         ),
-        in_specs=[smem, vmem, vmem],
+        in_specs=[vmem, vmem],
         out_specs=(vmem, vmem),
         compiler_params=pltpu.CompilerParams(vmem_limit_bytes=48 << 20),
         name="finish",
-    )(where, gram, basis)
-    state = lax.all_to_all(blocks, "term", 0, 0)
-    return (state.reshape((1, sectors, width, width)), energy[0, :3])
+    )(gram, basis)
+    anywhere = pl.BlockSpec(memory_space=pl.ANY)
+    state = pl.pallas_call(
+        functools.partial(assemble_kernel, plan),
+        out_shape=jax.ShapeDtypeStruct((sectors, width, width), jnp.bfloat16),
+        in_specs=[anywhere] * owners,
+        out_specs=anywhere,
+        scratch_shapes=[pltpu.SemaphoreType.DMA((owners,))],
+        name="assemble",
+    )(*[from_owner(plan, blocks, m) for m in range(owners)])
+    return (state[None], energy[0, :3])
 
 
 def solution(mesh):
@@ -282,7 +345,7 @@
     )
     out_specs = (P("sector", None, None, None), P())
     return jax.shard_map(
-        functools.partial(local, mesh.shape["sector"]),
+        functools.partial(local, Plan(mesh.shape["term"], mesh.shape["sector"])),
         mesh=mesh,
         in_specs=in_specs,
         out_specs=out_specs,

time: 52.4 us -> 53.9 us (1.029)
  waiting for transfers between devices: 13.2 us -> 3.75 us
  starting transfers between devices: 9.59 us -> 18.5 us
  Pallas kernels: 4.71 us -> 12.6 us
  blocking collectives: 20 us -> 13.6 us
  local copies, waits for them, and re-layouts: 3.65 us -> 4.52 us
    ppermute x4 -> x14, starting transfers between devices: 6.19 us -> 18.5 us  [the longest x6 10.5 us: from_owner(): return lax.ppermute(value, 'term', moves)]
    all_to_all x1 -> x0, blocking collectives: 10.6 us -> none  [local(): got = lax.all_to_all(jnp.concatenate([by_chip, left], axis=1), 'term', 0, 0)]
    pallas_call x1 -> x2, Pallas kernels: 3.07 us -> 12.2 us  [the longest x1 9.08 us: local(): pl.pallas_call(functools.partial(assemble_kernel, plan), out_shape=jax.Sh...]
    all_to_all x1 -> x0, waiting for transfers between devices: 5.14 us -> none  [local(): state = lax.all_to_all(blocks, 'term', 0, 0)]
    ppermute x4 -> x14, waiting for transfers between devices: 8.08 us -> 3.75 us  [the longest x6 3.73 us: from_owner(): return lax.ppermute(value, 'term', moves)]
    all_to_all x1, blocking collectives: 9.35 us -> 13.6 us  [local(): gram = lax.all_to_all(gram, ('term', 'sector'), 0, 0, tiled=True)]
    all_to_all x1 -> x0, starting transfers between devices: 3.41 us -> none  [local(): state = lax.all_to_all(blocks, 'term', 0, 0)]
    pallas_call x1, Pallas kernels: 1.64 us -> 0.39 us  [local(): pl.pallas_call(functools.partial(finish_kernel, count), out_shape=(jax.Sh...]
  transfers between devices with their start and end apart: 5 -> 14, of which waited for: 4 -> 4; matrix products, arithmetic and copies ran while one was open for 1% -> 1% of each run, Pallas kernels for 0% -> 0%
where the time goes in v2:
time: 53.9 us; the launch traced here: 53.6 us
  starting transfers between devices  18.5 us (34%)
  blocking collectives  13.6 us (25%)
  Pallas kernels  12.6 us (23%)
  local copies, waits for them, and re-layouts  4.52 us (8%)
  waiting for transfers between devices  3.75 us (7%)
  between operations  0.7 us (1%)
    all_to_all x1, blocking collectives, local(): gram = lax.all_to_all(gram, ('term', 'sector'), 0, 0, tiled=True)  13.6 us
    ppermute x6, starting transfers between devices, from_owner(): return lax.ppermute(value, 'term', moves)  10.5 us
    pallas_call x1, Pallas kernels, local(): pl.pallas_call(functools.partial(assemble_kernel, plan), out_shape=jax.Sh...  9.08 us
    ppermute x4, starting transfers between devices, inputs(): own.append(lax.ppermute(right, ('term', 'sector'), moves)[None])  7 us
    unnamed x16, local copies, waits for them, and re-layouts  4.01 us
    ppermute x6, waiting for transfers between devices, from_owner(): return lax.ppermute(value, 'term', moves)  3.73 us
    pallas_call x1, Pallas kernels, local(): pl.pallas_call(functools.partial(main_kernel, plan), out_shape=(jax.Shape...  3.12 us
  transfers between devices with their start and end apart: 14, of which 4 were waited for; matrix products, arithmetic and copies ran while one was open for 1% of the time, Pallas kernels for 0%

profile of v2, /device:TPU:0, one launch (start us, length us, event | category | flops | bytes accessed | tf_op | source)
XLA Modules:
  0.0 53.6 jit_solution(6417289495283718021)
XLA Ops:
  0.6 4.0 %collective-permute-start.2 = (bf16[2,128,128]{2,1,0:T(8,128)(2,1)}, bf16[2,128,128]{2,1,0:T(8,128)(2,1)S(1)}, u32[]{:S(2)}, u32[]{:S(2)}) collective-permute-start(bf16[2,128,128]{2,1,0:T(8,128)(2,1)} %bitcast.18), channel_id=1, source_target_pairs={{24,0},{16,8},{8,16},{0,24},{25,1},{17,9},{9,17},{1,25},{26,2},{18... | collective-permute-start | bytes 196616 | tf_op jit(solution)/shard_map/ppermute | solution.py:258
  4.6 0.5 collective-permute-start.1
  5.1 4.5 %collective-permute-start.6 = (bf16[2,128,128]{2,1,0:T(8,128)(2,1)}, bf16[2,128,128]{2,1,0:T(8,128)(2,1)S(1)}, u32[]{:S(2)}, u32[]{:S(2)}) collective-permute-start(bf16[2,128,128]{2,1,0:T(8,128)(2,1)} %bitcast.32), channel_id=1, source_target_pairs={{24,0},{25,1},{26,4},{27,5},{28,2},{29,3},{30,6},{31,7},{16,10},{1... | collective-permute-start | bytes 196616 | tf_op jit(solution)/shard_map/ppermute | solution.py:274
  9.6 1.0 %collective-permute-start.4 = (bf16[2,128,128]{2,1,0:T(8,128)(2,1)}, bf16[2,128,128]{2,1,0:T(8,128)(2,1)S(1)}, u32[]{:S(2)}, u32[]{:S(2)}) collective-permute-start(bf16[2,128,128]{2,1,0:T(8,128)(2,1)} %bitcast.34), channel_id=1, source_target_pairs={{8,0},{9,1},{10,4},{11,5},{12,2},{13,3},{14,6},{15,7},{0,10},{1,11... | collective-permute-start | bytes 196616 | tf_op jit(solution)/shard_map/ppermute | solution.py:274
  10.6 0.0 collective-permute-done.2.refs_3_
  10.6 1.5 %collective-permute-start.3 = (bf16[2,128,128]{2,1,0:T(8,128)(2,1)}, bf16[2,128,128]{2,1,0:T(8,128)(2,1)S(1)}, u32[]{:S(2)}, u32[]{:S(2)}) collective-permute-start(bf16[2,128,128]{2,1,0:T(8,128)(2,1)} %bitcast.35), channel_id=1, source_target_pairs={{0,0},{1,1},{2,4},{3,5},{4,2},{5,3},{6,6},{7,7},{8,10},{9,11},{10,... | collective-permute-start | bytes 196616 | tf_op jit(solution)/shard_map/ppermute | solution.py:274
  12.1 0.0 collective-permute-done.1.refs_2_
  12.1 2.5 %collective-permute-start = (bf16[2,128,128]{2,1,0:T(8,128)(2,1)}, bf16[2,128,128]{2,1,0:T(8,128)(2,1)S(1)}, u32[]{:S(2)}, u32[]{:S(2)}) collective-permute-start(bf16[2,128,128]{2,1,0:T(8,128)(2,1)} %bitcast.20), channel_id=1, source_target_pairs={{8,0},{0,8},{24,16},{16,24},{9,1},{1,9},{25,17},{17,25},{10,2},{2,... | collective-permute-start | bytes 196616 | tf_op jit(solution)/shard_map/ppermute | solution.py:258
  14.6 0.0 collective-permute-done.6
  14.6 0.0 collective-permute-start.10
  14.6 0.0 collective-permute-done.5
  14.6 0.5 collective-permute-start.9
  15.1 0.0 collective-permute-done.4
  15.1 0.1 collective-permute-start.8
  15.2 0.4 collective-permute-start.7
  15.6 1.4 %collective-permute-done.refs_1_ = bf16[2,128,128]{2,1,0:T(8,128)(2,1)S(1)} collective-permute-done((bf16[2,128,128]{2,1,0:T(8,128)(2,1)}, bf16[2,128,128]{2,1,0:T(8,128)(2,1)S(1)}, u32[]{:S(2)}, u32[]{:S(2)}) %collective-permute-start) | collective-permute-done | bytes 65568 | tf_op jit(solution)/shard_map/ppermute | solution.py:258
  17.1 0.6 %copy-done.4 = s32[8]{0:T(128)S(1)} copy-done((s32[8]{0:T(128)S(1)}, s32[8]{0:T(128)}, u32[]{:S(2)}) %copy-start.4) | copy-done | bytes 56
  17.7 0.9 %copy-done = bf16[1,8,128,128]{3,2,1,0:T(8,128)(2,1)S(1)} copy-done((bf16[1,8,128,128]{3,2,1,0:T(8,128)(2,1)S(1)}, bf16[1,8,128,128]{3,2,1,0:T(8,128)(2,1)}, u32[]{:S(2)}) %copy-start) | copy-done | bytes 262168
  18.7 0.9 %copy-done.1 = bf16[1,8,128,128]{3,2,1,0:T(8,128)(2,1)S(1)} copy-done((bf16[1,8,128,128]{3,2,1,0:T(8,128)(2,1)S(1)}, bf16[1,8,128,128]{3,2,1,0:T(8,128)(2,1)}, u32[]{:S(2)}) %copy-start.1) | copy-done | bytes 262168
  19.6 0.8 %copy-done.2 = bf16[2,1,128,128]{3,2,1,0:T(8,128)(2,1)S(1)} copy-done((bf16[2,1,128,128]{3,2,1,0:T(8,128)(2,1)S(1)}, bf16[2,1,128,128]{3,2,1,0:T(8,128)(2,1)}, u32[]{:S(2)}) %copy-start.2) | copy-done | bytes 65560
  20.5 3.1 %levels.1 = (f32[32,128]{1,0:T(8,128)S(1)}, f32[8,2,128,128]{3,2,1,0:T(8,128)S(1)}) custom-call(s32[8]{0:T(128)S(1)} %copy-done.4, bf16[8,128,128]{2,1,0:T(8,128)(2,1)S(1)} %bitcast.15, bf16[8,128,128]{2,1,0:T(8,128)(2,1)S(1)} %bitcast.16, bf16[2,128,128]{2,1,0:T(8,128)(2,1)S(1)} %bitcast.21, bf16[2,128,128]{2,1,0:T(8,128)(2,1)S(1)} %collective-permute-done.refs_1_, ...), custom_call_target="tpu_custom_call" | custom-call | tf_op jit(solution)/shard_map/levels/pallas_call | solution.py:297
  23.6 13.6 %all_to_all.11 = f32[32,1,128]{2,1,0:T(1,128)S(1)} all-to-all(f32[32,1,128]{2,1,0:T(1,128)S(1)} %bitcast.30), channel_id=1, replica_groups=mesh['term'=4,'sector'=8] {'term','sector'}, dimensions={0} | all-to-all | bytes 32768 | tf_op jit(solution)/shard_map/all_to_all | solution.py:313
  37.1 0.4 finish.1
  37.5 0.7 %collective-permute-start.13 = (bf16[2,128,128]{2,1,0:T(8,128)(2,1)S(1)}, bf16[2,128,128]{2,1,0:T(8,128)(2,1)S(1)}, u32[]{:S(2)}, u32[]{:S(2)}) collective-permute-start(bf16[2,128,128]{2,1,0:T(8,128)(2,1)S(1)} %get-tuple-element.8.refs_0_), channel_id=1, source_target_pairs={{24,0},{16,8},{8,16},{0,24},{25,1},{17,9},{9,17},{1,25},{26,2},{18... | collective-permute-start | bytes 196616 | tf_op jit(solution)/shard_map/ppermute | solution.py:258
  38.2 1.4 %collective-permute-start.12 = (bf16[2,128,128]{2,1,0:T(8,128)(2,1)S(1)}, bf16[2,128,128]{2,1,0:T(8,128)(2,1)S(1)}, u32[]{:S(2)}, u32[]{:S(2)}) collective-permute-start(bf16[2,128,128]{2,1,0:T(8,128)(2,1)S(1)} %get-tuple-element.8.refs_0_), channel_id=1, source_target_pairs={{16,0},{24,8},{0,16},{8,24},{17,1},{25,9},{1,17},{9,25},{18,2},{26... | collective-permute-start | bytes 196616 | tf_op jit(solution)/shard_map/ppermute | solution.py:258
  39.7 1.4 %collective-permute-start.11 = (bf16[2,128,128]{2,1,0:T(8,128)(2,1)S(1)}, bf16[2,128,128]{2,1,0:T(8,128)(2,1)S(1)}, u32[]{:S(2)}, u32[]{:S(2)}) collective-permute-start(bf16[2,128,128]{2,1,0:T(8,128)(2,1)S(1)} %get-tuple-element.8.refs_0_), channel_id=1, source_target_pairs={{8,0},{0,8},{24,16},{16,24},{9,1},{1,9},{25,17},{17,25},{10,2},{2,... | collective-permute-start | bytes 196616 | tf_op jit(solution)/shard_map/ppermute | solution.py:258
  41.1 0.5 slice_bitcast_fusion
  41.6 1.5 %collective-permute-done.13.refs_3_ = bf16[2,128,128]{2,1,0:T(8,128)(2,1)S(1)} collective-permute-done((bf16[2,128,128]{2,1,0:T(8,128)(2,1)S(1)}, bf16[2,128,128]{2,1,0:T(8,128)(2,1)S(1)}, u32[]{:S(2)}, u32[]{:S(2)}) %collective-permute-start.13) | collective-permute-done | bytes 65568 | tf_op jit(solution)/shard_map/ppermute | solution.py:258
  43.1 0.1 collective-permute-done.12.refs_2_
  43.2 0.7 %collective-permute-done.11.refs_1_ = bf16[2,128,128]{2,1,0:T(8,128)(2,1)S(1)} collective-permute-done((bf16[2,128,128]{2,1,0:T(8,128)(2,1)S(1)}, bf16[2,128,128]{2,1,0:T(8,128)(2,1)S(1)}, u32[]{:S(2)}, u32[]{:S(2)}) %collective-permute-start.11) | collective-permute-done | bytes 65568 | tf_op jit(solution)/shard_map/ppermute | solution.py:258
  44.0 0.6 %copy-done.7 = bf16[2,128,128]{2,1,0:T(8,128)(2,1)} copy-done((bf16[2,128,128]{2,1,0:T(8,128)(2,1)}, bf16[2,128,128]{2,1,0:T(8,128)(2,1)S(1)}, u32[]{:S(2)}) %copy-start.7) | copy-done | bytes 65560
  44.6 9.1 %assemble.1 = bf16[8,128,128]{2,1,0:T(8,128)(2,1)} custom-call(bf16[2,128,128]{2,1,0:T(8,128)(2,1)} %copy-done.3, bf16[2,128,128]{2,1,0:T(8,128)(2,1)} %copy-done.7, bf16[2,128,128]{2,1,0:T(8,128)(2,1)} %copy-done.6, bf16[2,128,128]{2,1,0:T(8,128)(2,1)} %copy-done.5), custom_call_target="tpu_custom_call" | custom-call | tf_op jit(solution)/shard_map/assemble/pallas_call | solution.py:327
  (17 shorter events, 0.0 us)
Async XLA Ops:
  0.6 10.0 %collective-permute-start.2 = (bf16[2,128,128]{2,1,0:T(8,128)(2,1)}, bf16[2,128,128]{2,1,0:T(8,128)(2,1)S(1)}, u32[]{:S(2)}, u32[]{:S(2)}) collective-permute-start(bf16[2,128,128]{2,1,0:T(8,128)(2,1)} %bitcast.18), channel_id=1, source_target_pairs={{24,0},{16,8},{8,16},{0,24},{25,1},{17,9},{9,17},{1,25},{26,2},{18... | collective-permute-start | bytes 196616 | tf_op jit(solution)/shard_map/ppermute | solution.py:258
  4.6 7.5 %collective-permute-start.1 = (bf16[2,128,128]{2,1,0:T(8,128)(2,1)}, bf16[2,128,128]{2,1,0:T(8,128)(2,1)S(1)}, u32[]{:S(2)}, u32[]{:S(2)}) collective-permute-start(bf16[2,128,128]{2,1,0:T(8,128)(2,1)} %bitcast.19), channel_id=1, source_target_pairs={{16,0},{24,8},{0,16},{8,24},{17,1},{25,9},{1,17},{9,25},{18,2},{26... | collective-permute-start | bytes 196616 | tf_op jit(solution)/shard_map/ppermute | solution.py:258
  5.1 9.5 %collective-permute-start.6 = (bf16[2,128,128]{2,1,0:T(8,128)(2,1)}, bf16[2,128,128]{2,1,0:T(8,128)(2,1)S(1)}, u32[]{:S(2)}, u32[]{:S(2)}) collective-permute-start(bf16[2,128,128]{2,1,0:T(8,128)(2,1)} %bitcast.32), channel_id=1, source_target_pairs={{24,0},{25,1},{26,4},{27,5},{28,2},{29,3},{30,6},{31,7},{16,10},{1... | collective-permute-start | bytes 196616 | tf_op jit(solution)/shard_map/ppermute | solution.py:274
  9.6 5.0 %collective-permute-start.5 = (bf16[2,128,128]{2,1,0:T(8,128)(2,1)}, bf16[2,128,128]{2,1,0:T(8,128)(2,1)S(1)}, u32[]{:S(2)}, u32[]{:S(2)}) collective-permute-start(bf16[2,128,128]{2,1,0:T(8,128)(2,1)} %bitcast.33), channel_id=1, source_target_pairs={{16,0},{17,1},{18,4},{19,5},{20,2},{21,3},{22,6},{23,7},{24,10},{2... | collective-permute-start | bytes 196616 | tf_op jit(solution)/shard_map/ppermute | solution.py:274
  9.6 5.5 %collective-permute-start.4 = (bf16[2,128,128]{2,1,0:T(8,128)(2,1)}, bf16[2,128,128]{2,1,0:T(8,128)(2,1)S(1)}, u32[]{:S(2)}, u32[]{:S(2)}) collective-permute-start(bf16[2,128,128]{2,1,0:T(8,128)(2,1)} %bitcast.34), channel_id=1, source_target_pairs={{8,0},{9,1},{10,4},{11,5},{12,2},{13,3},{14,6},{15,7},{0,10},{1,11... | collective-permute-start | bytes 196616 | tf_op jit(solution)/shard_map/ppermute | solution.py:274
  10.6 4.6 %collective-permute-start.3 = (bf16[2,128,128]{2,1,0:T(8,128)(2,1)}, bf16[2,128,128]{2,1,0:T(8,128)(2,1)S(1)}, u32[]{:S(2)}, u32[]{:S(2)}) collective-permute-start(bf16[2,128,128]{2,1,0:T(8,128)(2,1)} %bitcast.35), channel_id=1, source_target_pairs={{0,0},{1,1},{2,4},{3,5},{4,2},{5,3},{6,6},{7,7},{8,10},{9,11},{10,... | collective-permute-start | bytes 196616 | tf_op jit(solution)/shard_map/ppermute | solution.py:274
  12.1 4.9 %collective-permute-start = (bf16[2,128,128]{2,1,0:T(8,128)(2,1)}, bf16[2,128,128]{2,1,0:T(8,128)(2,1)S(1)}, u32[]{:S(2)}, u32[]{:S(2)}) collective-permute-start(bf16[2,128,128]{2,1,0:T(8,128)(2,1)} %bitcast.20), channel_id=1, source_target_pairs={{8,0},{0,8},{24,16},{16,24},{9,1},{1,9},{25,17},{17,25},{10,2},{2,... | collective-permute-start | bytes 196616 | tf_op jit(solution)/shard_map/ppermute | solution.py:258
  14.6 2.5 %collective-permute-start.10 = (bf16[1,2,128,128]{3,2,1,0:T(8,128)(2,1)S(1)}, bf16[1,2,128,128]{3,2,1,0:T(8,128)(2,1)S(1)}, u32[]{:S(2)}, u32[]{:S(2)}) collective-permute-start(bf16[1,2,128,128]{3,2,1,0:T(8,128)(2,1)S(1)} %bitcast.22), channel_id=1, source_target_pairs={{0,1},{1,0},{2,3},{3,2},{4,5},{5,4},{6,7},{7,6},{8,9},{9,8},{10,11... | collective-permute-start | bytes 196616 | tf_op jit(solution)/shard_map/ppermute | solution.py:275
  14.6 2.4 %collective-permute-start.9 = (bf16[1,2,128,128]{3,2,1,0:T(8,128)(2,1)S(1)}, bf16[1,2,128,128]{3,2,1,0:T(8,128)(2,1)S(1)}, u32[]{:S(2)}, u32[]{:S(2)}) collective-permute-start(bf16[1,2,128,128]{3,2,1,0:T(8,128)(2,1)S(1)} %bitcast.24), channel_id=1, source_target_pairs={{0,1},{1,0},{2,3},{3,2},{4,5},{5,4},{6,7},{7,6},{8,9},{9,8},{10,11... | collective-permute-start | bytes 196616 | tf_op jit(solution)/shard_map/ppermute | solution.py:275
  15.1 1.9 %collective-permute-start.8 = (bf16[1,2,128,128]{3,2,1,0:T(8,128)(2,1)S(1)}, bf16[1,2,128,128]{3,2,1,0:T(8,128)(2,1)S(1)}, u32[]{:S(2)}, u32[]{:S(2)}) collective-permute-start(bf16[1,2,128,128]{3,2,1,0:T(8,128)(2,1)S(1)} %bitcast.26), channel_id=1, source_target_pairs={{0,1},{1,0},{2,3},{3,2},{4,5},{5,4},{6,7},{7,6},{8,9},{9,8},{10,11... | collective-permute-start | bytes 196616 | tf_op jit(solution)/shard_map/ppermute | solution.py:275
  15.2 1.9 %collective-permute-start.7 = (bf16[1,2,128,128]{3,2,1,0:T(8,128)(2,1)S(1)}, bf16[1,2,128,128]{3,2,1,0:T(8,128)(2,1)S(1)}, u32[]{:S(2)}, u32[]{:S(2)}) collective-permute-start(bf16[1,2,128,128]{3,2,1,0:T(8,128)(2,1)S(1)} %bitcast.28), channel_id=1, source_target_pairs={{0,1},{1,0},{2,3},{3,2},{4,5},{5,4},{6,7},{7,6},{8,9},{9,8},{10,11... | collective-permute-start | bytes 196616 | tf_op jit(solution)/shard_map/ppermute | solution.py:275
  17.1 0.7 %copy-start.4 = (s32[8]{0:T(128)S(1)}, s32[8]{0:T(128)}, u32[]{:S(2)}) copy-start(s32[8]{0:T(128)} %sizes_ref.1) | copy-start | bytes 100
  17.7 0.9 %copy-start = (bf16[1,8,128,128]{3,2,1,0:T(8,128)(2,1)S(1)}, bf16[1,8,128,128]{3,2,1,0:T(8,128)(2,1)}, u32[]{:S(2)}) copy-start(bf16[1,8,128,128]{3,2,1,0:T(8,128)(2,1)} %param.5) | copy-start | bytes 786436
  18.7 0.9 %copy-start.1 = (bf16[1,8,128,128]{3,2,1,0:T(8,128)(2,1)S(1)}, bf16[1,8,128,128]{3,2,1,0:T(8,128)(2,1)}, u32[]{:S(2)}) copy-start(bf16[1,8,128,128]{3,2,1,0:T(8,128)(2,1)} %param.8) | copy-start | bytes 786436
  19.6 0.8 %copy-start.2 = (bf16[2,1,128,128]{3,2,1,0:T(8,128)(2,1)S(1)}, bf16[2,1,128,128]{3,2,1,0:T(8,128)(2,1)}, u32[]{:S(2)}) copy-start(bf16[2,1,128,128]{3,2,1,0:T(8,128)(2,1)} %param.6) | copy-start | bytes 196612
  37.5 6.4 %copy-start.3 = (bf16[2,128,128]{2,1,0:T(8,128)(2,1)}, bf16[2,128,128]{2,1,0:T(8,128)(2,1)S(1)}, u32[]{:S(2)}) copy-start(bf16[2,128,128]{2,1,0:T(8,128)(2,1)S(1)} %get-tuple-element.8.refs_0_) | copy-start | bytes 196612
  37.5 5.6 %collective-permute-start.13 = (bf16[2,128,128]{2,1,0:T(8,128)(2,1)S(1)}, bf16[2,128,128]{2,1,0:T(8,128)(2,1)S(1)}, u32[]{:S(2)}, u32[]{:S(2)}) collective-permute-start(bf16[2,128,128]{2,1,0:T(8,128)(2,1)S(1)} %get-tuple-element.8.refs_0_), channel_id=1, source_target_pairs={{24,0},{16,8},{8,16},{0,24},{25,1},{17,9},{9,17},{1,25},{26,2},{18... | collective-permute-start | bytes 196616 | tf_op jit(solution)/shard_map/ppermute | solution.py:258
  38.2 5.0 %collective-permute-start.12 = (bf16[2,128,128]{2,1,0:T(8,128)(2,1)S(1)}, bf16[2,128,128]{2,1,0:T(8,128)(2,1)S(1)}, u32[]{:S(2)}, u32[]{:S(2)}) collective-permute-start(bf16[2,128,128]{2,1,0:T(8,128)(2,1)S(1)} %get-tuple-element.8.refs_0_), channel_id=1, source_target_pairs={{16,0},{24,8},{0,16},{8,24},{17,1},{25,9},{1,17},{9,25},{18,2},{26... | collective-permute-start | bytes 196616 | tf_op jit(solution)/shard_map/ppermute | solution.py:258
  39.7 4.3 %collective-permute-start.11 = (bf16[2,128,128]{2,1,0:T(8,128)(2,1)S(1)}, bf16[2,128,128]{2,1,0:T(8,128)(2,1)S(1)}, u32[]{:S(2)}, u32[]{:S(2)}) collective-permute-start(bf16[2,128,128]{2,1,0:T(8,128)(2,1)S(1)} %get-tuple-element.8.refs_0_), channel_id=1, source_target_pairs={{8,0},{0,8},{24,16},{16,24},{9,1},{1,9},{25,17},{17,25},{10,2},{2,... | collective-permute-start | bytes 196616 | tf_op jit(solution)/shard_map/ppermute | solution.py:258
  43.1 0.8 %copy-start.5 = (bf16[2,128,128]{2,1,0:T(8,128)(2,1)}, bf16[2,128,128]{2,1,0:T(8,128)(2,1)S(1)}, u32[]{:S(2)}) copy-start(bf16[2,128,128]{2,1,0:T(8,128)(2,1)S(1)} %collective-permute-done.13.refs_3_) | copy-start | bytes 196612
  43.2 0.7 %copy-start.6 = (bf16[2,128,128]{2,1,0:T(8,128)(2,1)}, bf16[2,128,128]{2,1,0:T(8,128)(2,1)S(1)}, u32[]{:S(2)}) copy-start(bf16[2,128,128]{2,1,0:T(8,128)(2,1)S(1)} %collective-permute-done.12.refs_2_) | copy-start | bytes 196612
  43.9 0.6 %copy-start.7 = (bf16[2,128,128]{2,1,0:T(8,128)(2,1)}, bf16[2,128,128]{2,1,0:T(8,128)(2,1)S(1)}, u32[]{:S(2)}) copy-start(bf16[2,128,128]{2,1,0:T(8,128)(2,1)S(1)} %collective-permute-done.11.refs_1_) | copy-start | bytes 196612

commit v3 on v2

--- a/solution.py
+++ b/solution.py
@@ -30,19 +30,34 @@
     return functools.reduce(lambda a, b: a + b, [x[r : r + 8] for r in range(0, x.shape[0], 8)])
 
 
-def main_kernel(plan, sizes_ref, psi_ref, pre_ref, *refs):
+def main_kernel(plan, sizes_hbm, psi_hbm, pre_hbm, left_hbm, *refs):
     owners = plan.owners
-    left_refs, own_refs, swap_refs = refs[:owners], refs[owners : 2 * owners], refs[2 * owners : 3 * owners]
-    gram_ref, basis_ref, left_cat, right_cat, sums = refs[3 * owners :]
+    left_refs, refs = refs[: owners - 1], refs[owners - 1 :]
+    own_refs, swap_refs, refs = refs[:owners], refs[owners : 2 * owners], refs[2 * owners :]
+    gram_ref, basis_ref, sizes_ref, psi_ref, pre_ref, own_left, left_cat, right_cat, sums, sems = refs
     groups, depth, width = own_refs[0].shape[0], own_refs[0].shape[1], own_refs[0].shape[-1]
     terms = owners * depth
     row = lax.axis_index("sector")
     core = row % 2
     chip = plan.first_chip(lax.axis_index("term"), row // 2)
-    own_size = sizes_ref[row]
+    blocks = pl.ds(2 * chip, psi_ref.shape[0])
+    copies = [
+        pltpu.make_async_copy(sizes_hbm, sizes_ref, sems.at[0]),
+        pltpu.make_async_copy(psi_hbm.at[blocks], psi_ref, sems.at[1]),
+        pltpu.make_async_copy(pre_hbm.at[blocks], pre_ref, sems.at[2]),
+        pltpu.make_async_copy(left_hbm, own_left, sems.at[3]),
+    ]
+    for copy in copies:
+        copy.start()
     sums[...] = jnp.zeros_like(sums)
-    for k in range(terms):
-        left_cat[:, k * width : (k + 1) * width] = left_refs[k // depth][k % depth]
+    for k in range(depth, terms):
+        left_cat[:, k * width : (k + 1) * width] = left_refs[k // depth - 1][k % depth]
+
+    def finish_copies():
+        for copy in copies:
+            copy.wait()
+        for k in range(depth):
+            left_cat[:, k * width : (k + 1) * width] = own_left[k]
 
     def apply(vectors):
         columns = []
@@ -77,12 +92,14 @@
                 cols = slice(half * width, (half + 1) * width)
                 right_cat[0, rows, cols] = own_refs[k // depth][g, k % depth]
                 right_cat[1, rows, cols] = swap_refs[k // depth][g, k % depth]
+        if groups == 1:
+            finish_copies()
         row_ids = lax.broadcasted_iota(jnp.int32, (width, width), 0)
         col_ids = lax.broadcasted_iota(jnp.int32, (width, width), 1)
         start, inverse = [], []
         for b in range(2):
-            block = (chip + g) * 2 + (core if b == 0 else 1 - core)
-            valid = (row_ids < own_size) & (col_ids < sizes_ref[block])
+            block = 2 * g + (core if b == 0 else 1 - core)
+            valid = (row_ids < sizes_ref[row]) & (col_ids < sizes_ref[2 * chip + block])
             start.append(jnp.where(valid, psi_ref[block].astype(jnp.float32), 0.0))
             inverse.append(jnp.where(valid, 1.0 / pre_ref[block].astype(jnp.float32), 0.0))
 
@@ -146,6 +163,7 @@
     if groups == 1:
         group(0)
     else:
+        finish_copies()
 
         @pl.loop(0, groups)
         def _(g):
@@ -291,8 +309,11 @@
     share = 2 * plan.groups
     lefts, own, swapped = inputs(plan, left_env[:, 0], right_env[:, 0])
 
-    smem = pl.BlockSpec(memory_space=pltpu.SMEM)
+    anywhere = pl.BlockSpec(memory_space=pltpu.HBM)
     vmem = pl.BlockSpec(memory_space=pltpu.VMEM)
+    parked = [
+        pltpu.with_memory_space_constraint(x, pltpu.HBM) for x in (block_sizes, psi[0], precond[0], lefts[0])
+    ]
     terms = owners * depth
     gram, basis = pl.pallas_call(
         functools.partial(main_kernel, plan),
@@ -300,16 +321,21 @@
             jax.ShapeDtypeStruct((devices, LANES), jnp.float32),
             jax.ShapeDtypeStruct((8, share, width, width), jnp.float32),
         ),
-        in_specs=[smem] + [vmem] * (2 + 3 * owners),
+        in_specs=[anywhere] * 4 + [vmem] * (3 * owners - 1),
         out_specs=(vmem, vmem),
         scratch_shapes=[
+            pltpu.SMEM((sectors,), jnp.int32),
+            pltpu.VMEM((share, width, width), jnp.bfloat16),
+            pltpu.VMEM((share, width, width), jnp.bfloat16),
+            pltpu.VMEM((depth, width, width), jnp.bfloat16),
             pltpu.VMEM((width, terms * width), jnp.bfloat16),
             pltpu.VMEM((2, terms * width, 2 * width), jnp.bfloat16),
             pltpu.VMEM((ROWS * 8, LANES), jnp.float32),
+            pltpu.SemaphoreType.DMA((4,)),
         ],
         compiler_params=pltpu.CompilerParams(vmem_limit_bytes=48 << 20),
         name="levels",
-    )(block_sizes, psi[0], precond[0], *lefts, *own, *swapped)
+    )(*parked, *lefts[1:], *own, *swapped)
     gram = lax.all_to_all(gram, ("term", "sector"), 0, 0, tiled=True)
     count = float(sectors * sectors * width * width)
     blocks, energy = pl.pallas_call(
@@ -323,13 +349,13 @@
         compiler_params=pltpu.CompilerParams(vmem_limit_bytes=48 << 20),
         name="finish",
     )(gram, basis)
-    anywhere = pl.BlockSpec(memory_space=pl.ANY)
     state = pl.pallas_call(
         functools.partial(assemble_kernel, plan),
         out_shape=jax.ShapeDtypeStruct((sectors, width, width), jnp.bfloat16),
-        in_specs=[anywhere] * owners,
+        in_specs=[vmem] * owners,
         out_specs=anywhere,
         scratch_shapes=[pltpu.SemaphoreType.DMA((owners,))],
+        compiler_params=pltpu.CompilerParams(vmem_limit_bytes=16 << 20),
         name="assemble",
     )(*[from_owner(plan, blocks, m) for m in range(owners)])
     return (state[None], energy[0, :3])

time: 53.9 us -> 41.9 us (0.78)
  Pallas kernels: 12.6 us -> 4.63 us
  local copies, waits for them, and re-layouts: 4.52 us -> 0.51 us
    pallas_call x1, Pallas kernels: 9.08 us -> 0.73 us  [local(): pl.pallas_call(functools.partial(assemble_kernel, plan), out_shape=jax.Sh...]
    unnamed x16 -> x0, local copies, waits for them, and re-layouts: 4.01 us -> none
where the time goes in v3:
time: 41.9 us; the launch traced here: 41.7 us
  starting transfers between devices  18.5 us (44%)
  blocking collectives  13.6 us (32%)
  Pallas kernels  4.63 us (11%)
  waiting for transfers between devices  3.76 us (9%)
  between operations  0.68 us (2%)
  local copies, waits for them, and re-layouts  0.51 us (1%)
    all_to_all x1, blocking collectives, local(): gram = lax.all_to_all(gram, ('term', 'sector'), 0, 0, tiled=True)  13.6 us
    ppermute x6, starting transfers between devices, from_owner(): return lax.ppermute(value, 'term', moves)  10.5 us
    ppermute x4, starting transfers between devices, inputs(): own.append(lax.ppermute(right, ('term', 'sector'), moves)[None])  7 us
    ppermute x6, waiting for transfers between devices, from_owner(): return lax.ppermute(value, 'term', moves)  3.74 us
    pallas_call x1, Pallas kernels, local(): pl.pallas_call(functools.partial(main_kernel, plan), out_shape=(jax.Shape...  3.51 us
    ppermute x4, starting transfers between devices, inputs(): swapped = [lax.ppermute(x, 'sector', cores) for x in own]  1.02 us
  transfers between devices with their start and end apart: 14, of which 4 were waited for; matrix products, arithmetic and copies ran while one was open for 1% of the time, Pallas kernels for 0%

profile of v3, /device:TPU:0, one launch (start us, length us, event | category | flops | bytes accessed | tf_op | source)
XLA Modules:
  0.0 41.7 jit_solution(7190861942084877516)
XLA Ops:
  0.6 4.0 %collective-permute-start.2 = (bf16[2,128,128]{2,1,0:T(8,128)(2,1)}, bf16[2,128,128]{2,1,0:T(8,128)(2,1)S(1)}, u32[]{:S(2)}, u32[]{:S(2)}) collective-permute-start(bf16[2,128,128]{2,1,0:T(8,128)(2,1)} %bitcast.28), channel_id=1, source_target_pairs={{24,0},{16,8},{8,16},{0,24},{25,1},{17,9},{9,17},{1,25},{26,2},{18... | collective-permute-start | bytes 196616 | tf_op jit(solution)/shard_map/ppermute | solution.py:276
  4.6 0.5 %collective-permute-start.1 = (bf16[2,128,128]{2,1,0:T(8,128)(2,1)}, bf16[2,128,128]{2,1,0:T(8,128)(2,1)S(1)}, u32[]{:S(2)}, u32[]{:S(2)}) collective-permute-start(bf16[2,128,128]{2,1,0:T(8,128)(2,1)} %bitcast.29), channel_id=1, source_target_pairs={{16,0},{24,8},{0,16},{8,24},{17,1},{25,9},{1,17},{9,25},{18,2},{26... | collective-permute-start | bytes 196616 | tf_op jit(solution)/shard_map/ppermute | solution.py:276
  5.1 4.5 %collective-permute-start.6 = (bf16[2,128,128]{2,1,0:T(8,128)(2,1)}, bf16[2,128,128]{2,1,0:T(8,128)(2,1)S(1)}, u32[]{:S(2)}, u32[]{:S(2)}) collective-permute-start(bf16[2,128,128]{2,1,0:T(8,128)(2,1)} %bitcast.32), channel_id=1, source_target_pairs={{24,0},{25,1},{26,4},{27,5},{28,2},{29,3},{30,6},{31,7},{16,10},{1... | collective-permute-start | bytes 196616 | tf_op jit(solution)/shard_map/ppermute | solution.py:292
  9.6 0.0 collective-permute-start.5
  9.6 1.0 %collective-permute-start.4 = (bf16[2,128,128]{2,1,0:T(8,128)(2,1)}, bf16[2,128,128]{2,1,0:T(8,128)(2,1)S(1)}, u32[]{:S(2)}, u32[]{:S(2)}) collective-permute-start(bf16[2,128,128]{2,1,0:T(8,128)(2,1)} %bitcast.34), channel_id=1, source_target_pairs={{8,0},{9,1},{10,4},{11,5},{12,2},{13,3},{14,6},{15,7},{0,10},{1,11... | collective-permute-start | bytes 196616 | tf_op jit(solution)/shard_map/ppermute | solution.py:292
  10.6 0.0 collective-permute-done.2.refs_2_
  10.6 1.5 %collective-permute-start.3 = (bf16[2,128,128]{2,1,0:T(8,128)(2,1)}, bf16[2,128,128]{2,1,0:T(8,128)(2,1)S(1)}, u32[]{:S(2)}, u32[]{:S(2)}) collective-permute-start(bf16[2,128,128]{2,1,0:T(8,128)(2,1)} %bitcast.35), channel_id=1, source_target_pairs={{0,0},{1,1},{2,4},{3,5},{4,2},{5,3},{6,6},{7,7},{8,10},{9,11},{10,... | collective-permute-start | bytes 196616 | tf_op jit(solution)/shard_map/ppermute | solution.py:292
  12.1 0.0 collective-permute-done.1.refs_1_
  12.1 2.5 %collective-permute-start = (bf16[2,128,128]{2,1,0:T(8,128)(2,1)}, bf16[2,128,128]{2,1,0:T(8,128)(2,1)S(1)}, u32[]{:S(2)}, u32[]{:S(2)}) collective-permute-start(bf16[2,128,128]{2,1,0:T(8,128)(2,1)} %bitcast.30), channel_id=1, source_target_pairs={{8,0},{0,8},{24,16},{16,24},{9,1},{1,9},{25,17},{17,25},{10,2},{2,... | collective-permute-start | bytes 196616 | tf_op jit(solution)/shard_map/ppermute | solution.py:276
  14.6 0.0 collective-permute-done.6
  14.6 0.0 collective-permute-start.10
  14.6 0.0 collective-permute-done.5
  14.6 0.5 %collective-permute-start.9 = (bf16[1,2,128,128]{3,2,1,0:T(8,128)(2,1)S(1)}, bf16[1,2,128,128]{3,2,1,0:T(8,128)(2,1)S(1)}, u32[]{:S(2)}, u32[]{:S(2)}) collective-permute-start(bf16[1,2,128,128]{3,2,1,0:T(8,128)(2,1)S(1)} %bitcast.18), channel_id=1, source_target_pairs={{0,1},{1,0},{2,3},{3,2},{4,5},{5,4},{6,7},{7,6},{8,9},{9,8},{10,11... | collective-permute-start | bytes 196616 | tf_op jit(solution)/shard_map/ppermute | solution.py:293
  15.1 0.0 collective-permute-done.4
  15.1 0.1 collective-permute-start.8
  15.2 0.0 collective-permute-done.3
  15.2 0.4 %collective-permute-start.7 = (bf16[1,2,128,128]{3,2,1,0:T(8,128)(2,1)S(1)}, bf16[1,2,128,128]{3,2,1,0:T(8,128)(2,1)S(1)}, u32[]{:S(2)}, u32[]{:S(2)}) collective-permute-start(bf16[1,2,128,128]{3,2,1,0:T(8,128)(2,1)S(1)} %bitcast.22), channel_id=1, source_target_pairs={{0,1},{1,0},{2,3},{3,2},{4,5},{5,4},{6,7},{7,6},{8,9},{9,8},{10,11... | collective-permute-start | bytes 196616 | tf_op jit(solution)/shard_map/ppermute | solution.py:293
  15.6 1.4 %collective-permute-done.refs_0_ = bf16[2,128,128]{2,1,0:T(8,128)(2,1)S(1)} collective-permute-done((bf16[2,128,128]{2,1,0:T(8,128)(2,1)}, bf16[2,128,128]{2,1,0:T(8,128)(2,1)S(1)}, u32[]{:S(2)}, u32[]{:S(2)}) %collective-permute-start) | collective-permute-done | bytes 65568 | tf_op jit(solution)/shard_map/ppermute | solution.py:276
  17.1 0.0 collective-permute-done.10.refs_10_
  17.1 0.0 collective-permute-done.9.refs_9_
  17.1 0.0 collective-permute-done.8.refs_8_
  17.1 3.5 %levels.1 = (f32[32,128]{1,0:T(8,128)S(1)}, f32[8,2,128,128]{3,2,1,0:T(8,128)S(1)}) custom-call(s32[8]{0:T(128)} %sizes_hbm.1, bf16[8,128,128]{2,1,0:T(8,128)(2,1)} %bitcast.25, bf16[8,128,128]{2,1,0:T(8,128)(2,1)} %bitcast.26, bf16[2,128,128]{2,1,0:T(8,128)(2,1)} %bitcast.31, bf16[2,128,128]{2,1,0:T(8,128)(2,1)S(1)} %collective-permute-done.refs_0_, ...), custom_call_target="tpu_custom_call" | custom-call | tf_op jit(solution)/shard_map/levels/pallas_call | solution.py:318
  20.6 13.6 %all_to_all.11 = f32[32,1,128]{2,1,0:T(1,128)S(1)} all-to-all(f32[32,1,128]{2,1,0:T(1,128)S(1)} %bitcast.24), channel_id=1, replica_groups=mesh['term'=4,'sector'=8] {'term','sector'}, dimensions={0} | all-to-all | bytes 32768 | tf_op jit(solution)/shard_map/all_to_all | solution.py:339
  34.2 0.4 finish.1
  34.6 0.7 %collective-permute-start.13 = (bf16[2,128,128]{2,1,0:T(8,128)(2,1)S(1)}, bf16[2,128,128]{2,1,0:T(8,128)(2,1)S(1)}, u32[]{:S(2)}, u32[]{:S(2)}) collective-permute-start(bf16[2,128,128]{2,1,0:T(8,128)(2,1)S(1)} %get-tuple-element.8.refs_0_), channel_id=1, source_target_pairs={{24,0},{16,8},{8,16},{0,24},{25,1},{17,9},{9,17},{1,25},{26,2},{18... | collective-permute-start | bytes 196616 | tf_op jit(solution)/shard_map/ppermute | solution.py:276
  35.2 1.4 %collective-permute-start.12 = (bf16[2,128,128]{2,1,0:T(8,128)(2,1)S(1)}, bf16[2,128,128]{2,1,0:T(8,128)(2,1)S(1)}, u32[]{:S(2)}, u32[]{:S(2)}) collective-permute-start(bf16[2,128,128]{2,1,0:T(8,128)(2,1)S(1)} %get-tuple-element.8.refs_0_), channel_id=1, source_target_pairs={{16,0},{24,8},{0,16},{8,24},{17,1},{25,9},{1,17},{9,25},{18,2},{26... | collective-permute-start | bytes 196616 | tf_op jit(solution)/shard_map/ppermute | solution.py:276
  36.7 1.4 %collective-permute-start.11 = (bf16[2,128,128]{2,1,0:T(8,128)(2,1)S(1)}, bf16[2,128,128]{2,1,0:T(8,128)(2,1)S(1)}, u32[]{:S(2)}, u32[]{:S(2)}) collective-permute-start(bf16[2,128,128]{2,1,0:T(8,128)(2,1)S(1)} %get-tuple-element.8.refs_0_), channel_id=1, source_target_pairs={{8,0},{0,8},{24,16},{16,24},{9,1},{1,9},{25,17},{17,25},{10,2},{2,... | collective-permute-start | bytes 196616 | tf_op jit(solution)/shard_map/ppermute | solution.py:276
  38.1 0.5 %slice_bitcast_fusion = f32[3]{0:T(128)} fusion(f32[1,128]{1,0:T(1,128)S(1)} %get-tuple-element.9), kind=kLoop, calls=%fused_computation | loop fusion | bytes 24 | tf_op jit(solution)/shard_map/squeeze | solution.py:361
  38.6 1.5 %collective-permute-done.13.refs_3_ = bf16[2,128,128]{2,1,0:T(8,128)(2,1)S(1)} collective-permute-done((bf16[2,128,128]{2,1,0:T(8,128)(2,1)S(1)}, bf16[2,128,128]{2,1,0:T(8,128)(2,1)S(1)}, u32[]{:S(2)}, u32[]{:S(2)}) %collective-permute-start.13) | collective-permute-done | bytes 65568 | tf_op jit(solution)/shard_map/ppermute | solution.py:276
  40.1 0.1 collective-permute-done.12.refs_2_
  40.2 0.7 %collective-permute-done.11.refs_1_ = bf16[2,128,128]{2,1,0:T(8,128)(2,1)S(1)} collective-permute-done((bf16[2,128,128]{2,1,0:T(8,128)(2,1)S(1)}, bf16[2,128,128]{2,1,0:T(8,128)(2,1)S(1)}, u32[]{:S(2)}, u32[]{:S(2)}) %collective-permute-start.11) | collective-permute-done | bytes 65568 | tf_op jit(solution)/shard_map/ppermute | solution.py:276
  40.9 0.7 %assemble.1 = bf16[8,128,128]{2,1,0:T(8,128)(2,1)} custom-call(bf16[2,128,128]{2,1,0:T(8,128)(2,1)S(1)} %get-tuple-element.8.refs_0_, bf16[2,128,128]{2,1,0:T(8,128)(2,1)S(1)} %collective-permute-done.11.refs_1_, bf16[2,128,128]{2,1,0:T(8,128)(2,1)S(1)} %collective-permute-done.12.refs_2_, bf16[2,128,128]{2,1,0:T(8,128)(2,1)S(1)} %collective-permute-done.13.refs_3_), custom_call_target="tpu_custom_call" | custom-call | tf_op jit(solution)/shard_map/assemble/pallas_call | solution.py:352
  (1 shorter events, 0.0 us)
Async XLA Ops:
  0.6 10.0 %collective-permute-start.2 = (bf16[2,128,128]{2,1,0:T(8,128)(2,1)}, bf16[2,128,128]{2,1,0:T(8,128)(2,1)S(1)}, u32[]{:S(2)}, u32[]{:S(2)}) collective-permute-start(bf16[2,128,128]{2,1,0:T(8,128)(2,1)} %bitcast.28), channel_id=1, source_target_pairs={{24,0},{16,8},{8,16},{0,24},{25,1},{17,9},{9,17},{1,25},{26,2},{18... | collective-permute-start | bytes 196616 | tf_op jit(solution)/shard_map/ppermute | solution.py:276
  4.6 7.5 %collective-permute-start.1 = (bf16[2,128,128]{2,1,0:T(8,128)(2,1)}, bf16[2,128,128]{2,1,0:T(8,128)(2,1)S(1)}, u32[]{:S(2)}, u32[]{:S(2)}) collective-permute-start(bf16[2,128,128]{2,1,0:T(8,128)(2,1)} %bitcast.29), channel_id=1, source_target_pairs={{16,0},{24,8},{0,16},{8,24},{17,1},{25,9},{1,17},{9,25},{18,2},{26... | collective-permute-start | bytes 196616 | tf_op jit(solution)/shard_map/ppermute | solution.py:276
  5.1 9.5 %collective-permute-start.6 = (bf16[2,128,128]{2,1,0:T(8,128)(2,1)}, bf16[2,128,128]{2,1,0:T(8,128)(2,1)S(1)}, u32[]{:S(2)}, u32[]{:S(2)}) collective-permute-start(bf16[2,128,128]{2,1,0:T(8,128)(2,1)} %bitcast.32), channel_id=1, source_target_pairs={{24,0},{25,1},{26,4},{27,5},{28,2},{29,3},{30,6},{31,7},{16,10},{1... | collective-permute-start | bytes 196616 | tf_op jit(solution)/shard_map/ppermute | solution.py:292
  9.6 5.0 %collective-permute-start.5 = (bf16[2,128,128]{2,1,0:T(8,128)(2,1)}, bf16[2,128,128]{2,1,0:T(8,128)(2,1)S(1)}, u32[]{:S(2)}, u32[]{:S(2)}) collective-permute-start(bf16[2,128,128]{2,1,0:T(8,128)(2,1)} %bitcast.33), channel_id=1, source_target_pairs={{16,0},{17,1},{18,4},{19,5},{20,2},{21,3},{22,6},{23,7},{24,10},{2... | collective-permute-start | bytes 196616 | tf_op jit(solution)/shard_map/ppermute | solution.py:292
  9.6 5.5 %collective-permute-start.4 = (bf16[2,128,128]{2,1,0:T(8,128)(2,1)}, bf16[2,128,128]{2,1,0:T(8,128)(2,1)S(1)}, u32[]{:S(2)}, u32[]{:S(2)}) collective-permute-start(bf16[2,128,128]{2,1,0:T(8,128)(2,1)} %bitcast.34), channel_id=1, source_target_pairs={{8,0},{9,1},{10,4},{11,5},{12,2},{13,3},{14,6},{15,7},{0,10},{1,11... | collective-permute-start | bytes 196616 | tf_op jit(solution)/shard_map/ppermute | solution.py:292
  10.6 4.6 %collective-permute-start.3 = (bf16[2,128,128]{2,1,0:T(8,128)(2,1)}, bf16[2,128,128]{2,1,0:T(8,128)(2,1)S(1)}, u32[]{:S(2)}, u32[]{:S(2)}) collective-permute-start(bf16[2,128,128]{2,1,0:T(8,128)(2,1)} %bitcast.35), channel_id=1, source_target_pairs={{0,0},{1,1},{2,4},{3,5},{4,2},{5,3},{6,6},{7,7},{8,10},{9,11},{10,... | collective-permute-start | bytes 196616 | tf_op jit(solution)/shard_map/ppermute | solution.py:292
  12.1 4.9 %collective-permute-start = (bf16[2,128,128]{2,1,0:T(8,128)(2,1)}, bf16[2,128,128]{2,1,0:T(8,128)(2,1)S(1)}, u32[]{:S(2)}, u32[]{:S(2)}) collective-permute-start(bf16[2,128,128]{2,1,0:T(8,128)(2,1)} %bitcast.30), channel_id=1, source_target_pairs={{8,0},{0,8},{24,16},{16,24},{9,1},{1,9},{25,17},{17,25},{10,2},{2,... | collective-permute-start | bytes 196616 | tf_op jit(solution)/shard_map/ppermute | solution.py:276
  14.6 2.5 %collective-permute-start.10 = (bf16[1,2,128,128]{3,2,1,0:T(8,128)(2,1)S(1)}, bf16[1,2,128,128]{3,2,1,0:T(8,128)(2,1)S(1)}, u32[]{:S(2)}, u32[]{:S(2)}) collective-permute-start(bf16[1,2,128,128]{3,2,1,0:T(8,128)(2,1)S(1)} %bitcast.16), channel_id=1, source_target_pairs={{0,1},{1,0},{2,3},{3,2},{4,5},{5,4},{6,7},{7,6},{8,9},{9,8},{10,11... | collective-permute-start | bytes 196616 | tf_op jit(solution)/shard_map/ppermute | solution.py:293
  14.6 2.4 %collective-permute-start.9 = (bf16[1,2,128,128]{3,2,1,0:T(8,128)(2,1)S(1)}, bf16[1,2,128,128]{3,2,1,0:T(8,128)(2,1)S(1)}, u32[]{:S(2)}, u32[]{:S(2)}) collective-permute-start(bf16[1,2,128,128]{3,2,1,0:T(8,128)(2,1)S(1)} %bitcast.18), channel_id=1, source_target_pairs={{0,1},{1,0},{2,3},{3,2},{4,5},{5,4},{6,7},{7,6},{8,9},{9,8},{10,11... | collective-permute-start | bytes 196616 | tf_op jit(solution)/shard_map/ppermute | solution.py:293
  15.1 1.9 %collective-permute-start.8 = (bf16[1,2,128,128]{3,2,1,0:T(8,128)(2,1)S(1)}, bf16[1,2,128,128]{3,2,1,0:T(8,128)(2,1)S(1)}, u32[]{:S(2)}, u32[]{:S(2)}) collective-permute-start(bf16[1,2,128,128]{3,2,1,0:T(8,128)(2,1)S(1)} %bitcast.20), channel_id=1, source_target_pairs={{0,1},{1,0},{2,3},{3,2},{4,5},{5,4},{6,7},{7,6},{8,9},{9,8},{10,11... | collective-permute-start | bytes 196616 | tf_op jit(solution)/shard_map/ppermute | solution.py:293
  15.2 1.9 %collective-permute-start.7 = (bf16[1,2,128,128]{3,2,1,0:T(8,128)(2,1)S(1)}, bf16[1,2,128,128]{3,2,1,0:T(8,128)(2,1)S(1)}, u32[]{:S(2)}, u32[]{:S(2)}) collective-permute-start(bf16[1,2,128,128]{3,2,1,0:T(8,128)(2,1)S(1)} %bitcast.22), channel_id=1, source_target_pairs={{0,1},{1,0},{2,3},{3,2},{4,5},{5,4},{6,7},{7,6},{8,9},{9,8},{10,11... | collective-permute-start | bytes 196616 | tf_op jit(solution)/shard_map/ppermute | solution.py:293
  34.6 5.6 %collective-permute-start.13 = (bf16[2,128,128]{2,1,0:T(8,128)(2,1)S(1)}, bf16[2,128,128]{2,1,0:T(8,128)(2,1)S(1)}, u32[]{:S(2)}, u32[]{:S(2)}) collective-permute-start(bf16[2,128,128]{2,1,0:T(8,128)(2,1)S(1)} %get-tuple-element.8.refs_0_), channel_id=1, source_target_pairs={{24,0},{16,8},{8,16},{0,24},{25,1},{17,9},{9,17},{1,25},{26,2},{18... | collective-permute-start | bytes 196616 | tf_op jit(solution)/shard_map/ppermute | solution.py:276
  35.2 5.0 %collective-permute-start.12 = (bf16[2,128,128]{2,1,0:T(8,128)(2,1)S(1)}, bf16[2,128,128]{2,1,0:T(8,128)(2,1)S(1)}, u32[]{:S(2)}, u32[]{:S(2)}) collective-permute-start(bf16[2,128,128]{2,1,0:T(8,128)(2,1)S(1)} %get-tuple-element.8.refs_0_), channel_id=1, source_target_pairs={{16,0},{24,8},{0,16},{8,24},{17,1},{25,9},{1,17},{9,25},{18,2},{26... | collective-permute-start | bytes 196616 | tf_op jit(solution)/shard_map/ppermute | solution.py:276
  36.7 4.3 %collective-permute-start.11 = (bf16[2,128,128]{2,1,0:T(8,128)(2,1)S(1)}, bf16[2,128,128]{2,1,0:T(8,128)(2,1)S(1)}, u32[]{:S(2)}, u32[]{:S(2)}) collective-permute-start(bf16[2,128,128]{2,1,0:T(8,128)(2,1)S(1)} %get-tuple-element.8.refs_0_), channel_id=1, source_target_pairs={{8,0},{0,8},{24,16},{16,24},{9,1},{1,9},{25,17},{17,25},{10,2},{2,... | collective-permute-start | bytes 196616 | tf_op jit(solution)/shard_map/ppermute | solution.py:276

commit v4 on v3

--- a/solution.py
+++ b/solution.py
@@ -30,12 +30,95 @@
     return functools.reduce(lambda a, b: a + b, [x[r : r + 8] for r in range(0, x.shape[0], 8)])
 
 
-def main_kernel(plan, sizes_hbm, psi_hbm, pre_hbm, left_hbm, *refs):
-    owners = plan.owners
-    left_refs, refs = refs[: owners - 1], refs[owners - 1 :]
-    own_refs, swap_refs, refs = refs[:owners], refs[owners : 2 * owners], refs[2 * owners :]
-    gram_ref, basis_ref, sizes_ref, psi_ref, pre_ref, own_left, left_cat, right_cat, sums, sems = refs
-    groups, depth, width = own_refs[0].shape[0], own_refs[0].shape[1], own_refs[0].shape[-1]
+def stack_right(right_cat, right_refs, g, depth, width):
+    for k in range(len(right_refs) * depth):
+        for half in range(2):
+            right_cat[k * width : (k + 1) * width, half * width : (half + 1) * width] = right_refs[k // depth][
+                g, k % depth
+            ]
+
+
+def levels(left_cat, right_cat, sums, basis_ref, g, start, inv):
+    width = start.shape[0]
+    terms = left_cat.shape[1] // width
+
+    def apply(vectors):
+        stacked = jnp.concatenate(vectors, axis=0)
+        images = lax.dot_general(
+            stacked,
+            right_cat[:, : stacked.shape[1]],
+            (((1,), (1,)), ((), ())),
+            preferred_element_type=jnp.float32,
+        ).astype(jnp.bfloat16)
+        columns = []
+        for n in range(len(vectors)):
+            rows = images[n * width : (n + 1) * width]
+            columns.append(jnp.concatenate([rows[:, k * width : (k + 1) * width] for k in range(terms)], axis=0))
+        out = jnp.dot(left_cat[...], jnp.concatenate(columns, axis=1), preferred_element_type=jnp.float32)
+        return [out[:, n * width : (n + 1) * width] for n in range(len(vectors))]
+
+    def add(slot, value):
+        sums[slot * 8 : slot * 8 + 8] += value
+
+    def put(table, at, value):
+        table[at] = value if table[at] is None else table[at] + value
+
+    def advance(vectors, images):
+        level = []
+        for x, h in zip(vectors, images):
+            level += [SCALE * x - (SCALE * inv) * h, inv * x]
+        return level
+
+    (image,) = apply([start])
+    state = start.astype(jnp.float32)
+    add(N0, fold(state * state))
+    add(E0, fold(state * image))
+    first = advance([state], [image])
+
+    images = apply([split(x) for x in first])
+    for m in range(2):
+        for n in range(2):
+            if m <= n:
+                add(N1 + m + n, (1.0 if m == n else 2.0) * fold(first[m] * first[n]))
+            add(E1 + m + n, fold(first[m] * images[n]))
+    second = advance(first, images)
+
+    images = apply([split(x) for x in second])
+    third = advance(second, images)
+    for m in range(8):
+        basis_ref[m, g] = third[m]
+    norm, energy, last = [None] * 9, [None] * 9, [None] * 27
+    for m in range(4):
+        for n in range(4):
+            a0, a1 = POWERS[m][0] + POWERS[n][0], POWERS[m][1] + POWERS[n][1]
+            put(energy, 3 * a0 + a1, fold(second[m] * images[n]))
+            if m <= n:
+                put(norm, 3 * a0 + a1, (1.0 if m == n else 2.0) * fold(second[m] * second[n]))
+            for d in range(2):
+                for e in range(2):
+                    if (m, d) <= (n, e):
+                        scale = 1.0 if (m, d) == (n, e) else 2.0
+                        put(last, 9 * a0 + 3 * a1 + d + e, scale * fold(third[2 * m + d] * third[2 * n + e]))
+    for at in range(9):
+        add(N2 + at, norm[at])
+        add(E2 + at, energy[at])
+    for at in range(27):
+        add(N3 + at, last[at])
+
+
+def each_group(groups, body):
+    if groups == 1:
+        body(0)
+    else:
+        pl.loop(0, groups)(body)
+
+
+def own_kernel(plan, sizes_hbm, psi_hbm, pre_hbm, left_hbm, *refs):
+    owners, groups = plan.owners, plan.groups
+    left_refs, right_refs, refs = refs[: owners - 1], refs[owners - 1 : 2 * owners - 1], refs[2 * owners - 1 :]
+    left_cat, start_ref, inverse_ref, sums, basis_ref = refs[:5]
+    sizes_ref, psi_ref, pre_ref, own_left, right_cat, sems = refs[5:]
+    depth, width = own_left.shape[0], own_left.shape[-1]
     terms = owners * depth
     row = lax.axis_index("sector")
     core = row % 2
@@ -52,123 +135,41 @@
     sums[...] = jnp.zeros_like(sums)
     for k in range(depth, terms):
         left_cat[:, k * width : (k + 1) * width] = left_refs[k // depth - 1][k % depth]
-
-    def finish_copies():
-        for copy in copies:
-            copy.wait()
-        for k in range(depth):
-            left_cat[:, k * width : (k + 1) * width] = own_left[k]
-
-    def apply(vectors):
-        columns = []
-        for b in range(2):
-            stacked = jnp.concatenate(vectors[b], axis=0)
-            inner = stacked.shape[1]
-            images = lax.dot_general(
-                stacked,
-                right_cat[b, :, :inner],
-                (((1,), (1,)), ((), ())),
-                preferred_element_type=jnp.float32,
-            ).astype(jnp.bfloat16)
-            for n in range(len(vectors[b])):
-                rows = images[n * width : (n + 1) * width]
-                columns.append(
-                    jnp.concatenate([rows[:, k * width : (k + 1) * width] for k in range(terms)], axis=0)
-                )
-        out = jnp.dot(left_cat[...], jnp.concatenate(columns, axis=1), preferred_element_type=jnp.float32)
-        count = len(vectors[0])
-        return [
-            [out[:, (b * count + n) * width : (b * count + n + 1) * width] for n in range(count)]
-            for b in range(2)
-        ]
-
-    def add(slot, value):
-        sums[slot * 8 : slot * 8 + 8] += value
-
-    def group(g):
-        for k in range(terms):
-            rows = slice(k * width, (k + 1) * width)
-            for half in range(2):
-                cols = slice(half * width, (half + 1) * width)
-                right_cat[0, rows, cols] = own_refs[k // depth][g, k % depth]
-                right_cat[1, rows, cols] = swap_refs[k // depth][g, k % depth]
-        if groups == 1:
-            finish_copies()
+    if groups == 1:
+        stack_right(right_cat, right_refs, 0, depth, width)
+    for copy in copies:
+        copy.wait()
+    for k in range(depth):
+        left_cat[:, k * width : (k + 1) * width] = own_left[k]
+
+    def body(g):
         row_ids = lax.broadcasted_iota(jnp.int32, (width, width), 0)
         col_ids = lax.broadcasted_iota(jnp.int32, (width, width), 1)
-        start, inverse = [], []
-        for b in range(2):
-            block = 2 * g + (core if b == 0 else 1 - core)
+        if groups > 1:
+            stack_right(right_cat, right_refs, g, depth, width)
+
+        def masked(block):
             valid = (row_ids < sizes_ref[row]) & (col_ids < sizes_ref[2 * chip + block])
-            start.append(jnp.where(valid, psi_ref[block].astype(jnp.float32), 0.0))
-            inverse.append(jnp.where(valid, 1.0 / pre_ref[block].astype(jnp.float32), 0.0))
-
-        images = apply([[s.astype(jnp.bfloat16)] for s in start])
-        first = []
-        for b in range(2):
-            s, h, inv = start[b], images[b][0], inverse[b]
-            add(N0, fold(s * s))
-            add(E0, fold(s * h))
-            first.append([SCALE * s - (SCALE * inv) * h, inv * s])
-
-        images = apply([[split(x) for x in first[b]] for b in range(2)])
-        second = []
-        for b in range(2):
-            inv = inverse[b]
-            for m in range(2):
-                for n in range(2):
-                    if m <= n:
-                        scale = 1.0 if m == n else 2.0
-                        add(N1 + m + n, scale * fold(first[b][m] * first[b][n]))
-                    add(E1 + m + n, fold(first[b][m] * images[b][n]))
-            level = []
-            for x, h in zip(first[b], images[b]):
-                level += [SCALE * x - (SCALE * inv) * h, inv * x]
-            second.append(level)
-
-        images = apply([[split(x) for x in second[b]] for b in range(2)])
-        for b in range(2):
-            inv = inverse[b]
-            third = []
-            for x, h in zip(second[b], images[b]):
-                third.append((SCALE * x - (SCALE * inv) * h, inv * x))
-            for m in range(4):
-                for d in range(2):
-                    basis_ref[2 * m + d, 2 * g + b] = third[m][d]
-            norm = [None] * 9
-            energy = [None] * 9
-            last = [None] * 27
-
-            def put(table, at, value):
-                table[at] = value if table[at] is None else table[at] + value
-
-            for m in range(4):
-                for n in range(4):
-                    a0, a1 = POWERS[m][0] + POWERS[n][0], POWERS[m][1] + POWERS[n][1]
-                    put(energy, 3 * a0 + a1, fold(second[b][m] * images[b][n]))
-                    for d in range(2):
-                        for e in range(2):
-                            if (m, d) <= (n, e):
-                                scale = 1.0 if (m, d) == (n, e) else 2.0
-                                put(last, 9 * a0 + 3 * a1 + d + e, scale * fold(third[m][d] * third[n][e]))
-                    if m <= n:
-                        scale = 1.0 if m == n else 2.0
-                        put(norm, 3 * a0 + a1, scale * fold(second[b][m] * second[b][n]))
-            for at in range(9):
-                add(N2 + at, norm[at])
-                add(E2 + at, energy[at])
-            for at in range(27):
-                add(N3 + at, last[at])
-
-    if groups == 1:
-        group(0)
-    else:
-        finish_copies()
-
-        @pl.loop(0, groups)
-        def _(g):
-            group(g)
-
+            start = jnp.where(valid, psi_ref[block].astype(jnp.float32), 0.0).astype(jnp.bfloat16)
+            return start, jnp.where(valid, 1.0 / pre_ref[block].astype(jnp.float32), 0.0)
+
+        start, inverse = masked(2 * g + core)
+        levels(left_cat, right_cat, sums, basis_ref, g, start, inverse)
+        start_ref[g], inverse_ref[g] = masked(2 * g + 1 - core)
+
+    each_group(groups, body)
+
+
+def other_kernel(plan, left_cat, start_ref, inverse_ref, sums_in, *refs):
+    right_refs, (gram_ref, basis_ref, sums, right_cat) = refs[: plan.owners], refs[plan.owners :]
+    depth, width = right_refs[0].shape[1], right_refs[0].shape[-1]
+    sums[...] = sums_in[...]
+
+    def body(g):
+        stack_right(right_cat, right_refs, g, depth, width)
+        levels(left_cat, right_cat, sums, basis_ref, g, start_ref[g], inverse_ref[g])
+
+    each_group(plan.groups, body)
     folded = functools.reduce(lambda a, b: a + b, [sums[pl.ds(s, ROWS, stride=8), :] for s in range(8)])
     totals = jnp.sum(folded, axis=1, keepdims=True)
     row_ids = lax.broadcasted_iota(jnp.int32, (ROWS, LANES), 0)
@@ -177,9 +178,9 @@
     gram_ref[...] = jnp.broadcast_to(line, gram_ref.shape)
 
 
-def finish_kernel(count, gram_ref, basis_ref, out_ref, energy_ref):
+def finish_kernel(count, gram_ref, own_ref, other_ref, out_ref, energy_ref):
     core = lax.axis_index("sector") % 2
-    share = basis_ref.shape[1]
+    share = out_ref.shape[0]
     gram = jnp.sum(gram_ref[...], axis=0, keepdims=True)
     lane = lax.broadcasted_iota(jnp.int32, (1, LANES), 1)
 
@@ -215,10 +216,10 @@
     gain = factor(gain, norm3) * gain
     weights = [gain, gain * tau1, gain * tau0, gain * tau0 * tau1]
     for at in range(share):
-        even = at % 2 == 0
+        even, basis_ref = (True, own_ref) if at % 2 == 0 else (False, other_ref)
         value = None
         for m in range(4):
-            part = weights[m] * (basis_ref[2 * m, at] + tau2 * basis_ref[2 * m + 1, at])
+            part = weights[m] * (basis_ref[2 * m, at // 2] + tau2 * basis_ref[2 * m + 1, at // 2])
             value = part if value is None else value + part
         block = (at // 2) * 2 + (core if even else 1 - core)
         out_ref[block] = value.astype(jnp.bfloat16)
@@ -314,28 +315,45 @@
     parked = [
         pltpu.with_memory_space_constraint(x, pltpu.HBM) for x in (block_sizes, psi[0], precond[0], lefts[0])
     ]
-    terms = owners * depth
-    gram, basis = pl.pallas_call(
-        functools.partial(main_kernel, plan),
+    terms, groups = owners * depth, plan.groups
+    right_cat = pltpu.VMEM((terms * width, 2 * width), jnp.bfloat16)
+    basis = jax.ShapeDtypeStruct((8, groups, width, width), jnp.float32)
+    params = pltpu.CompilerParams(vmem_limit_bytes=32 << 20)
+    flops = share * 7 * 3 * terms * width**3
+    cost = pl.CostEstimate(flops=flops, bytes_accessed=1 << 20, transcendentals=0)
+    *passed, own_basis = pl.pallas_call(
+        functools.partial(own_kernel, plan),
         out_shape=(
-            jax.ShapeDtypeStruct((devices, LANES), jnp.float32),
-            jax.ShapeDtypeStruct((8, share, width, width), jnp.float32),
+            jax.ShapeDtypeStruct((width, terms * width), jnp.bfloat16),
+            jax.ShapeDtypeStruct((groups, width, width), jnp.bfloat16),
+            jax.ShapeDtypeStruct((groups, width, width), jnp.float32),
+            jax.ShapeDtypeStruct((ROWS * 8, LANES), jnp.float32),
+            basis,
         ),
-        in_specs=[anywhere] * 4 + [vmem] * (3 * owners - 1),
-        out_specs=(vmem, vmem),
+        in_specs=[anywhere] * 4 + [vmem] * (2 * owners - 1),
+        out_specs=(vmem,) * 5,
         scratch_shapes=[
             pltpu.SMEM((sectors,), jnp.int32),
             pltpu.VMEM((share, width, width), jnp.bfloat16),
             pltpu.VMEM((share, width, width), jnp.bfloat16),
             pltpu.VMEM((depth, width, width), jnp.bfloat16),
-            pltpu.VMEM((width, terms * width), jnp.bfloat16),
-            pltpu.VMEM((2, terms * width, 2 * width), jnp.bfloat16),
-            pltpu.VMEM((ROWS * 8, LANES), jnp.float32),
+            right_cat,
             pltpu.SemaphoreType.DMA((4,)),
         ],
-        compiler_params=pltpu.CompilerParams(vmem_limit_bytes=48 << 20),
-        name="levels",
-    )(*parked, *lefts[1:], *own, *swapped)
+        compiler_params=params,
+        cost_estimate=cost,
+        name="own_columns",
+    )(*parked, *lefts[1:], *own)
+    gram, other_basis = pl.pallas_call(
+        functools.partial(other_kernel, plan),
+        out_shape=(jax.ShapeDtypeStruct((devices, LANES), jnp.float32), basis),
+        in_specs=[vmem] * (4 + owners),
+        out_specs=(vmem, vmem),
+        scratch_shapes=[pltpu.VMEM((ROWS * 8, LANES), jnp.float32), right_cat],
+        compiler_params=params,
+        cost_estimate=cost,
+        name="other_columns",
+    )(*passed, *swapped)
     gram = lax.all_to_all(gram, ("term", "sector"), 0, 0, tiled=True)
     count = float(sectors * sectors * width * width)
     blocks, energy = pl.pallas_call(
@@ -344,11 +362,11 @@
             jax.ShapeDtypeStruct((share, width, width), jnp.bfloat16),
             jax.ShapeDtypeStruct((1, LANES), jnp.float32),
         ),
-        in_specs=[vmem, vmem],
+        in_specs=[vmem] * 3,
         out_specs=(vmem, vmem),
-        compiler_params=pltpu.CompilerParams(vmem_limit_bytes=48 << 20),
+        compiler_params=params,
         name="finish",
-    )(gram, basis)
+    )(gram, own_basis, other_basis)
     state = pl.pallas_call(
         functools.partial(assemble_kernel, plan),
         out_shape=jax.ShapeDtypeStruct((sectors, width, width), jnp.bfloat16),

time: 41.9 us -> 41.8 us (level)
  blocking collectives: 13.6 us -> 12.4 us
  Pallas kernels: 4.63 us -> 5.62 us
    all_to_all x1, blocking collectives: 13.6 us -> 12.4 us  [local(): gram = lax.all_to_all(gram, ('term', 'sector'), 0, 0, tiled=True)]
    pallas_call x1 -> x2, Pallas kernels: 3.51 us -> 4.51 us  [the longest x1 2.72 us: local(): pl.pallas_call(functools.partial(own_kernel, plan), out_shape=(jax.ShapeD...]
  transfers between devices with their start and end apart: 14 -> 14, of which waited for: 4 -> 4; matrix products, arithmetic and copies ran while one was open for 1% -> 1% of each run, Pallas kernels for 0% -> 7%
where the time goes in v4:
time: 41.8 us; the launch traced here: 41.6 us
  starting transfers between devices  18.5 us (44%)
  blocking collectives  12.4 us (30%)
  Pallas kernels  5.62 us (13%)
  waiting for transfers between devices  3.76 us (9%)
  between operations  0.7 us (2%)
  local copies, waits for them, and re-layouts  0.51 us (1%)
    all_to_all x1, blocking collectives, local(): gram = lax.all_to_all(gram, ('term', 'sector'), 0, 0, tiled=True)  12.4 us
    ppermute x6, starting transfers between devices, from_owner(): return lax.ppermute(value, 'term', moves)  10.5 us
    ppermute x4, starting transfers between devices, inputs(): own.append(lax.ppermute(right, ('term', 'sector'), moves)[None])  7 us
    ppermute x6, waiting for transfers between devices, from_owner(): return lax.ppermute(value, 'term', moves)  3.74 us
    pallas_call x1, Pallas kernels, local(): pl.pallas_call(functools.partial(own_kernel, plan), out_shape=(jax.ShapeD...  2.72 us
    pallas_call x1, Pallas kernels, local(): pl.pallas_call(functools.partial(other_kernel, plan), out_shape=(jax.Shap...  1.78 us
    ppermute x4, starting transfers between devices, inputs(): swapped = [lax.ppermute(x, 'sector', cores) for x in own]  1.02 us
  transfers between devices with their start and end apart: 14, of which 4 were waited for; matrix products, arithmetic and copies ran while one was open for 1% of the time, Pallas kernels for 7%

profile of v4, /device:TPU:0, one launch (start us, length us, event | category | flops | bytes accessed | tf_op | source)
XLA Modules:
  0.0 41.6 jit_solution(10705176617383162154)
XLA Ops:
  0.6 4.0 %collective-permute-start.2 = (bf16[2,128,128]{2,1,0:T(8,128)(2,1)}, bf16[2,128,128]{2,1,0:T(8,128)(2,1)S(1)}, u32[]{:S(2)}, u32[]{:S(2)}) collective-permute-start(bf16[2,128,128]{2,1,0:T(8,128)(2,1)} %bitcast.32), channel_id=1, source_target_pairs={{24,0},{16,8},{8,16},{0,24},{25,1},{17,9},{9,17},{1,25},{26,2},{18... | collective-permute-start | bytes 196616 | tf_op jit(solution)/shard_map/ppermute | solution.py:277
  4.6 0.5 %collective-permute-start.1 = (bf16[2,128,128]{2,1,0:T(8,128)(2,1)}, bf16[2,128,128]{2,1,0:T(8,128)(2,1)S(1)}, u32[]{:S(2)}, u32[]{:S(2)}) collective-permute-start(bf16[2,128,128]{2,1,0:T(8,128)(2,1)} %bitcast.33), channel_id=1, source_target_pairs={{16,0},{24,8},{0,16},{8,24},{17,1},{25,9},{1,17},{9,25},{18,2},{26... | collective-permute-start | bytes 196616 | tf_op jit(solution)/shard_map/ppermute | solution.py:277
  5.1 4.5 %collective-permute-start.6 = (bf16[2,128,128]{2,1,0:T(8,128)(2,1)}, bf16[2,128,128]{2,1,0:T(8,128)(2,1)S(1)}, u32[]{:S(2)}, u32[]{:S(2)}) collective-permute-start(bf16[2,128,128]{2,1,0:T(8,128)(2,1)} %bitcast.28), channel_id=1, source_target_pairs={{24,0},{25,1},{26,4},{27,5},{28,2},{29,3},{30,6},{31,7},{16,10},{1... | collective-permute-start | bytes 196616 | tf_op jit(solution)/shard_map/ppermute | solution.py:293
  9.6 0.0 collective-permute-start.5
  9.6 1.0 %collective-permute-start.4 = (bf16[2,128,128]{2,1,0:T(8,128)(2,1)}, bf16[2,128,128]{2,1,0:T(8,128)(2,1)S(1)}, u32[]{:S(2)}, u32[]{:S(2)}) collective-permute-start(bf16[2,128,128]{2,1,0:T(8,128)(2,1)} %bitcast.30), channel_id=1, source_target_pairs={{8,0},{9,1},{10,4},{11,5},{12,2},{13,3},{14,6},{15,7},{0,10},{1,11... | collective-permute-start | bytes 196616 | tf_op jit(solution)/shard_map/ppermute | solution.py:293
  10.6 0.0 collective-permute-done.2.refs_2_
  10.6 1.5 %collective-permute-start.3 = (bf16[2,128,128]{2,1,0:T(8,128)(2,1)}, bf16[2,128,128]{2,1,0:T(8,128)(2,1)S(1)}, u32[]{:S(2)}, u32[]{:S(2)}) collective-permute-start(bf16[2,128,128]{2,1,0:T(8,128)(2,1)} %bitcast.31), channel_id=1, source_target_pairs={{0,0},{1,1},{2,4},{3,5},{4,2},{5,3},{6,6},{7,7},{8,10},{9,11},{10,... | collective-permute-start | bytes 196616 | tf_op jit(solution)/shard_map/ppermute | solution.py:293
  12.1 0.0 collective-permute-done.1.refs_1_
  12.1 2.5 %collective-permute-start = (bf16[2,128,128]{2,1,0:T(8,128)(2,1)}, bf16[2,128,128]{2,1,0:T(8,128)(2,1)S(1)}, u32[]{:S(2)}, u32[]{:S(2)}) collective-permute-start(bf16[2,128,128]{2,1,0:T(8,128)(2,1)} %bitcast.34), channel_id=1, source_target_pairs={{8,0},{0,8},{24,16},{16,24},{9,1},{1,9},{25,17},{17,25},{10,2},{2,... | collective-permute-start | bytes 196616 | tf_op jit(solution)/shard_map/ppermute | solution.py:277
  14.6 0.0 collective-permute-done.6
  14.6 0.0 collective-permute-start.10
  14.6 0.0 collective-permute-done.5
  14.6 0.5 %collective-permute-start.9 = (bf16[1,2,128,128]{3,2,1,0:T(8,128)(2,1)S(1)}, bf16[1,2,128,128]{3,2,1,0:T(8,128)(2,1)S(1)}, u32[]{:S(2)}, u32[]{:S(2)}) collective-permute-start(bf16[1,2,128,128]{3,2,1,0:T(8,128)(2,1)S(1)} %bitcast.19), channel_id=1, source_target_pairs={{0,1},{1,0},{2,3},{3,2},{4,5},{5,4},{6,7},{7,6},{8,9},{9,8},{10,11... | collective-permute-start | bytes 196616 | tf_op jit(solution)/shard_map/ppermute | solution.py:294
  15.1 0.0 collective-permute-done.4
  15.1 0.1 collective-permute-start.8
  15.2 0.0 collective-permute-done.3
  15.2 0.4 %collective-permute-start.7 = (bf16[1,2,128,128]{3,2,1,0:T(8,128)(2,1)S(1)}, bf16[1,2,128,128]{3,2,1,0:T(8,128)(2,1)S(1)}, u32[]{:S(2)}, u32[]{:S(2)}) collective-permute-start(bf16[1,2,128,128]{3,2,1,0:T(8,128)(2,1)S(1)} %bitcast.23), channel_id=1, source_target_pairs={{0,1},{1,0},{2,3},{3,2},{4,5},{5,4},{6,7},{7,6},{8,9},{9,8},{10,11... | collective-permute-start | bytes 196616 | tf_op jit(solution)/shard_map/ppermute | solution.py:294
  15.6 1.4 %collective-permute-done.refs_0_ = bf16[2,128,128]{2,1,0:T(8,128)(2,1)S(1)} collective-permute-done((bf16[2,128,128]{2,1,0:T(8,128)(2,1)}, bf16[2,128,128]{2,1,0:T(8,128)(2,1)S(1)}, u32[]{:S(2)}, u32[]{:S(2)}) %collective-permute-start) | collective-permute-done | bytes 65568 | tf_op jit(solution)/shard_map/ppermute | solution.py:277
  17.1 2.7 %own_columns.1 = (bf16[128,1024]{1,0:T(8,128)(2,1)S(1)}, bf16[1,128,128]{2,1,0:T(8,128)(2,1)S(1)}, f32[1,128,128]{2,1,0:T(8,128)S(1)}, f32[512,128]{1,0:T(8,128)S(1)}, f32[8,1,128,128]{3,2,1,0:T(8,128)S(1)}) custom-call(s32[8]{0:T(128)} %sizes_hbm.1, bf16[8,128,128]{2,1,0:T(8,128)(2,1)} %bitcast.26, bf16[8,128,128]{2,1,0:T(8,128)(2,1)} %bitcast.27, ...), custom_call_target="tpu_custom_call" | custom-call | flops 704643072 | bytes 1048576 | tf_op jit(solution)/shard_map/own_columns/pallas_call | solution.py:324
  19.8 0.0 collective-permute-done.10.refs_3_
  19.8 0.0 collective-permute-done.7.refs_0_
  19.8 1.8 %other_columns.1 = (f32[32,128]{1,0:T(8,128)S(1)}, f32[8,1,128,128]{3,2,1,0:T(8,128)S(1)}) custom-call(bf16[128,1024]{1,0:T(8,128)(2,1)S(1)} %get-tuple-element.11.left_cat, bf16[1,128,128]{2,1,0:T(8,128)(2,1)S(1)} %get-tuple-element.12.start_ref, f32[1,128,128]{2,1,0:T(8,128)S(1)} %get-tuple-element.13.inverse_ref, ...), custom_call_target="tpu_custom_call" | custom-call | flops 704643072 | bytes 1048576 | tf_op jit(solution)/shard_map/other_columns/pallas_call | solution.py:347
  21.6 12.4 %all_to_all.11 = f32[32,1,128]{2,1,0:T(1,128)S(1)} all-to-all(f32[32,1,128]{2,1,0:T(1,128)S(1)} %bitcast.16), channel_id=1, replica_groups=mesh['term'=4,'sector'=8] {'term','sector'}, dimensions={0} | all-to-all | bytes 32768 | tf_op jit(solution)/shard_map/all_to_all | solution.py:357
  34.1 0.4 finish.1
  34.5 0.7 %collective-permute-start.13 = (bf16[2,128,128]{2,1,0:T(8,128)(2,1)S(1)}, bf16[2,128,128]{2,1,0:T(8,128)(2,1)S(1)}, u32[]{:S(2)}, u32[]{:S(2)}) collective-permute-start(bf16[2,128,128]{2,1,0:T(8,128)(2,1)S(1)} %get-tuple-element.18.refs_0_), channel_id=1, source_target_pairs={{24,0},{16,8},{8,16},{0,24},{25,1},{17,9},{9,17},{1,25},{26,2},{18... | collective-permute-start | bytes 196616 | tf_op jit(solution)/shard_map/ppermute | solution.py:277
  35.1 1.4 %collective-permute-start.12 = (bf16[2,128,128]{2,1,0:T(8,128)(2,1)S(1)}, bf16[2,128,128]{2,1,0:T(8,128)(2,1)S(1)}, u32[]{:S(2)}, u32[]{:S(2)}) collective-permute-start(bf16[2,128,128]{2,1,0:T(8,128)(2,1)S(1)} %get-tuple-element.18.refs_0_), channel_id=1, source_target_pairs={{16,0},{24,8},{0,16},{8,24},{17,1},{25,9},{1,17},{9,25},{18,2},{26... | collective-permute-start | bytes 196616 | tf_op jit(solution)/shard_map/ppermute | solution.py:277
  36.6 1.4 %collective-permute-start.11 = (bf16[2,128,128]{2,1,0:T(8,128)(2,1)S(1)}, bf16[2,128,128]{2,1,0:T(8,128)(2,1)S(1)}, u32[]{:S(2)}, u32[]{:S(2)}) collective-permute-start(bf16[2,128,128]{2,1,0:T(8,128)(2,1)S(1)} %get-tuple-element.18.refs_0_), channel_id=1, source_target_pairs={{8,0},{0,8},{24,16},{16,24},{9,1},{1,9},{25,17},{17,25},{10,2},{2,... | collective-permute-start | bytes 196616 | tf_op jit(solution)/shard_map/ppermute | solution.py:277
  38.0 0.5 %slice_bitcast_fusion = f32[3]{0:T(128)} fusion(f32[1,128]{1,0:T(1,128)S(1)} %get-tuple-element.19), kind=kLoop, calls=%fused_computation | loop fusion | bytes 24 | tf_op jit(solution)/shard_map/squeeze | solution.py:379
  38.5 1.5 %collective-permute-done.13.refs_3_ = bf16[2,128,128]{2,1,0:T(8,128)(2,1)S(1)} collective-permute-done((bf16[2,128,128]{2,1,0:T(8,128)(2,1)S(1)}, bf16[2,128,128]{2,1,0:T(8,128)(2,1)S(1)}, u32[]{:S(2)}, u32[]{:S(2)}) %collective-permute-start.13) | collective-permute-done | bytes 65568 | tf_op jit(solution)/shard_map/ppermute | solution.py:277
  40.0 0.1 collective-permute-done.12.refs_2_
  40.1 0.7 %collective-permute-done.11.refs_1_ = bf16[2,128,128]{2,1,0:T(8,128)(2,1)S(1)} collective-permute-done((bf16[2,128,128]{2,1,0:T(8,128)(2,1)S(1)}, bf16[2,128,128]{2,1,0:T(8,128)(2,1)S(1)}, u32[]{:S(2)}, u32[]{:S(2)}) %collective-permute-start.11) | collective-permute-done | bytes 65568 | tf_op jit(solution)/shard_map/ppermute | solution.py:277
  40.8 0.7 %assemble.1 = bf16[8,128,128]{2,1,0:T(8,128)(2,1)} custom-call(bf16[2,128,128]{2,1,0:T(8,128)(2,1)S(1)} %get-tuple-element.18.refs_0_, bf16[2,128,128]{2,1,0:T(8,128)(2,1)S(1)} %collective-permute-done.11.refs_1_, bf16[2,128,128]{2,1,0:T(8,128)(2,1)S(1)} %collective-permute-done.12.refs_2_, bf16[2,128,128]{2,1,0:T(8,128)(2,1)S(1)} %collective-permute-done.13.refs_3_), custom_call_target="tpu_custom_call" | custom-call | tf_op jit(solution)/shard_map/assemble/pallas_call | solution.py:370
  (2 shorter events, 0.0 us)
Async XLA Ops:
  0.6 10.0 %collective-permute-start.2 = (bf16[2,128,128]{2,1,0:T(8,128)(2,1)}, bf16[2,128,128]{2,1,0:T(8,128)(2,1)S(1)}, u32[]{:S(2)}, u32[]{:S(2)}) collective-permute-start(bf16[2,128,128]{2,1,0:T(8,128)(2,1)} %bitcast.32), channel_id=1, source_target_pairs={{24,0},{16,8},{8,16},{0,24},{25,1},{17,9},{9,17},{1,25},{26,2},{18... | collective-permute-start | bytes 196616 | tf_op jit(solution)/shard_map/ppermute | solution.py:277
  4.6 7.5 %collective-permute-start.1 = (bf16[2,128,128]{2,1,0:T(8,128)(2,1)}, bf16[2,128,128]{2,1,0:T(8,128)(2,1)S(1)}, u32[]{:S(2)}, u32[]{:S(2)}) collective-permute-start(bf16[2,128,128]{2,1,0:T(8,128)(2,1)} %bitcast.33), channel_id=1, source_target_pairs={{16,0},{24,8},{0,16},{8,24},{17,1},{25,9},{1,17},{9,25},{18,2},{26... | collective-permute-start | bytes 196616 | tf_op jit(solution)/shard_map/ppermute | solution.py:277
  5.1 9.5 %collective-permute-start.6 = (bf16[2,128,128]{2,1,0:T(8,128)(2,1)}, bf16[2,128,128]{2,1,0:T(8,128)(2,1)S(1)}, u32[]{:S(2)}, u32[]{:S(2)}) collective-permute-start(bf16[2,128,128]{2,1,0:T(8,128)(2,1)} %bitcast.28), channel_id=1, source_target_pairs={{24,0},{25,1},{26,4},{27,5},{28,2},{29,3},{30,6},{31,7},{16,10},{1... | collective-permute-start | bytes 196616 | tf_op jit(solution)/shard_map/ppermute | solution.py:293
  9.6 5.0 %collective-permute-start.5 = (bf16[2,128,128]{2,1,0:T(8,128)(2,1)}, bf16[2,128,128]{2,1,0:T(8,128)(2,1)S(1)}, u32[]{:S(2)}, u32[]{:S(2)}) collective-permute-start(bf16[2,128,128]{2,1,0:T(8,128)(2,1)} %bitcast.29), channel_id=1, source_target_pairs={{16,0},{17,1},{18,4},{19,5},{20,2},{21,3},{22,6},{23,7},{24,10},{2... | collective-permute-start | bytes 196616 | tf_op jit(solution)/shard_map/ppermute | solution.py:293
  9.6 5.5 %collective-permute-start.4 = (bf16[2,128,128]{2,1,0:T(8,128)(2,1)}, bf16[2,128,128]{2,1,0:T(8,128)(2,1)S(1)}, u32[]{:S(2)}, u32[]{:S(2)}) collective-permute-start(bf16[2,128,128]{2,1,0:T(8,128)(2,1)} %bitcast.30), channel_id=1, source_target_pairs={{8,0},{9,1},{10,4},{11,5},{12,2},{13,3},{14,6},{15,7},{0,10},{1,11... | collective-permute-start | bytes 196616 | tf_op jit(solution)/shard_map/ppermute | solution.py:293
  10.6 4.6 %collective-permute-start.3 = (bf16[2,128,128]{2,1,0:T(8,128)(2,1)}, bf16[2,128,128]{2,1,0:T(8,128)(2,1)S(1)}, u32[]{:S(2)}, u32[]{:S(2)}) collective-permute-start(bf16[2,128,128]{2,1,0:T(8,128)(2,1)} %bitcast.31), channel_id=1, source_target_pairs={{0,0},{1,1},{2,4},{3,5},{4,2},{5,3},{6,6},{7,7},{8,10},{9,11},{10,... | collective-permute-start | bytes 196616 | tf_op jit(solution)/shard_map/ppermute | solution.py:293
  12.1 4.9 %collective-permute-start = (bf16[2,128,128]{2,1,0:T(8,128)(2,1)}, bf16[2,128,128]{2,1,0:T(8,128)(2,1)S(1)}, u32[]{:S(2)}, u32[]{:S(2)}) collective-permute-start(bf16[2,128,128]{2,1,0:T(8,128)(2,1)} %bitcast.34), channel_id=1, source_target_pairs={{8,0},{0,8},{24,16},{16,24},{9,1},{1,9},{25,17},{17,25},{10,2},{2,... | collective-permute-start | bytes 196616 | tf_op jit(solution)/shard_map/ppermute | solution.py:277
  14.6 5.2 %collective-permute-start.10 = (bf16[1,2,128,128]{3,2,1,0:T(8,128)(2,1)S(1)}, bf16[1,2,128,128]{3,2,1,0:T(8,128)(2,1)S(1)}, u32[]{:S(2)}, u32[]{:S(2)}) collective-permute-start(bf16[1,2,128,128]{3,2,1,0:T(8,128)(2,1)S(1)} %bitcast.17), channel_id=1, source_target_pairs={{0,1},{1,0},{2,3},{3,2},{4,5},{5,4},{6,7},{7,6},{8,9},{9,8},{10,11... | collective-permute-start | bytes 196616 | tf_op jit(solution)/shard_map/ppermute | solution.py:294
  14.6 5.2 %collective-permute-start.9 = (bf16[1,2,128,128]{3,2,1,0:T(8,128)(2,1)S(1)}, bf16[1,2,128,128]{3,2,1,0:T(8,128)(2,1)S(1)}, u32[]{:S(2)}, u32[]{:S(2)}) collective-permute-start(bf16[1,2,128,128]{3,2,1,0:T(8,128)(2,1)S(1)} %bitcast.19), channel_id=1, source_target_pairs={{0,1},{1,0},{2,3},{3,2},{4,5},{5,4},{6,7},{7,6},{8,9},{9,8},{10,11... | collective-permute-start | bytes 196616 | tf_op jit(solution)/shard_map/ppermute | solution.py:294
  15.1 4.7 %collective-permute-start.8 = (bf16[1,2,128,128]{3,2,1,0:T(8,128)(2,1)S(1)}, bf16[1,2,128,128]{3,2,1,0:T(8,128)(2,1)S(1)}, u32[]{:S(2)}, u32[]{:S(2)}) collective-permute-start(bf16[1,2,128,128]{3,2,1,0:T(8,128)(2,1)S(1)} %bitcast.21), channel_id=1, source_target_pairs={{0,1},{1,0},{2,3},{3,2},{4,5},{5,4},{6,7},{7,6},{8,9},{9,8},{10,11... | collective-permute-start | bytes 196616 | tf_op jit(solution)/shard_map/ppermute | solution.py:294
  15.2 4.6 %collective-permute-start.7 = (bf16[1,2,128,128]{3,2,1,0:T(8,128)(2,1)S(1)}, bf16[1,2,128,128]{3,2,1,0:T(8,128)(2,1)S(1)}, u32[]{:S(2)}, u32[]{:S(2)}) collective-permute-start(bf16[1,2,128,128]{3,2,1,0:T(8,128)(2,1)S(1)} %bitcast.23), channel_id=1, source_target_pairs={{0,1},{1,0},{2,3},{3,2},{4,5},{5,4},{6,7},{7,6},{8,9},{9,8},{10,11... | collective-permute-start | bytes 196616 | tf_op jit(solution)/shard_map/ppermute | solution.py:294
  34.5 5.6 %collective-permute-start.13 = (bf16[2,128,128]{2,1,0:T(8,128)(2,1)S(1)}, bf16[2,128,128]{2,1,0:T(8,128)(2,1)S(1)}, u32[]{:S(2)}, u32[]{:S(2)}) collective-permute-start(bf16[2,128,128]{2,1,0:T(8,128)(2,1)S(1)} %get-tuple-element.18.refs_0_), channel_id=1, source_target_pairs={{24,0},{16,8},{8,16},{0,24},{25,1},{17,9},{9,17},{1,25},{26,2},{18... | collective-permute-start | bytes 196616 | tf_op jit(solution)/shard_map/ppermute | solution.py:277
  35.1 5.0 %collective-permute-start.12 = (bf16[2,128,128]{2,1,0:T(8,128)(2,1)S(1)}, bf16[2,128,128]{2,1,0:T(8,128)(2,1)S(1)}, u32[]{:S(2)}, u32[]{:S(2)}) collective-permute-start(bf16[2,128,128]{2,1,0:T(8,128)(2,1)S(1)} %get-tuple-element.18.refs_0_), channel_id=1, source_target_pairs={{16,0},{24,8},{0,16},{8,24},{17,1},{25,9},{1,17},{9,25},{18,2},{26... | collective-permute-start | bytes 196616 | tf_op jit(solution)/shard_map/ppermute | solution.py:277
  36.6 4.3 %collective-permute-start.11 = (bf16[2,128,128]{2,1,0:T(8,128)(2,1)S(1)}, bf16[2,128,128]{2,1,0:T(8,128)(2,1)S(1)}, u32[]{:S(2)}, u32[]{:S(2)}) collective-permute-start(bf16[2,128,128]{2,1,0:T(8,128)(2,1)S(1)} %get-tuple-element.18.refs_0_), channel_id=1, source_target_pairs={{8,0},{0,8},{24,16},{16,24},{9,1},{1,9},{25,17},{17,25},{10,2},{2,... | collective-permute-start | bytes 196616 | tf_op jit(solution)/shard_map/ppermute | solution.py:277

commit v5 on v4

v5 whole, which is shorter than its diff:
```python
import functools

import jax
import jax.numpy as jnp
from jax import lax
from jax.experimental import pallas as pl
from jax.experimental.pallas import tpu as pltpu
from jax.sharding import PartitionSpec as P

EPS = 1e-06
SCALE = 2.0**-12
UNSCALE = 2.0**12
ROWS = 64
LANES = 128

POWERS = ((0, 0), (0, 1), (1, 0), (1, 1))
N0, E0 = 0, 1
N1, E1 = 2, 5
N2, E2 = 8, 17
N3 = 26


def split(x):
    high = x.astype(jnp.bfloat16)
    low = (x - high.astype(jnp.float32)).astype(jnp.bfloat16)
    return jnp.concatenate([high, low], axis=1)


def fold(x):
    return functools.reduce(lambda a, b: a + b, [x[r : r + 8] for r in range(0, x.shape[0], 8)])


def stack_right(plan, right_cat, right_refs, g, width):
    depth = right_refs[0].shape[1]
    for k in range(plan.owners * depth):
        rows, ref = slice(k * width, (k + 1) * width), right_refs[plan.places[k // depth]]
        for half in range(2):
            right_cat[rows, half * width : (half + 1) * width] = ref[g, k % depth]


def levels(left_cat, right_cats, sums, basis_ref, slots, starts, inverses):
    width = starts[0].shape[0]
    terms = left_cat.shape[1] // width
    some = range(len(starts))

    def apply(vectors):
        columns = []
        for b in some:
            stacked = jnp.concatenate(vectors[b], axis=0)
            images = lax.dot_general(
                stacked,
                right_cats[b][:, : stacked.shape[1]],
                (((1,), (1,)), ((), ())),
                preferred_element_type=jnp.float32,
            ).astype(jnp.bfloat16)
            for n in range(len(vectors[b])):
                rows = images[n * width : (n + 1) * width]
                columns.append(jnp.concatenate([rows[:, k * width : (k + 1) * width] for k in range(terms)], axis=0))
        out = jnp.dot(left_cat[...], jnp.concatenate(columns, axis=1), preferred_element_type=jnp.float32)
        count = len(vectors[0])
        return [[out[:, (b * count + n) * width : (b * count + n + 1) * width] for n in range(count)] for b in some]

    def add(slot, value):
        sums[slot * 8 : slot * 8 + 8] += value

    def put(table, at, value):
        table[at] = value if table[at] is None else table[at] + value

    def advance(vectors, images):
        level = []
        for b in some:
            level.append([])
            for x, h in zip(vectors[b], images[b]):
                level[b] += [SCALE * x - (SCALE * inverses[b]) * h, inverses[b] * x]
        return level

    images = apply([[start] for start in starts])
    zeroth = [[start.astype(jnp.float32)] for start in starts]
    for b in some:
        add(N0, fold(zeroth[b][0] * zeroth[b][0]))
        add(E0, fold(zeroth[b][0] * images[b][0]))
    first = advance(zeroth, images)

    images = apply([[split(x) for x in vectors] for vectors in first])
    for b in some:
        for m in range(2):
            for n in range(2):
                if m <= n:
                    add(N1 + m + n, (1.0 if m == n else 2.0) * fold(first[b][m] * first[b][n]))
                add(E1 + m + n, fold(first[b][m] * images[b][n]))
    second = advance(first, images)

    images = apply([[split(x) for x in vectors] for vectors in second])
    third = advance(second, images)
    for b in some:
        for m in range(8):
            basis_ref[m, slots[b]] = third[b][m]
        norm, energy, last = [None] * 9, [None] * 9, [None] * 27
        for m in range(4):
            for n in range(4):
                a0, a1 = POWERS[m][0] + POWERS[n][0], POWERS[m][1] + POWERS[n][1]
                put(energy, 3 * a0 + a1, fold(second[b][m] * images[b][n]))
                if m <= n:
                    put(norm, 3 * a0 + a1, (1.0 if m == n else 2.0) * fold(second[b][m] * second[b][n]))
                for d in range(2):
                    for e in range(2):
                        if (m, d) <= (n, e):
                            scale = 1.0 if (m, d) == (n, e) else 2.0
                            put(last, 9 * a0 + 3 * a1 + d + e, scale * fold(third[b][2 * m + d] * third[b][2 * n + e]))
        for at in range(9):
            add(N2 + at, norm[at])
            add(E2 + at, energy[at])
        for at in range(27):
            add(N3 + at, last[at])


def each_group(groups, body):
    if groups == 1:
        body(0)
    else:
        pl.loop(0, groups)(body)


def prepare_kernel(plan, sizes_hbm, psi_hbm, pre_hbm, *refs):
    own_refs, refs = refs[: plan.owners], refs[plan.owners :]
    own_cat, start_ref, inverse_ref, sizes_ref, psi_ref, pre_ref, sems = refs
    width = psi_ref.shape[-1]
    row = lax.axis_index("sector")
    core = row % 2
    chip = plan.first_chip(lax.axis_index("term"), row // 2)
    blocks = pl.ds(2 * chip, psi_ref.shape[0])
    copies = [
        pltpu.make_async_copy(sizes_hbm, sizes_ref, sems.at[0]),
        pltpu.make_async_copy(psi_hbm.at[blocks], psi_ref, sems.at[1]),
        pltpu.make_async_copy(pre_hbm.at[blocks], pre_ref, sems.at[2]),
    ]
    for copy in copies:
        copy.start()
    each_group(plan.groups, lambda g: stack_right(plan, own_cat.at[g], own_refs, g, psi_ref.shape[-1]))
    for copy in copies:
        copy.wait()
    row_ids = lax.broadcasted_iota(jnp.int32, (width, width), 0)
    col_ids = lax.broadcasted_iota(jnp.int32, (width, width), 1)

    def body(g):
        for b in range(2):
            block = 2 * g + (core if b == 0 else 1 - core)
            valid = (row_ids < sizes_ref[row]) & (col_ids < sizes_ref[2 * chip + block])
            start_ref[b, g] = jnp.where(valid, psi_ref[block].astype(jnp.float32), 0.0).astype(jnp.bfloat16)
            inverse_ref[b, g] = jnp.where(valid, 1.0 / pre_ref[block].astype(jnp.float32), 0.0)

    each_group(plan.groups, body)


def levels_kernel(plan, pieces, own_cat, start_ref, inverse_ref, *refs):
    left_refs, swap_refs, refs = refs[:pieces], refs[pieces : pieces + plan.owners], refs[pieces + plan.owners :]
    gram_ref, basis_ref, left_cat, swap_cat, sums = refs
    width = left_cat.shape[0]
    sums[...] = jnp.zeros_like(sums)
    for k, (ref, at) in enumerate((ref, at) for ref in left_refs for at in range(ref.shape[0])):
        left_cat[:, k * width : (k + 1) * width] = ref[at]

    def body(g):
        stack_right(plan, swap_cat, swap_refs, g, width)
        starts = [start_ref[b, g] for b in range(2)]
        inverses = [inverse_ref[b, g] for b in range(2)]
        levels(left_cat, (own_cat.at[g], swap_cat), sums, basis_ref, (2 * g, 2 * g + 1), starts, inverses)

    each_group(plan.groups, body)
    folded = functools.reduce(lambda a, b: a + b, [sums[pl.ds(s, ROWS, stride=8), :] for s in range(8)])
    totals = jnp.sum(folded, axis=1, keepdims=True)
    row_ids = lax.broadcasted_iota(jnp.int32, (ROWS, LANES), 0)
    col_ids = lax.broadcasted_iota(jnp.int32, (ROWS, LANES), 1)
    line = jnp.sum(jnp.where(row_ids == col_ids, totals, 0.0), axis=0, keepdims=True)
    gram_ref[...] = jnp.broadcast_to(line, gram_ref.shape)


def finish_kernel(count, gram_ref, basis_ref, out_ref, energy_ref):
    core = lax.axis_index("sector") % 2
    share = out_ref.shape[0]
    gram = jnp.sum(gram_ref[...], axis=0, keepdims=True)
    lane = lax.broadcasted_iota(jnp.int32, (1, LANES), 1)

    def total(base, size, weight):
        inside = (lane >= base) & (lane < base + size)
        return jnp.sum(jnp.where(inside, gram * weight, 0.0), axis=1, keepdims=True)

    def power(exponent, value):
        return jnp.where(exponent == 0, 1.0, jnp.where(exponent == 1, value, value * value))

    theta0 = total(E0, 1, 1.0) / total(N0, 1, 1.0)
    tau0 = SCALE * theta0
    norm1 = total(N1, 3, power(lane - N1, tau0))
    theta1 = total(E1, 3, power(lane - E1, tau0)) / norm1
    tau1 = SCALE * theta1

    def weight2(base):
        at = lane - base
        return power(at // 3, tau0) * power(at % 3, tau1)

    norm2 = total(N2, 9, weight2(N2))
    theta2 = total(E2, 9, weight2(E2)) / norm2
    tau2 = SCALE * theta2
    at = lane - N3
    norm3 = total(N3, 27, power(at // 9, tau0) * power(at // 3 % 3, tau1) * power(at % 3, tau2))

    def factor(gain, norm):
        return lax.rsqrt(gain * gain * jnp.maximum(norm, 0.0) / count + EPS)

    gain = jnp.full((1, 1), UNSCALE, jnp.float32)
    gain = factor(gain, norm1) * gain * UNSCALE
    gain = factor(gain, norm2) * gain * UNSCALE
    gain = factor(gain, norm3) * gain
    weights = [gain, gain * tau1, gain * tau0, gain * tau0 * tau1]
    for at in range(share):
        even = at % 2 == 0
        value = None
        for m in range(4):
            part = weights[m] * (basis_ref[2 * m, at] + tau2 * basis_ref[2 * m + 1, at])
            value = part if value is None else value + part
        block = (at // 2) * 2 + (core if even else 1 - core)
        out_ref[block] = value.astype(jnp.bfloat16)
    energy_ref[...] = jnp.where(lane == 0, theta0, jnp.where(lane == 1, theta1, theta2))


def assemble_kernel(plan, *refs):
    pieces, out_ref, sems = refs[: plan.owners], refs[plan.owners], refs[plan.owners + 1]
    share = pieces[0].shape[0]
    term, chip = lax.axis_index("term"), lax.axis_index("sector") // 2
    copies = []
    for m in range(plan.owners):
        first = plan.first_chip(plan.hop(term, m), chip) * 2
        copies.append(pltpu.make_async_copy(pieces[m], out_ref.at[pl.ds(first, share)], sems.at[m]))
        copies[-1].start()
    for copy in copies:
        copy.wait()


class Plan:
    def __init__(self, owners, sectors):
        self.owners, self.sectors, self.chips = owners, sectors, sectors // 2
        self.groups = self.chips // owners
        self.direct = self.groups == 1 and owners > 1 and owners & (owners - 1) == 0
        self.bits = [1 << b for b in reversed(range(owners.bit_length() - 1))]
        self.order = (0, 3, 1, 2) if self.direct and owners == 4 else tuple(range(owners))
        offsets = [0]
        for bit in self.bits if self.direct else []:
            offsets = offsets + [offset ^ bit for offset in offsets]
        self.places = [self.order.index(offset) for offset in offsets] if self.direct else self.order
        if owners == 4:
            self.spread = ((0, 2, 1, 3), (1, 3, 0, 2), (2, 0, 3, 1), (3, 1, 2, 0))
        else:
            self.spread = tuple(tuple((q + t) % owners for q in range(owners)) for t in range(owners))

    def hop(self, term, offset):
        if self.owners & (self.owners - 1) == 0:
            return term ^ offset
        return (term + offset) % self.owners

    def back(self, offset):
        if self.owners & (self.owners - 1) == 0:
            return offset
        return (self.owners - offset) % self.owners

    def first_chip(self, term, chip):
        if not self.direct:
            return term * self.groups
        found = jnp.int32(0)
        for t in range(self.owners):
            for q in range(self.owners):
                hit = (term == t) & (chip == self.spread[t][q])
                found = jnp.where(hit, q, found)
        return found


def from_owner(plan, value, offset):
    if offset == 0:
        return value
    moves = [(plan.hop(t, offset), t) for t in range(plan.owners)]
    return lax.ppermute(value, "term", moves)


def inputs(plan, left, right):
    sectors, owners, groups = plan.sectors, plan.owners, plan.groups
    cores = [(i, i ^ 1) for i in range(sectors)]
    if plan.direct:
        held = left
        for bit in plan.bits:
            lefts = [held, from_owner(plan, held, bit)]
            held = jnp.concatenate(lefts, axis=0)
        own = {}
        for m in plan.order:
            moves = []
            for t in range(owners):
                for q in range(plan.chips):
                    for c in range(2):
                        source = plan.hop(t, m) * sectors + 2 * q + c
                        moves.append((source, t * sectors + 2 * plan.spread[t][q] + c))
            own[m] = lax.ppermute(right, ("term", "sector"), moves)[None]
        own = [own[m] for m in plan.order]
        swapped = [lax.ppermute(x, "sector", cores) for x in own]
        return lefts, own, swapped
    everything = lax.all_gather(right, "sector").reshape((owners, groups, 2) + right.shape)
    by_chip = lax.dynamic_index_in_dim(everything, lax.axis_index("sector") % 2, 2, keepdims=False)
    spread_left = jnp.broadcast_to(left, (owners, 1) + left.shape)
    got = lax.all_to_all(jnp.concatenate([by_chip, spread_left], axis=1), "term", 0, 0)
    swapped = lax.ppermute(got[:, :groups], "sector", cores)
    lefts = [got[t, groups] for t in range(owners)]
    own = [got[t, :groups] for t in range(owners)]
    return lefts, own, [swapped[t] for t in range(owners)]


def local(plan, psi, left_env, right_env, precond, block_sizes):
    owners, sectors = plan.owners, plan.sectors
    devices = owners * sectors
    depth, width = right_env.shape[0], right_env.shape[-1]
    share = 2 * plan.groups
    lefts, own, swapped = inputs(plan, left_env[:, 0], right_env[:, 0])
    pieces = len(lefts)

    anywhere = pl.BlockSpec(memory_space=pltpu.HBM)
    vmem = pl.BlockSpec(memory_space=pltpu.VMEM)
    parked = [pltpu.with_memory_space_constraint(x, pltpu.HBM) for x in (block_sizes, psi[0], precond[0])]
    terms, groups = owners * depth, plan.groups
    params = pltpu.CompilerParams(vmem_limit_bytes=32 << 20)
    prepared = pl.pallas_call(
        functools.partial(prepare_kernel, plan),
        out_shape=(
            jax.ShapeDtypeStruct((groups, terms * width, 2 * width), jnp.bfloat16),
            jax.ShapeDtypeStruct((2, groups, width, width), jnp.bfloat16),
            jax.ShapeDtypeStruct((2, groups, width, width), jnp.float32),
        ),
        in_specs=[anywhere] * 3 + [vmem] * owners,
        out_specs=(vmem,) * 3,
        scratch_shapes=[
            pltpu.SMEM((sectors,), jnp.int32),
            pltpu.VMEM((share, width, width), jnp.bfloat16),
            pltpu.VMEM((share, width, width), jnp.bfloat16),
            pltpu.SemaphoreType.DMA((3,)),
        ],
        compiler_params=params,
        name="prepare",
    )(*parked, *own)
    gram, basis = pl.pallas_call(
        functools.partial(levels_kernel, plan, pieces),
        out_shape=(
            jax.ShapeDtypeStruct((devices, LANES), jnp.float32),
            jax.ShapeDtypeStruct((8, share, width, width), jnp.float32),
        ),
        in_specs=[vmem] * (3 + pieces + owners),
        out_specs=(vmem, vmem),
        scratch_shapes=[
            pltpu.VMEM((width, terms * width), jnp.bfloat16),
            pltpu.VMEM((terms * width, 2 * width), jnp.bfloat16),
            pltpu.VMEM((ROWS * 8, LANES), jnp.float32),
        ],
        compiler_params=params,
        name="levels",
    )(*prepared, *lefts, *swapped)
    gram = lax.all_to_all(gram, ("term", "sector"), 0, 0, tiled=True)
    count = float(sectors * sectors * width * width)
    blocks, energy = pl.pallas_call(
        functools.partial(finish_kernel, count),
        out_shape=(
            jax.ShapeDtypeStruct((share, width, width), jnp.bfloat16),
            jax.ShapeDtypeStruct((1, LANES), jnp.float32),
        ),
        in_specs=[vmem, vmem],
        out_specs=(vmem, vmem),
        compiler_params=params,
        name="finish",
    )(gram, basis)
    state = pl.pallas_call(
        functools.partial(assemble_kernel, plan),
        out_shape=jax.ShapeDtypeStruct((sectors, width, width), jnp.bfloat16),
        in_specs=[vmem] * owners,
        out_specs=anywhere,
        scratch_shapes=[pltpu.SemaphoreType.DMA((owners,))],
        compiler_params=pltpu.CompilerParams(vmem_limit_bytes=16 << 20),
        name="assemble",
    )(*[from_owner(plan, blocks, m) for m in range(owners)])
    return (state[None], energy[0, :3])


def solution(mesh):
    in_specs = (
        P("sector", None, None, None),
        P("term", "sector", None, None),
        P("term", "sector", None, None),
        P("sector", None, None, None),
        P(),
    )
    out_specs = (P("sector", None, None, None), P())
    return jax.shard_map(
        functools.partial(local, Plan(mesh.shape["term"], mesh.shape["sector"])),
        mesh=mesh,
        in_specs=in_specs,
        out_specs=out_specs,
        check_vma=False,
    )
```

time: 41.8 us -> 39.5 us (0.945)
  blocking collectives: 12.4 us -> 10.5 us
  Pallas kernels: 5.62 us -> 4.58 us
  other arithmetic: 0 us -> 0.85 us
  waiting for transfers between devices: 3.76 us -> 3.18 us
    all_to_all x1, blocking collectives: 12.4 us -> 10.5 us  [local(): gram = lax.all_to_all(gram, ('term', 'sector'), 0, 0, tiled=True)]
    ppermute x4, starting transfers between devices: 7 us -> 8.8 us  [inputs(): own[m] = lax.ppermute(right, ('term', 'sector'), moves)[None]]
    ppermute x6 -> x5, starting transfers between devices: 10.5 us -> 9.13 us  [from_owner(): return lax.ppermute(value, 'term', moves)]
    pallas_call x2, Pallas kernels: 4.51 us -> 3.46 us  [the longest x1 2.45 us: local(): pl.pallas_call(functools.partial(levels_kernel, plan, pieces), out_shape=...]
    concatenate x0 -> x1, other arithmetic: none -> 0.85 us  [inputs(): held = jnp.concatenate(lefts, axis=0)]
    ppermute x6 -> x5, waiting for transfers between devices: 3.74 us -> 3.16 us  [from_owner(): return lax.ppermute(value, 'term', moves)]
  transfers between devices with their start and end apart: 14 -> 13, of which waited for: 4 -> 4; matrix products, arithmetic and copies ran while one was open for 1% -> 3% of each run, Pallas kernels for 7% -> 3%
where the time goes in v5:
time: 39.5 us; the launch traced here: 39.3 us
  starting transfers between devices  18.9 us (48%)
  blocking collectives  10.5 us (27%)
  Pallas kernels  4.58 us (12%)
  waiting for transfers between devices  3.18 us (8%)
  other arithmetic  0.85 us (2%)
  between operations  0.7 us (2%)
  local copies, waits for them, and re-layouts  0.51 us (1%)
    all_to_all x1, blocking collectives, local(): gram = lax.all_to_all(gram, ('term', 'sector'), 0, 0, tiled=True)  10.5 us
    ppermute x5, starting transfers between devices, from_owner(): return lax.ppermute(value, 'term', moves)  9.13 us
    ppermute x4, starting transfers between devices, inputs(): own[m] = lax.ppermute(right, ('term', 'sector'), moves)[None]  8.8 us
    ppermute x5, waiting for transfers between devices, from_owner(): return lax.ppermute(value, 'term', moves)  3.16 us
    pallas_call x1, Pallas kernels, local(): pl.pallas_call(functools.partial(levels_kernel, plan, pieces), out_shape=...  2.45 us
    ppermute x4, starting transfers between devices, inputs(): swapped = [lax.ppermute(x, 'sector', cores) for x in own]  1.02 us
    pallas_call x1, Pallas kernels, local(): pl.pallas_call(functools.partial(prepare_kernel, plan), out_shape=(jax.Sh...  1.01 us
    concatenate x1, other arithmetic, inputs(): held = jnp.concatenate(lefts, axis=0)  0.85 us
  transfers between devices with their start and end apart: 13, of which 4 were waited for; matrix products, arithmetic and copies ran while one was open for 3% of the time, Pallas kernels for 3%

profile of v5, /device:TPU:0, one launch (start us, length us, event | category | flops | bytes accessed | tf_op | source)
XLA Modules:
  0.0 39.3 jit_solution(14787628127423835899)
XLA Ops:
  0.6 3.0 %collective-permute-start.4 = (bf16[2,128,128]{2,1,0:T(8,128)(2,1)}, bf16[2,128,128]{2,1,0:T(8,128)(2,1)S(1)}, u32[]{:S(2)}, u32[]{:S(2)}) collective-permute-start(bf16[2,128,128]{2,1,0:T(8,128)(2,1)} %bitcast.28), channel_id=1, source_target_pairs={{16,0},{24,8},{0,16},{8,24},{17,1},{25,9},{1,17},{9,25},{18,2},{26... | collective-permute-start | bytes 196616 | tf_op jit(solution)/shard_map/ppermute | solution.py:280
  3.7 2.5 %collective-permute-start.3 = (bf16[2,128,128]{2,1,0:T(8,128)(2,1)}, bf16[2,128,128]{2,1,0:T(8,128)(2,1)S(1)}, u32[]{:S(2)}, u32[]{:S(2)}) collective-permute-start(bf16[2,128,128]{2,1,0:T(8,128)(2,1)} %bitcast.30), channel_id=1, source_target_pairs={{16,0},{17,1},{18,4},{19,5},{20,2},{21,3},{22,6},{23,7},{24,10},{2... | collective-permute-start | bytes 196616 | tf_op jit(solution)/shard_map/ppermute | solution.py:299
  6.2 0.5 %collective-permute-start.2 = (bf16[2,128,128]{2,1,0:T(8,128)(2,1)}, bf16[2,128,128]{2,1,0:T(8,128)(2,1)S(1)}, u32[]{:S(2)}, u32[]{:S(2)}) collective-permute-start(bf16[2,128,128]{2,1,0:T(8,128)(2,1)} %bitcast.31), channel_id=1, source_target_pairs={{8,0},{9,1},{10,4},{11,5},{12,2},{13,3},{14,6},{15,7},{0,10},{1,11... | collective-permute-start | bytes 196616 | tf_op jit(solution)/shard_map/ppermute | solution.py:299
  6.7 4.3 %collective-permute-start.1 = (bf16[2,128,128]{2,1,0:T(8,128)(2,1)}, bf16[2,128,128]{2,1,0:T(8,128)(2,1)S(1)}, u32[]{:S(2)}, u32[]{:S(2)}) collective-permute-start(bf16[2,128,128]{2,1,0:T(8,128)(2,1)} %bitcast.32), channel_id=1, source_target_pairs={{24,0},{25,1},{26,4},{27,5},{28,2},{29,3},{30,6},{31,7},{16,10},{1... | collective-permute-start | bytes 196616 | tf_op jit(solution)/shard_map/ppermute | solution.py:299
  11.0 1.5 %collective-permute-start = (bf16[2,128,128]{2,1,0:T(8,128)(2,1)}, bf16[2,128,128]{2,1,0:T(8,128)(2,1)S(1)}, u32[]{:S(2)}, u32[]{:S(2)}) collective-permute-start(bf16[2,128,128]{2,1,0:T(8,128)(2,1)} %bitcast.33), channel_id=1, source_target_pairs={{0,0},{1,1},{2,4},{3,5},{4,2},{5,3},{6,6},{7,7},{8,10},{9,11},{10,... | collective-permute-start | bytes 196616 | tf_op jit(solution)/shard_map/ppermute | solution.py:299
  12.5 0.0 collective-permute-done.4
  12.5 0.9 %pad_maximum_fusion.refs_0_ = bf16[4,128,128]{2,1,0:T(8,128)(2,1)S(1)} fusion(bf16[2,128,128]{2,1,0:T(8,128)(2,1)S(1)} %collective-permute-done.4, bf16[2,128,128]{2,1,0:T(8,128)(2,1)} %bitcast.29), kind=kLoop, calls=%fused_computation | loop fusion | flops 65536 | bytes 262144 | tf_op jit(solution)/shard_map/concatenate | solution.py:290
  13.3 2.5 %collective-permute-start.5 = (bf16[4,128,128]{2,1,0:T(8,128)(2,1)S(1)}, bf16[4,128,128]{2,1,0:T(8,128)(2,1)S(1)}, u32[]{:S(2)}, u32[]{:S(2)}) collective-permute-start(bf16[4,128,128]{2,1,0:T(8,128)(2,1)S(1)} %pad_maximum_fusion.refs_0_), channel_id=1, source_target_pairs={{8,0},{0,8},{24,16},{16,24},{9,1},{1,9},{25,17},{17,25},{10,2},{2,... | collective-permute-start | bytes 393224 | tf_op jit(solution)/shard_map/ppermute | solution.py:280
  15.9 0.0 collective-permute-done.3
  15.9 0.0 collective-permute-start.9
  15.9 0.0 collective-permute-done.2
  15.9 0.5 %collective-permute-start.8 = (bf16[1,2,128,128]{3,2,1,0:T(8,128)(2,1)S(1)}, bf16[1,2,128,128]{3,2,1,0:T(8,128)(2,1)S(1)}, u32[]{:S(2)}, u32[]{:S(2)}) collective-permute-start(bf16[1,2,128,128]{3,2,1,0:T(8,128)(2,1)S(1)} %bitcast.18), channel_id=1, source_target_pairs={{0,1},{1,0},{2,3},{3,2},{4,5},{5,4},{6,7},{7,6},{8,9},{9,8},{10,11... | collective-permute-start | bytes 196616 | tf_op jit(solution)/shard_map/ppermute | solution.py:301
  16.4 0.0 collective-permute-done.1
  16.4 0.1 collective-permute-start.7
  16.5 0.0 collective-permute-done
  16.5 0.4 %collective-permute-start.6 = (bf16[1,2,128,128]{3,2,1,0:T(8,128)(2,1)S(1)}, bf16[1,2,128,128]{3,2,1,0:T(8,128)(2,1)S(1)}, u32[]{:S(2)}, u32[]{:S(2)}) collective-permute-start(bf16[1,2,128,128]{3,2,1,0:T(8,128)(2,1)S(1)} %bitcast.22), channel_id=1, source_target_pairs={{0,1},{1,0},{2,3},{3,2},{4,5},{5,4},{6,7},{7,6},{8,9},{9,8},{10,11... | collective-permute-start | bytes 196616 | tf_op jit(solution)/shard_map/ppermute | solution.py:301
  16.9 1.0 %prepare.1 = (bf16[1,1024,256]{2,1,0:T(8,128)(2,1)S(1)}, bf16[2,1,128,128]{3,2,1,0:T(8,128)(2,1)S(1)}, f32[2,1,128,128]{3,2,1,0:T(8,128)S(1)}) custom-call(s32[8]{0:T(128)} %sizes_hbm.1, bf16[8,128,128]{2,1,0:T(8,128)(2,1)} %bitcast.26, bf16[8,128,128]{2,1,0:T(8,128)(2,1)} %bitcast.27, bf16[1,2,128,128]{3,2,1,0:T(8,128)(2,1)S(1)} %bitcast.23, ...), custom_call_target="tpu_custom_call" | custom-call | tf_op jit(solution)/shard_map/prepare/pallas_call | solution.py:326
  17.9 0.0 collective-permute-done.9.refs_5_
  17.9 0.0 collective-permute-done.8.refs_4_
  17.9 0.0 collective-permute-done.7.refs_3_
  18.0 0.8 %collective-permute-done.5.refs_1_ = bf16[4,128,128]{2,1,0:T(8,128)(2,1)S(1)} collective-permute-done((bf16[4,128,128]{2,1,0:T(8,128)(2,1)S(1)}, bf16[4,128,128]{2,1,0:T(8,128)(2,1)S(1)}, u32[]{:S(2)}, u32[]{:S(2)}) %collective-permute-start.5) | collective-permute-done | bytes 131104 | tf_op jit(solution)/shard_map/ppermute | solution.py:280
  18.8 2.4 %levels.1 = (f32[32,128]{1,0:T(8,128)S(1)}, f32[8,2,128,128]{3,2,1,0:T(8,128)S(1)}) custom-call(bf16[1,1024,256]{2,1,0:T(8,128)(2,1)S(1)} %get-tuple-element.9.own_cat, bf16[2,1,128,128]{3,2,1,0:T(8,128)(2,1)S(1)} %get-tuple-element.10.start_ref, f32[2,1,128,128]{3,2,1,0:T(8,128)S(1)} %get-tuple-element.11.inverse_ref, ...), custom_call_target="tpu_custom_call" | custom-call | tf_op jit(solution)/shard_map/levels/pallas_call | solution.py:344
  21.3 10.5 %all_to_all.11 = f32[32,1,128]{2,1,0:T(1,128)S(1)} all-to-all(f32[32,1,128]{2,1,0:T(1,128)S(1)} %bitcast.24), channel_id=1, replica_groups=mesh['term'=4,'sector'=8] {'term','sector'}, dimensions={0} | all-to-all | bytes 32768 | tf_op jit(solution)/shard_map/all_to_all | solution.py:360
  31.8 0.4 finish.1
  32.2 0.7 %collective-permute-start.12 = (bf16[2,128,128]{2,1,0:T(8,128)(2,1)S(1)}, bf16[2,128,128]{2,1,0:T(8,128)(2,1)S(1)}, u32[]{:S(2)}, u32[]{:S(2)}) collective-permute-start(bf16[2,128,128]{2,1,0:T(8,128)(2,1)S(1)} %get-tuple-element.14.refs_0_), channel_id=1, source_target_pairs={{24,0},{16,8},{8,16},{0,24},{25,1},{17,9},{9,17},{1,25},{26,2},{18... | collective-permute-start | bytes 196616 | tf_op jit(solution)/shard_map/ppermute | solution.py:280
  32.8 1.4 %collective-permute-start.11 = (bf16[2,128,128]{2,1,0:T(8,128)(2,1)S(1)}, bf16[2,128,128]{2,1,0:T(8,128)(2,1)S(1)}, u32[]{:S(2)}, u32[]{:S(2)}) collective-permute-start(bf16[2,128,128]{2,1,0:T(8,128)(2,1)S(1)} %get-tuple-element.14.refs_0_), channel_id=1, source_target_pairs={{16,0},{24,8},{0,16},{8,24},{17,1},{25,9},{1,17},{9,25},{18,2},{26... | collective-permute-start | bytes 196616 | tf_op jit(solution)/shard_map/ppermute | solution.py:280
  34.3 1.4 %collective-permute-start.10 = (bf16[2,128,128]{2,1,0:T(8,128)(2,1)S(1)}, bf16[2,128,128]{2,1,0:T(8,128)(2,1)S(1)}, u32[]{:S(2)}, u32[]{:S(2)}) collective-permute-start(bf16[2,128,128]{2,1,0:T(8,128)(2,1)S(1)} %get-tuple-element.14.refs_0_), channel_id=1, source_target_pairs={{8,0},{0,8},{24,16},{16,24},{9,1},{1,9},{25,17},{17,25},{10,2},{2,... | collective-permute-start | bytes 196616 | tf_op jit(solution)/shard_map/ppermute | solution.py:280
  35.7 0.5 %slice_bitcast_fusion = f32[3]{0:T(128)} fusion(f32[1,128]{1,0:T(1,128)S(1)} %get-tuple-element.15), kind=kLoop, calls=%fused_computation.1 | loop fusion | bytes 24 | tf_op jit(solution)/shard_map/squeeze | solution.py:382
  36.2 1.5 %collective-permute-done.12.refs_3_ = bf16[2,128,128]{2,1,0:T(8,128)(2,1)S(1)} collective-permute-done((bf16[2,128,128]{2,1,0:T(8,128)(2,1)S(1)}, bf16[2,128,128]{2,1,0:T(8,128)(2,1)S(1)}, u32[]{:S(2)}, u32[]{:S(2)}) %collective-permute-start.12) | collective-permute-done | bytes 65568 | tf_op jit(solution)/shard_map/ppermute | solution.py:280
  37.7 0.1 collective-permute-done.11.refs_2_
  37.8 0.7 %collective-permute-done.10.refs_1_ = bf16[2,128,128]{2,1,0:T(8,128)(2,1)S(1)} collective-permute-done((bf16[2,128,128]{2,1,0:T(8,128)(2,1)S(1)}, bf16[2,128,128]{2,1,0:T(8,128)(2,1)S(1)}, u32[]{:S(2)}, u32[]{:S(2)}) %collective-permute-start.10) | collective-permute-done | bytes 65568 | tf_op jit(solution)/shard_map/ppermute | solution.py:280
  38.5 0.7 %assemble.1 = bf16[8,128,128]{2,1,0:T(8,128)(2,1)} custom-call(bf16[2,128,128]{2,1,0:T(8,128)(2,1)S(1)} %get-tuple-element.14.refs_0_, bf16[2,128,128]{2,1,0:T(8,128)(2,1)S(1)} %collective-permute-done.10.refs_1_, bf16[2,128,128]{2,1,0:T(8,128)(2,1)S(1)} %collective-permute-done.11.refs_2_, bf16[2,128,128]{2,1,0:T(8,128)(2,1)S(1)} %collective-permute-done.12.refs_3_), custom_call_target="tpu_custom_call" | custom-call | tf_op jit(solution)/shard_map/assemble/pallas_call | solution.py:373
  (1 shorter events, 0.0 us)
Async XLA Ops:
  0.6 11.8 %collective-permute-start.4 = (bf16[2,128,128]{2,1,0:T(8,128)(2,1)}, bf16[2,128,128]{2,1,0:T(8,128)(2,1)S(1)}, u32[]{:S(2)}, u32[]{:S(2)}) collective-permute-start(bf16[2,128,128]{2,1,0:T(8,128)(2,1)} %bitcast.28), channel_id=1, source_target_pairs={{16,0},{24,8},{0,16},{8,24},{17,1},{25,9},{1,17},{9,25},{18,2},{26... | collective-permute-start | bytes 196616 | tf_op jit(solution)/shard_map/ppermute | solution.py:280
  3.7 12.2 %collective-permute-start.3 = (bf16[2,128,128]{2,1,0:T(8,128)(2,1)}, bf16[2,128,128]{2,1,0:T(8,128)(2,1)S(1)}, u32[]{:S(2)}, u32[]{:S(2)}) collective-permute-start(bf16[2,128,128]{2,1,0:T(8,128)(2,1)} %bitcast.30), channel_id=1, source_target_pairs={{16,0},{17,1},{18,4},{19,5},{20,2},{21,3},{22,6},{23,7},{24,10},{2... | collective-permute-start | bytes 196616 | tf_op jit(solution)/shard_map/ppermute | solution.py:299
  6.2 9.7 %collective-permute-start.2 = (bf16[2,128,128]{2,1,0:T(8,128)(2,1)}, bf16[2,128,128]{2,1,0:T(8,128)(2,1)S(1)}, u32[]{:S(2)}, u32[]{:S(2)}) collective-permute-start(bf16[2,128,128]{2,1,0:T(8,128)(2,1)} %bitcast.31), channel_id=1, source_target_pairs={{8,0},{9,1},{10,4},{11,5},{12,2},{13,3},{14,6},{15,7},{0,10},{1,11... | collective-permute-start | bytes 196616 | tf_op jit(solution)/shard_map/ppermute | solution.py:299
  6.7 9.7 %collective-permute-start.1 = (bf16[2,128,128]{2,1,0:T(8,128)(2,1)}, bf16[2,128,128]{2,1,0:T(8,128)(2,1)S(1)}, u32[]{:S(2)}, u32[]{:S(2)}) collective-permute-start(bf16[2,128,128]{2,1,0:T(8,128)(2,1)} %bitcast.32), channel_id=1, source_target_pairs={{24,0},{25,1},{26,4},{27,5},{28,2},{29,3},{30,6},{31,7},{16,10},{1... | collective-permute-start | bytes 196616 | tf_op jit(solution)/shard_map/ppermute | solution.py:299
  11.0 5.5 %collective-permute-start = (bf16[2,128,128]{2,1,0:T(8,128)(2,1)}, bf16[2,128,128]{2,1,0:T(8,128)(2,1)S(1)}, u32[]{:S(2)}, u32[]{:S(2)}) collective-permute-start(bf16[2,128,128]{2,1,0:T(8,128)(2,1)} %bitcast.33), channel_id=1, source_target_pairs={{0,0},{1,1},{2,4},{3,5},{4,2},{5,3},{6,6},{7,7},{8,10},{9,11},{10,... | collective-permute-start | bytes 196616 | tf_op jit(solution)/shard_map/ppermute | solution.py:299
  13.3 5.5 %collective-permute-start.5 = (bf16[4,128,128]{2,1,0:T(8,128)(2,1)S(1)}, bf16[4,128,128]{2,1,0:T(8,128)(2,1)S(1)}, u32[]{:S(2)}, u32[]{:S(2)}) collective-permute-start(bf16[4,128,128]{2,1,0:T(8,128)(2,1)S(1)} %pad_maximum_fusion.refs_0_), channel_id=1, source_target_pairs={{8,0},{0,8},{24,16},{16,24},{9,1},{1,9},{25,17},{17,25},{10,2},{2,... | collective-permute-start | bytes 393224 | tf_op jit(solution)/shard_map/ppermute | solution.py:280
  15.9 2.1 %collective-permute-start.9 = (bf16[1,2,128,128]{3,2,1,0:T(8,128)(2,1)S(1)}, bf16[1,2,128,128]{3,2,1,0:T(8,128)(2,1)S(1)}, u32[]{:S(2)}, u32[]{:S(2)}) collective-permute-start(bf16[1,2,128,128]{3,2,1,0:T(8,128)(2,1)S(1)} %bitcast.16), channel_id=1, source_target_pairs={{0,1},{1,0},{2,3},{3,2},{4,5},{5,4},{6,7},{7,6},{8,9},{9,8},{10,11... | collective-permute-start | bytes 196616 | tf_op jit(solution)/shard_map/ppermute | solution.py:301
  15.9 2.1 %collective-permute-start.8 = (bf16[1,2,128,128]{3,2,1,0:T(8,128)(2,1)S(1)}, bf16[1,2,128,128]{3,2,1,0:T(8,128)(2,1)S(1)}, u32[]{:S(2)}, u32[]{:S(2)}) collective-permute-start(bf16[1,2,128,128]{3,2,1,0:T(8,128)(2,1)S(1)} %bitcast.18), channel_id=1, source_target_pairs={{0,1},{1,0},{2,3},{3,2},{4,5},{5,4},{6,7},{7,6},{8,9},{9,8},{10,11... | collective-permute-start | bytes 196616 | tf_op jit(solution)/shard_map/ppermute | solution.py:301
  16.4 1.6 %collective-permute-start.7 = (bf16[1,2,128,128]{3,2,1,0:T(8,128)(2,1)S(1)}, bf16[1,2,128,128]{3,2,1,0:T(8,128)(2,1)S(1)}, u32[]{:S(2)}, u32[]{:S(2)}) collective-permute-start(bf16[1,2,128,128]{3,2,1,0:T(8,128)(2,1)S(1)} %bitcast.20), channel_id=1, source_target_pairs={{0,1},{1,0},{2,3},{3,2},{4,5},{5,4},{6,7},{7,6},{8,9},{9,8},{10,11... | collective-permute-start | bytes 196616 | tf_op jit(solution)/shard_map/ppermute | solution.py:301
  16.5 1.5 %collective-permute-start.6 = (bf16[1,2,128,128]{3,2,1,0:T(8,128)(2,1)S(1)}, bf16[1,2,128,128]{3,2,1,0:T(8,128)(2,1)S(1)}, u32[]{:S(2)}, u32[]{:S(2)}) collective-permute-start(bf16[1,2,128,128]{3,2,1,0:T(8,128)(2,1)S(1)} %bitcast.22), channel_id=1, source_target_pairs={{0,1},{1,0},{2,3},{3,2},{4,5},{5,4},{6,7},{7,6},{8,9},{9,8},{10,11... | collective-permute-start | bytes 196616 | tf_op jit(solution)/shard_map/ppermute | solution.py:301
  32.2 5.6 %collective-permute-start.12 = (bf16[2,128,128]{2,1,0:T(8,128)(2,1)S(1)}, bf16[2,128,128]{2,1,0:T(8,128)(2,1)S(1)}, u32[]{:S(2)}, u32[]{:S(2)}) collective-permute-start(bf16[2,128,128]{2,1,0:T(8,128)(2,1)S(1)} %get-tuple-element.14.refs_0_), channel_id=1, source_target_pairs={{24,0},{16,8},{8,16},{0,24},{25,1},{17,9},{9,17},{1,25},{26,2},{18... | collective-permute-start | bytes 196616 | tf_op jit(solution)/shard_map/ppermute | solution.py:280
  32.8 5.0 %collective-permute-start.11 = (bf16[2,128,128]{2,1,0:T(8,128)(2,1)S(1)}, bf16[2,128,128]{2,1,0:T(8,128)(2,1)S(1)}, u32[]{:S(2)}, u32[]{:S(2)}) collective-permute-start(bf16[2,128,128]{2,1,0:T(8,128)(2,1)S(1)} %get-tuple-element.14.refs_0_), channel_id=1, source_target_pairs={{16,0},{24,8},{0,16},{8,24},{17,1},{25,9},{1,17},{9,25},{18,2},{26... | collective-permute-start | bytes 196616 | tf_op jit(solution)/shard_map/ppermute | solution.py:280
  34.3 4.3 %collective-permute-start.10 = (bf16[2,128,128]{2,1,0:T(8,128)(2,1)S(1)}, bf16[2,128,128]{2,1,0:T(8,128)(2,1)S(1)}, u32[]{:S(2)}, u32[]{:S(2)}) collective-permute-start(bf16[2,128,128]{2,1,0:T(8,128)(2,1)S(1)} %get-tuple-element.14.refs_0_), channel_id=1, source_target_pairs={{8,0},{0,8},{24,16},{16,24},{9,1},{1,9},{25,17},{17,25},{10,2},{2,... | collective-permute-start | bytes 196616 | tf_op jit(solution)/shard_map/ppermute | solution.py:280

commit v6 on v5

--- a/solution.py
+++ b/solution.py
@@ -152,6 +152,31 @@
     each_group(plan.groups, body)
 
 
+def join_kernel(own_hbm, *refs):
+    held_refs, out_ref, sem = refs[:-2], refs[-2], refs[-1]
+    base = own_hbm.shape[0]
+    copy = pltpu.make_async_copy(own_hbm, out_ref.at[:base], sem)
+    copy.start()
+    for ref in held_refs:
+        out_ref[base : base + ref.shape[0]] = ref[...]
+        base += ref.shape[0]
+    copy.wait()
+
+
+def join(own, *held):
+    rows = own.shape[0] + sum(x.shape[0] for x in held)
+    vmem = pl.BlockSpec(memory_space=pltpu.VMEM)
+    return pl.pallas_call(
+        join_kernel,
+        out_shape=jax.ShapeDtypeStruct((rows,) + own.shape[1:], own.dtype),
+        in_specs=[pl.BlockSpec(memory_space=pltpu.HBM)] + [vmem] * len(held),
+        out_specs=vmem,
+        scratch_shapes=[pltpu.SemaphoreType.DMA],
+        compiler_params=pltpu.CompilerParams(vmem_limit_bytes=16 << 20),
+        name="join",
+    )(pltpu.with_memory_space_constraint(own, pltpu.HBM), *held)
+
+
 def levels_kernel(plan, pieces, own_cat, start_ref, inverse_ref, *refs):
     left_refs, swap_refs, refs = refs[:pieces], refs[pieces : pieces + plan.owners], refs[pieces + plan.owners :]
     gram_ref, basis_ref, left_cat, swap_cat, sums = refs
@@ -242,13 +267,13 @@
         self.groups = self.chips // owners
         self.direct = self.groups == 1 and owners > 1 and owners & (owners - 1) == 0
         self.bits = [1 << b for b in reversed(range(owners.bit_length() - 1))]
-        self.order = (0, 3, 1, 2) if self.direct and owners == 4 else tuple(range(owners))
+        self.order = (0, 2, 3, 1) if self.direct and owners == 4 else tuple(range(owners))
         offsets = [0]
         for bit in self.bits if self.direct else []:
             offsets = offsets + [offset ^ bit for offset in offsets]
         self.places = [self.order.index(offset) for offset in offsets] if self.direct else self.order
         if owners == 4:
-            self.spread = ((0, 2, 1, 3), (1, 3, 0, 2), (2, 0, 3, 1), (3, 1, 2, 0))
+            self.spread = ((1, 0, 3, 2), (0, 2, 1, 3), (2, 3, 0, 1), (3, 1, 2, 0))
         else:
             self.spread = tuple(tuple((q + t) % owners for q in range(owners)) for t in range(owners))
 
@@ -284,10 +309,11 @@
     sectors, owners, groups = plan.sectors, plan.owners, plan.groups
     cores = [(i, i ^ 1) for i in range(sectors)]
     if plan.direct:
-        held = left
+        lefts, held = [left], []
         for bit in plan.bits:
-            lefts = [held, from_owner(plan, held, bit)]
-            held = jnp.concatenate(lefts, axis=0)
+            lefts = [join(left, *held) if held else left]
+            held.append(from_owner(plan, lefts[0], bit))
+        lefts.append(held[-1])
         own = {}
         for m in plan.order:
             moves = []

time: 39.5 us -> 39.2 us (level)
  starting transfers between devices: 18.9 us -> 16.5 us
  waiting for transfers between devices: 3.18 us -> 5.26 us
  other arithmetic: 0.85 us -> 0 us
  Pallas kernels: 4.58 us -> 5.43 us
    ppermute x5, starting transfers between devices: 9.13 us -> 7.04 us  [from_owner(): return lax.ppermute(value, 'term', moves)]
    ppermute x5, waiting for transfers between devices: 3.16 us -> 4.17 us  [from_owner(): return lax.ppermute(value, 'term', moves)]
    ppermute x4, waiting for transfers between devices: 0.01 us -> 0.89 us  [inputs(): own[m] = lax.ppermute(right, ('term', 'sector'), moves)[None]]
    concatenate x1 -> x0, other arithmetic: 0.85 us -> none  [inputs(): held = jnp.concatenate(lefts, axis=0)]
    pallas_call x0 -> x1, Pallas kernels: none -> 0.85 us  [join(): pl.pallas_call(join_kernel, out_shape=jax.ShapeDtypeStruct((rows,) + own....]
    ppermute x4, starting transfers between devices: 1.02 us -> 0.58 us  [inputs(): swapped = [lax.ppermute(x, 'sector', cores) for x in own]]
  transfers between devices with their start and end apart: 13 -> 13, of which waited for: 4 -> 6; matrix products, arithmetic and copies ran while one was open for 3% -> 1% of each run, Pallas kernels for 3% -> 5%
where the time goes in v6:
time: 39.2 us; the launch traced here: 38.9 us
  starting transfers between devices  16.5 us (42%)
  blocking collectives  10.5 us (27%)
  Pallas kernels  5.43 us (14%)
  waiting for transfers between devices  5.26 us (13%)
  between operations  0.71 us (2%)
  local copies, waits for them, and re-layouts  0.51 us (1%)
    all_to_all x1, blocking collectives, local(): gram = lax.all_to_all(gram, ('term', 'sector'), 0, 0, tiled=True)  10.5 us
    ppermute x4, starting transfers between devices, inputs(): own[m] = lax.ppermute(right, ('term', 'sector'), moves)[None]  8.87 us
    ppermute x5, starting transfers between devices, from_owner(): return lax.ppermute(value, 'term', moves)  7.04 us
    ppermute x5, waiting for transfers between devices, from_owner(): return lax.ppermute(value, 'term', moves)  4.17 us
    pallas_call x1, Pallas kernels, local(): pl.pallas_call(functools.partial(levels_kernel, plan, pieces), out_shape=...  2.45 us
    pallas_call x1, Pallas kernels, local(): pl.pallas_call(functools.partial(prepare_kernel, plan), out_shape=(jax.Sh...  1.01 us
    ppermute x4, waiting for transfers between devices, inputs(): own[m] = lax.ppermute(right, ('term', 'sector'), moves)[None]  0.89 us
    pallas_call x1, Pallas kernels, join(): pl.pallas_call(join_kernel, out_shape=jax.ShapeDtypeStruct((rows,) + own....  0.85 us
  transfers between devices with their start and end apart: 13, of which 6 were waited for; matrix products, arithmetic and copies ran while one was open for 1% of the time, Pallas kernels for 5%

profile of v6, /device:TPU:0, one launch (start us, length us, event | category | flops | bytes accessed | tf_op | source)
XLA Modules:
  0.0 38.9 jit_solution(2522989437973319105)
XLA Ops:
  0.6 3.0 %collective-permute-start.4 = (bf16[2,128,128]{2,1,0:T(8,128)(2,1)}, bf16[2,128,128]{2,1,0:T(8,128)(2,1)S(1)}, u32[]{:S(2)}, u32[]{:S(2)}) collective-permute-start(bf16[2,128,128]{2,1,0:T(8,128)(2,1)} %bitcast.28), channel_id=1, source_target_pairs={{16,0},{24,8},{0,16},{8,24},{17,1},{25,9},{1,17},{9,25},{18,2},{26... | collective-permute-start | bytes 196616 | tf_op jit(solution)/shard_map/ppermute | solution.py:305
  3.7 1.5 %collective-permute-start.3 = (bf16[2,128,128]{2,1,0:T(8,128)(2,1)}, bf16[2,128,128]{2,1,0:T(8,128)(2,1)S(1)}, u32[]{:S(2)}, u32[]{:S(2)}) collective-permute-start(bf16[2,128,128]{2,1,0:T(8,128)(2,1)} %bitcast.30), channel_id=1, source_target_pairs={{8,2},{9,3},{10,0},{11,1},{12,6},{13,7},{14,4},{15,5},{0,8},{1,9},... | collective-permute-start | bytes 196616 | tf_op jit(solution)/shard_map/ppermute | solution.py:325
  5.2 3.3 %collective-permute-start.2 = (bf16[2,128,128]{2,1,0:T(8,128)(2,1)}, bf16[2,128,128]{2,1,0:T(8,128)(2,1)S(1)}, u32[]{:S(2)}, u32[]{:S(2)}) collective-permute-start(bf16[2,128,128]{2,1,0:T(8,128)(2,1)} %bitcast.31), channel_id=1, source_target_pairs={{24,2},{25,3},{26,0},{27,1},{28,6},{29,7},{30,4},{31,5},{16,8},{17... | collective-permute-start | bytes 196616 | tf_op jit(solution)/shard_map/ppermute | solution.py:325
  8.4 0.5 %collective-permute-start.1 = (bf16[2,128,128]{2,1,0:T(8,128)(2,1)}, bf16[2,128,128]{2,1,0:T(8,128)(2,1)S(1)}, u32[]{:S(2)}, u32[]{:S(2)}) collective-permute-start(bf16[2,128,128]{2,1,0:T(8,128)(2,1)} %bitcast.32), channel_id=1, source_target_pairs={{16,2},{17,3},{18,0},{19,1},{20,6},{21,7},{22,4},{23,5},{24,8},{25... | collective-permute-start | bytes 196616 | tf_op jit(solution)/shard_map/ppermute | solution.py:325
  8.9 3.6 %collective-permute-start = (bf16[2,128,128]{2,1,0:T(8,128)(2,1)}, bf16[2,128,128]{2,1,0:T(8,128)(2,1)S(1)}, u32[]{:S(2)}, u32[]{:S(2)}) collective-permute-start(bf16[2,128,128]{2,1,0:T(8,128)(2,1)} %bitcast.33), channel_id=1, source_target_pairs={{0,2},{1,3},{2,0},{3,1},{4,6},{5,7},{6,4},{7,5},{8,8},{9,9},{10,12... | collective-permute-start | bytes 196616 | tf_op jit(solution)/shard_map/ppermute | solution.py:325
  12.5 0.0 collective-permute-done.4.refs_0_
  12.6 0.8 %join.1.refs_0_ = bf16[4,128,128]{2,1,0:T(8,128)(2,1)S(1)} custom-call(bf16[2,128,128]{2,1,0:T(8,128)(2,1)} %bitcast.29, bf16[2,128,128]{2,1,0:T(8,128)(2,1)S(1)} %collective-permute-done.4.refs_0_), custom_call_target="tpu_custom_call" | custom-call | tf_op jit(solution)/shard_map/join/pallas_call | solution.py:169
  13.4 0.5 %collective-permute-start.5 = (bf16[4,128,128]{2,1,0:T(8,128)(2,1)S(1)}, bf16[4,128,128]{2,1,0:T(8,128)(2,1)S(1)}, u32[]{:S(2)}, u32[]{:S(2)}) collective-permute-start(bf16[4,128,128]{2,1,0:T(8,128)(2,1)S(1)} %join.1.refs_0_), channel_id=1, source_target_pairs={{8,0},{0,8},{24,16},{16,24},{9,1},{1,9},{25,17},{17,25},{10,2},{2,... | collective-permute-start | bytes 393224 | tf_op jit(solution)/shard_map/ppermute | solution.py:305
  13.9 0.0 collective-permute-done.3
  13.9 0.0 collective-permute-start.9
  13.9 0.0 collective-permute-done.2
  13.9 0.5 %collective-permute-start.8 = (bf16[1,2,128,128]{3,2,1,0:T(8,128)(2,1)S(1)}, bf16[1,2,128,128]{3,2,1,0:T(8,128)(2,1)S(1)}, u32[]{:S(2)}, u32[]{:S(2)}) collective-permute-start(bf16[1,2,128,128]{3,2,1,0:T(8,128)(2,1)S(1)} %bitcast.18), channel_id=1, source_target_pairs={{0,1},{1,0},{2,3},{3,2},{4,5},{5,4},{6,7},{7,6},{8,9},{9,8},{10,11... | collective-permute-start | bytes 196616 | tf_op jit(solution)/shard_map/ppermute | solution.py:327
  14.4 0.0 collective-permute-done.1
  14.4 0.1 collective-permute-start.7
  14.5 0.9 %collective-permute-done = bf16[2,128,128]{2,1,0:T(8,128)(2,1)S(1)} collective-permute-done((bf16[2,128,128]{2,1,0:T(8,128)(2,1)}, bf16[2,128,128]{2,1,0:T(8,128)(2,1)S(1)}, u32[]{:S(2)}, u32[]{:S(2)}) %collective-permute-start) | collective-permute-done | bytes 65568 | tf_op jit(solution)/shard_map/ppermute | solution.py:325
  15.3 0.0 collective-permute-start.6
  15.3 1.0 %prepare.1 = (bf16[1,1024,256]{2,1,0:T(8,128)(2,1)S(1)}, bf16[2,1,128,128]{3,2,1,0:T(8,128)(2,1)S(1)}, f32[2,1,128,128]{3,2,1,0:T(8,128)S(1)}) custom-call(s32[8]{0:T(128)} %sizes_hbm.1, bf16[8,128,128]{2,1,0:T(8,128)(2,1)} %bitcast.26, bf16[8,128,128]{2,1,0:T(8,128)(2,1)} %bitcast.27, bf16[1,2,128,128]{3,2,1,0:T(8,128)(2,1)S(1)} %bitcast.23, ...), custom_call_target="tpu_custom_call" | custom-call | tf_op jit(solution)/shard_map/prepare/pallas_call | solution.py:352
  16.4 0.0 collective-permute-done.9.refs_5_
  16.4 0.0 collective-permute-done.7.refs_3_
  16.4 0.2 collective-permute-done.6.refs_2_
  16.6 1.9 %collective-permute-done.5.refs_1_ = bf16[4,128,128]{2,1,0:T(8,128)(2,1)S(1)} collective-permute-done((bf16[4,128,128]{2,1,0:T(8,128)(2,1)S(1)}, bf16[4,128,128]{2,1,0:T(8,128)(2,1)S(1)}, u32[]{:S(2)}, u32[]{:S(2)}) %collective-permute-start.5) | collective-permute-done | bytes 131104 | tf_op jit(solution)/shard_map/ppermute | solution.py:305
  18.4 2.4 %levels.1 = (f32[32,128]{1,0:T(8,128)S(1)}, f32[8,2,128,128]{3,2,1,0:T(8,128)S(1)}) custom-call(bf16[1,1024,256]{2,1,0:T(8,128)(2,1)S(1)} %get-tuple-element.9.own_cat, bf16[2,1,128,128]{3,2,1,0:T(8,128)(2,1)S(1)} %get-tuple-element.10.start_ref, f32[2,1,128,128]{3,2,1,0:T(8,128)S(1)} %get-tuple-element.11.inverse_ref, ...), custom_call_target="tpu_custom_call" | custom-call | tf_op jit(solution)/shard_map/levels/pallas_call | solution.py:370
  20.9 10.5 %all_to_all.11 = f32[32,1,128]{2,1,0:T(1,128)S(1)} all-to-all(f32[32,1,128]{2,1,0:T(1,128)S(1)} %bitcast.24), channel_id=1, replica_groups=mesh['term'=4,'sector'=8] {'term','sector'}, dimensions={0} | all-to-all | bytes 32768 | tf_op jit(solution)/shard_map/all_to_all | solution.py:386
  31.4 0.4 %finish.1 = (bf16[2,128,128]{2,1,0:T(8,128)(2,1)S(1)}, f32[1,128]{1,0:T(1,128)S(1)}) custom-call(f32[32,128]{1,0:T(8,128)S(1)} %bitcast.15, f32[8,2,128,128]{3,2,1,0:T(8,128)S(1)} %get-tuple-element.13.basis_ref), custom_call_target="tpu_custom_call" | custom-call | tf_op jit(solution)/shard_map/finish/pallas_call | solution.py:388
  31.8 0.7 %collective-permute-start.12 = (bf16[2,128,128]{2,1,0:T(8,128)(2,1)S(1)}, bf16[2,128,128]{2,1,0:T(8,128)(2,1)S(1)}, u32[]{:S(2)}, u32[]{:S(2)}) collective-permute-start(bf16[2,128,128]{2,1,0:T(8,128)(2,1)S(1)} %get-tuple-element.14.refs_0_), channel_id=1, source_target_pairs={{24,0},{16,8},{8,16},{0,24},{25,1},{17,9},{9,17},{1,25},{26,2},{18... | collective-permute-start | bytes 196616 | tf_op jit(solution)/shard_map/ppermute | solution.py:305
  32.5 1.4 %collective-permute-start.11 = (bf16[2,128,128]{2,1,0:T(8,128)(2,1)S(1)}, bf16[2,128,128]{2,1,0:T(8,128)(2,1)S(1)}, u32[]{:S(2)}, u32[]{:S(2)}) collective-permute-start(bf16[2,128,128]{2,1,0:T(8,128)(2,1)S(1)} %get-tuple-element.14.refs_0_), channel_id=1, source_target_pairs={{16,0},{24,8},{0,16},{8,24},{17,1},{25,9},{1,17},{9,25},{18,2},{26... | collective-permute-start | bytes 196616 | tf_op jit(solution)/shard_map/ppermute | solution.py:305
  34.0 1.4 %collective-permute-start.10 = (bf16[2,128,128]{2,1,0:T(8,128)(2,1)S(1)}, bf16[2,128,128]{2,1,0:T(8,128)(2,1)S(1)}, u32[]{:S(2)}, u32[]{:S(2)}) collective-permute-start(bf16[2,128,128]{2,1,0:T(8,128)(2,1)S(1)} %get-tuple-element.14.refs_0_), channel_id=1, source_target_pairs={{8,0},{0,8},{24,16},{16,24},{9,1},{1,9},{25,17},{17,25},{10,2},{2,... | collective-permute-start | bytes 196616 | tf_op jit(solution)/shard_map/ppermute | solution.py:305
  35.4 0.5 %slice_bitcast_fusion = f32[3]{0:T(128)} fusion(f32[1,128]{1,0:T(1,128)S(1)} %get-tuple-element.15), kind=kLoop, calls=%fused_computation | loop fusion | bytes 24 | tf_op jit(solution)/shard_map/squeeze | solution.py:408
  35.9 1.5 %collective-permute-done.12.refs_3_ = bf16[2,128,128]{2,1,0:T(8,128)(2,1)S(1)} collective-permute-done((bf16[2,128,128]{2,1,0:T(8,128)(2,1)S(1)}, bf16[2,128,128]{2,1,0:T(8,128)(2,1)S(1)}, u32[]{:S(2)}, u32[]{:S(2)}) %collective-permute-start.12) | collective-permute-done | bytes 65568 | tf_op jit(solution)/shard_map/ppermute | solution.py:305
  37.4 0.1 collective-permute-done.11.refs_2_
  37.5 0.7 %collective-permute-done.10.refs_1_ = bf16[2,128,128]{2,1,0:T(8,128)(2,1)S(1)} collective-permute-done((bf16[2,128,128]{2,1,0:T(8,128)(2,1)S(1)}, bf16[2,128,128]{2,1,0:T(8,128)(2,1)S(1)}, u32[]{:S(2)}, u32[]{:S(2)}) %collective-permute-start.10) | collective-permute-done | bytes 65568 | tf_op jit(solution)/shard_map/ppermute | solution.py:305
  38.2 0.7 %assemble.1 = bf16[8,128,128]{2,1,0:T(8,128)(2,1)} custom-call(bf16[2,128,128]{2,1,0:T(8,128)(2,1)S(1)} %get-tuple-element.14.refs_0_, bf16[2,128,128]{2,1,0:T(8,128)(2,1)S(1)} %collective-permute-done.10.refs_1_, bf16[2,128,128]{2,1,0:T(8,128)(2,1)S(1)} %collective-permute-done.11.refs_2_, bf16[2,128,128]{2,1,0:T(8,128)(2,1)S(1)} %collective-permute-done.12.refs_3_), custom_call_target="tpu_custom_call" | custom-call | tf_op jit(solution)/shard_map/assemble/pallas_call | solution.py:399
  (1 shorter events, 0.0 us)
Async XLA Ops:
  0.6 11.9 %collective-permute-start.4 = (bf16[2,128,128]{2,1,0:T(8,128)(2,1)}, bf16[2,128,128]{2,1,0:T(8,128)(2,1)S(1)}, u32[]{:S(2)}, u32[]{:S(2)}) collective-permute-start(bf16[2,128,128]{2,1,0:T(8,128)(2,1)} %bitcast.28), channel_id=1, source_target_pairs={{16,0},{24,8},{0,16},{8,24},{17,1},{25,9},{1,17},{9,25},{18,2},{26... | collective-permute-start | bytes 196616 | tf_op jit(solution)/shard_map/ppermute | solution.py:305
  3.7 10.2 %collective-permute-start.3 = (bf16[2,128,128]{2,1,0:T(8,128)(2,1)}, bf16[2,128,128]{2,1,0:T(8,128)(2,1)S(1)}, u32[]{:S(2)}, u32[]{:S(2)}) collective-permute-start(bf16[2,128,128]{2,1,0:T(8,128)(2,1)} %bitcast.30), channel_id=1, source_target_pairs={{8,2},{9,3},{10,0},{11,1},{12,6},{13,7},{14,4},{15,5},{0,8},{1,9},... | collective-permute-start | bytes 196616 | tf_op jit(solution)/shard_map/ppermute | solution.py:325
  5.2 8.7 %collective-permute-start.2 = (bf16[2,128,128]{2,1,0:T(8,128)(2,1)}, bf16[2,128,128]{2,1,0:T(8,128)(2,1)S(1)}, u32[]{:S(2)}, u32[]{:S(2)}) collective-permute-start(bf16[2,128,128]{2,1,0:T(8,128)(2,1)} %bitcast.31), channel_id=1, source_target_pairs={{24,2},{25,3},{26,0},{27,1},{28,6},{29,7},{30,4},{31,5},{16,8},{17... | collective-permute-start | bytes 196616 | tf_op jit(solution)/shard_map/ppermute | solution.py:325
  8.4 5.9 %collective-permute-start.1 = (bf16[2,128,128]{2,1,0:T(8,128)(2,1)}, bf16[2,128,128]{2,1,0:T(8,128)(2,1)S(1)}, u32[]{:S(2)}, u32[]{:S(2)}) collective-permute-start(bf16[2,128,128]{2,1,0:T(8,128)(2,1)} %bitcast.32), channel_id=1, source_target_pairs={{16,2},{17,3},{18,0},{19,1},{20,6},{21,7},{22,4},{23,5},{24,8},{25... | collective-permute-start | bytes 196616 | tf_op jit(solution)/shard_map/ppermute | solution.py:325
  8.9 6.4 %collective-permute-start = (bf16[2,128,128]{2,1,0:T(8,128)(2,1)}, bf16[2,128,128]{2,1,0:T(8,128)(2,1)S(1)}, u32[]{:S(2)}, u32[]{:S(2)}) collective-permute-start(bf16[2,128,128]{2,1,0:T(8,128)(2,1)} %bitcast.33), channel_id=1, source_target_pairs={{0,2},{1,3},{2,0},{3,1},{4,6},{5,7},{6,4},{7,5},{8,8},{9,9},{10,12... | collective-permute-start | bytes 196616 | tf_op jit(solution)/shard_map/ppermute | solution.py:325
  13.4 5.0 %collective-permute-start.5 = (bf16[4,128,128]{2,1,0:T(8,128)(2,1)S(1)}, bf16[4,128,128]{2,1,0:T(8,128)(2,1)S(1)}, u32[]{:S(2)}, u32[]{:S(2)}) collective-permute-start(bf16[4,128,128]{2,1,0:T(8,128)(2,1)S(1)} %join.1.refs_0_), channel_id=1, source_target_pairs={{8,0},{0,8},{24,16},{16,24},{9,1},{1,9},{25,17},{17,25},{10,2},{2,... | collective-permute-start | bytes 393224 | tf_op jit(solution)/shard_map/ppermute | solution.py:305
  13.9 2.5 %collective-permute-start.9 = (bf16[1,2,128,128]{3,2,1,0:T(8,128)(2,1)S(1)}, bf16[1,2,128,128]{3,2,1,0:T(8,128)(2,1)S(1)}, u32[]{:S(2)}, u32[]{:S(2)}) collective-permute-start(bf16[1,2,128,128]{3,2,1,0:T(8,128)(2,1)S(1)} %bitcast.16), channel_id=1, source_target_pairs={{0,1},{1,0},{2,3},{3,2},{4,5},{5,4},{6,7},{7,6},{8,9},{9,8},{10,11... | collective-permute-start | bytes 196616 | tf_op jit(solution)/shard_map/ppermute | solution.py:327
  13.9 2.5 %collective-permute-start.8 = (bf16[1,2,128,128]{3,2,1,0:T(8,128)(2,1)S(1)}, bf16[1,2,128,128]{3,2,1,0:T(8,128)(2,1)S(1)}, u32[]{:S(2)}, u32[]{:S(2)}) collective-permute-start(bf16[1,2,128,128]{3,2,1,0:T(8,128)(2,1)S(1)} %bitcast.18), channel_id=1, source_target_pairs={{0,1},{1,0},{2,3},{3,2},{4,5},{5,4},{6,7},{7,6},{8,9},{9,8},{10,11... | collective-permute-start | bytes 196616 | tf_op jit(solution)/shard_map/ppermute | solution.py:327
  14.4 2.0 %collective-permute-start.7 = (bf16[1,2,128,128]{3,2,1,0:T(8,128)(2,1)S(1)}, bf16[1,2,128,128]{3,2,1,0:T(8,128)(2,1)S(1)}, u32[]{:S(2)}, u32[]{:S(2)}) collective-permute-start(bf16[1,2,128,128]{3,2,1,0:T(8,128)(2,1)S(1)} %bitcast.20), channel_id=1, source_target_pairs={{0,1},{1,0},{2,3},{3,2},{4,5},{5,4},{6,7},{7,6},{8,9},{9,8},{10,11... | collective-permute-start | bytes 196616 | tf_op jit(solution)/shard_map/ppermute | solution.py:327
  15.3 1.3 %collective-permute-start.6 = (bf16[1,2,128,128]{3,2,1,0:T(8,128)(2,1)S(1)}, bf16[1,2,128,128]{3,2,1,0:T(8,128)(2,1)S(1)}, u32[]{:S(2)}, u32[]{:S(2)}) collective-permute-start(bf16[1,2,128,128]{3,2,1,0:T(8,128)(2,1)S(1)} %bitcast.22), channel_id=1, source_target_pairs={{0,1},{1,0},{2,3},{3,2},{4,5},{5,4},{6,7},{7,6},{8,9},{9,8},{10,11... | collective-permute-start | bytes 196616 | tf_op jit(solution)/shard_map/ppermute | solution.py:327
  31.8 5.6 %collective-permute-start.12 = (bf16[2,128,128]{2,1,0:T(8,128)(2,1)S(1)}, bf16[2,128,128]{2,1,0:T(8,128)(2,1)S(1)}, u32[]{:S(2)}, u32[]{:S(2)}) collective-permute-start(bf16[2,128,128]{2,1,0:T(8,128)(2,1)S(1)} %get-tuple-element.14.refs_0_), channel_id=1, source_target_pairs={{24,0},{16,8},{8,16},{0,24},{25,1},{17,9},{9,17},{1,25},{26,2},{18... | collective-permute-start | bytes 196616 | tf_op jit(solution)/shard_map/ppermute | solution.py:305
  32.5 5.0 %collective-permute-start.11 = (bf16[2,128,128]{2,1,0:T(8,128)(2,1)S(1)}, bf16[2,128,128]{2,1,0:T(8,128)(2,1)S(1)}, u32[]{:S(2)}, u32[]{:S(2)}) collective-permute-start(bf16[2,128,128]{2,1,0:T(8,128)(2,1)S(1)} %get-tuple-element.14.refs_0_), channel_id=1, source_target_pairs={{16,0},{24,8},{0,16},{8,24},{17,1},{25,9},{1,17},{9,25},{18,2},{26... | collective-permute-start | bytes 196616 | tf_op jit(solution)/shard_map/ppermute | solution.py:305
  34.0 4.3 %collective-permute-start.10 = (bf16[2,128,128]{2,1,0:T(8,128)(2,1)S(1)}, bf16[2,128,128]{2,1,0:T(8,128)(2,1)S(1)}, u32[]{:S(2)}, u32[]{:S(2)}) collective-permute-start(bf16[2,128,128]{2,1,0:T(8,128)(2,1)S(1)} %get-tuple-element.14.refs_0_), channel_id=1, source_target_pairs={{8,0},{0,8},{24,16},{16,24},{9,1},{1,9},{25,17},{17,25},{10,2},{2,... | collective-permute-start | bytes 196616 | tf_op jit(solution)/shard_map/ppermute | solution.py:305

commit v7 on v6

--- a/solution.py
+++ b/solution.py
@@ -253,9 +253,9 @@
     share = pieces[0].shape[0]
     term, chip = lax.axis_index("term"), lax.axis_index("sector") // 2
     copies = []
-    for m in range(plan.owners):
+    for at, m in enumerate(plan.last):
         first = plan.first_chip(plan.hop(term, m), chip) * 2
-        copies.append(pltpu.make_async_copy(pieces[m], out_ref.at[pl.ds(first, share)], sems.at[m]))
+        copies.append(pltpu.make_async_copy(pieces[at], out_ref.at[pl.ds(first, share)], sems.at[at]))
         copies[-1].start()
     for copy in copies:
         copy.wait()
@@ -268,6 +268,7 @@
         self.direct = self.groups == 1 and owners > 1 and owners & (owners - 1) == 0
         self.bits = [1 << b for b in reversed(range(owners.bit_length() - 1))]
         self.order = (0, 2, 3, 1) if self.direct and owners == 4 else tuple(range(owners))
+        self.last = (0, 2, 1, 3) if owners == 4 else tuple(range(owners))
         offsets = [0]
         for bit in self.bits if self.direct else []:
             offsets = offsets + [offset ^ bit for offset in offsets]
@@ -404,7 +405,7 @@
         scratch_shapes=[pltpu.SemaphoreType.DMA((owners,))],
         compiler_params=pltpu.CompilerParams(vmem_limit_bytes=16 << 20),
         name="assemble",
-    )(*[from_owner(plan, blocks, m) for m in range(owners)])
+    )(*[from_owner(plan, blocks, m) for m in plan.last])
     return (state[None], energy[0, :3])
 
 

time: 39.2 us -> 39.2 us (level)
  transfers between devices with their start and end apart: 13 -> 13, of which waited for: 6 -> 5; matrix products, arithmetic and copies ran while one was open for 1% -> 1% of each run, Pallas kernels for 5% -> 5%
where the time goes in v7:
time: 39.2 us; the launch traced here: 39 us
  starting transfers between devices  16.5 us (42%)
  blocking collectives  10.5 us (27%)
  Pallas kernels  5.43 us (14%)
  waiting for transfers between devices  5.27 us (13%)
  between operations  0.71 us (2%)
  local copies, waits for them, and re-layouts  0.51 us (1%)
    all_to_all x1, blocking collectives, local(): gram = lax.all_to_all(gram, ('term', 'sector'), 0, 0, tiled=True)  10.5 us
    ppermute x4, starting transfers between devices, inputs(): own[m] = lax.ppermute(right, ('term', 'sector'), moves)[None]  8.87 us
    ppermute x5, starting transfers between devices, from_owner(): return lax.ppermute(value, 'term', moves)  7.04 us
    ppermute x5, waiting for transfers between devices, from_owner(): return lax.ppermute(value, 'term', moves)  4.18 us
    pallas_call x1, Pallas kernels, local(): pl.pallas_call(functools.partial(levels_kernel, plan, pieces), out_shape=...  2.45 us
    pallas_call x1, Pallas kernels, local(): pl.pallas_call(functools.partial(prepare_kernel, plan), out_shape=(jax.Sh...  1.01 us
    ppermute x4, waiting for transfers between devices, inputs(): own[m] = lax.ppermute(right, ('term', 'sector'), moves)[None]  0.89 us
    pallas_call x1, Pallas kernels, join(): pl.pallas_call(join_kernel, out_shape=jax.ShapeDtypeStruct((rows,) + own....  0.85 us
  transfers between devices with their start and end apart: 13, of which 5 were waited for; matrix products, arithmetic and copies ran while one was open for 1% of the time, Pallas kernels for 5%

profile of v7, /device:TPU:0, one launch (start us, length us, event | category | flops | bytes accessed | tf_op | source)
XLA Modules:
  0.0 39.0 jit_solution(17887045739257281374)
XLA Ops:
  0.6 3.0 %collective-permute-start.4 = (bf16[2,128,128]{2,1,0:T(8,128)(2,1)}, bf16[2,128,128]{2,1,0:T(8,128)(2,1)S(1)}, u32[]{:S(2)}, u32[]{:S(2)}) collective-permute-start(bf16[2,128,128]{2,1,0:T(8,128)(2,1)} %bitcast.28), channel_id=1, source_target_pairs={{16,0},{24,8},{0,16},{8,24},{17,1},{25,9},{1,17},{9,25},{18,2},{26... | collective-permute-start | bytes 196616 | tf_op jit(solution)/shard_map/ppermute | solution.py:306
  3.7 1.5 %collective-permute-start.3 = (bf16[2,128,128]{2,1,0:T(8,128)(2,1)}, bf16[2,128,128]{2,1,0:T(8,128)(2,1)S(1)}, u32[]{:S(2)}, u32[]{:S(2)}) collective-permute-start(bf16[2,128,128]{2,1,0:T(8,128)(2,1)} %bitcast.30), channel_id=1, source_target_pairs={{8,2},{9,3},{10,0},{11,1},{12,6},{13,7},{14,4},{15,5},{0,8},{1,9},... | collective-permute-start | bytes 196616 | tf_op jit(solution)/shard_map/ppermute | solution.py:326
  5.2 3.3 %collective-permute-start.2 = (bf16[2,128,128]{2,1,0:T(8,128)(2,1)}, bf16[2,128,128]{2,1,0:T(8,128)(2,1)S(1)}, u32[]{:S(2)}, u32[]{:S(2)}) collective-permute-start(bf16[2,128,128]{2,1,0:T(8,128)(2,1)} %bitcast.31), channel_id=1, source_target_pairs={{24,2},{25,3},{26,0},{27,1},{28,6},{29,7},{30,4},{31,5},{16,8},{17... | collective-permute-start | bytes 196616 | tf_op jit(solution)/shard_map/ppermute | solution.py:326
  8.4 0.5 %collective-permute-start.1 = (bf16[2,128,128]{2,1,0:T(8,128)(2,1)}, bf16[2,128,128]{2,1,0:T(8,128)(2,1)S(1)}, u32[]{:S(2)}, u32[]{:S(2)}) collective-permute-start(bf16[2,128,128]{2,1,0:T(8,128)(2,1)} %bitcast.32), channel_id=1, source_target_pairs={{16,2},{17,3},{18,0},{19,1},{20,6},{21,7},{22,4},{23,5},{24,8},{25... | collective-permute-start | bytes 196616 | tf_op jit(solution)/shard_map/ppermute | solution.py:326
  8.9 3.6 %collective-permute-start = (bf16[2,128,128]{2,1,0:T(8,128)(2,1)}, bf16[2,128,128]{2,1,0:T(8,128)(2,1)S(1)}, u32[]{:S(2)}, u32[]{:S(2)}) collective-permute-start(bf16[2,128,128]{2,1,0:T(8,128)(2,1)} %bitcast.33), channel_id=1, source_target_pairs={{0,2},{1,3},{2,0},{3,1},{4,6},{5,7},{6,4},{7,5},{8,8},{9,9},{10,12... | collective-permute-start | bytes 196616 | tf_op jit(solution)/shard_map/ppermute | solution.py:326
  12.5 0.0 collective-permute-done.4.refs_0_
  12.6 0.8 %join.1.refs_0_ = bf16[4,128,128]{2,1,0:T(8,128)(2,1)S(1)} custom-call(bf16[2,128,128]{2,1,0:T(8,128)(2,1)} %bitcast.29, bf16[2,128,128]{2,1,0:T(8,128)(2,1)S(1)} %collective-permute-done.4.refs_0_), custom_call_target="tpu_custom_call" | custom-call | tf_op jit(solution)/shard_map/join/pallas_call | solution.py:169
  13.4 0.5 %collective-permute-start.5 = (bf16[4,128,128]{2,1,0:T(8,128)(2,1)S(1)}, bf16[4,128,128]{2,1,0:T(8,128)(2,1)S(1)}, u32[]{:S(2)}, u32[]{:S(2)}) collective-permute-start(bf16[4,128,128]{2,1,0:T(8,128)(2,1)S(1)} %join.1.refs_0_), channel_id=1, source_target_pairs={{8,0},{0,8},{24,16},{16,24},{9,1},{1,9},{25,17},{17,25},{10,2},{2,... | collective-permute-start | bytes 393224 | tf_op jit(solution)/shard_map/ppermute | solution.py:306
  13.9 0.0 collective-permute-done.3
  13.9 0.0 collective-permute-start.9
  13.9 0.0 collective-permute-done.2
  13.9 0.5 %collective-permute-start.8 = (bf16[1,2,128,128]{3,2,1,0:T(8,128)(2,1)S(1)}, bf16[1,2,128,128]{3,2,1,0:T(8,128)(2,1)S(1)}, u32[]{:S(2)}, u32[]{:S(2)}) collective-permute-start(bf16[1,2,128,128]{3,2,1,0:T(8,128)(2,1)S(1)} %bitcast.18), channel_id=1, source_target_pairs={{0,1},{1,0},{2,3},{3,2},{4,5},{5,4},{6,7},{7,6},{8,9},{9,8},{10,11... | collective-permute-start | bytes 196616 | tf_op jit(solution)/shard_map/ppermute | solution.py:328
  14.4 0.0 collective-permute-done.1
  14.4 0.1 collective-permute-start.7
  14.5 0.9 %collective-permute-done = bf16[2,128,128]{2,1,0:T(8,128)(2,1)S(1)} collective-permute-done((bf16[2,128,128]{2,1,0:T(8,128)(2,1)}, bf16[2,128,128]{2,1,0:T(8,128)(2,1)S(1)}, u32[]{:S(2)}, u32[]{:S(2)}) %collective-permute-start) | collective-permute-done | bytes 65568 | tf_op jit(solution)/shard_map/ppermute | solution.py:326
  15.3 0.0 collective-permute-start.6
  15.3 1.0 %prepare.1 = (bf16[1,1024,256]{2,1,0:T(8,128)(2,1)S(1)}, bf16[2,1,128,128]{3,2,1,0:T(8,128)(2,1)S(1)}, f32[2,1,128,128]{3,2,1,0:T(8,128)S(1)}) custom-call(s32[8]{0:T(128)} %sizes_hbm.1, bf16[8,128,128]{2,1,0:T(8,128)(2,1)} %bitcast.26, bf16[8,128,128]{2,1,0:T(8,128)(2,1)} %bitcast.27, bf16[1,2,128,128]{3,2,1,0:T(8,128)(2,1)S(1)} %bitcast.23, ...), custom_call_target="tpu_custom_call" | custom-call | tf_op jit(solution)/shard_map/prepare/pallas_call | solution.py:353
  16.4 0.0 collective-permute-done.9.refs_5_
  16.4 0.0 collective-permute-done.8.refs_4_
  16.4 0.0 collective-permute-done.7.refs_3_
  16.4 0.2 collective-permute-done.6.refs_2_
  16.6 1.9 %collective-permute-done.5.refs_1_ = bf16[4,128,128]{2,1,0:T(8,128)(2,1)S(1)} collective-permute-done((bf16[4,128,128]{2,1,0:T(8,128)(2,1)S(1)}, bf16[4,128,128]{2,1,0:T(8,128)(2,1)S(1)}, u32[]{:S(2)}, u32[]{:S(2)}) %collective-permute-start.5) | collective-permute-done | bytes 131104 | tf_op jit(solution)/shard_map/ppermute | solution.py:306
  18.4 2.4 %levels.1 = (f32[32,128]{1,0:T(8,128)S(1)}, f32[8,2,128,128]{3,2,1,0:T(8,128)S(1)}) custom-call(bf16[1,1024,256]{2,1,0:T(8,128)(2,1)S(1)} %get-tuple-element.9.own_cat, bf16[2,1,128,128]{3,2,1,0:T(8,128)(2,1)S(1)} %get-tuple-element.10.start_ref, f32[2,1,128,128]{3,2,1,0:T(8,128)S(1)} %get-tuple-element.11.inverse_ref, ...), custom_call_target="tpu_custom_call" | custom-call | tf_op jit(solution)/shard_map/levels/pallas_call | solution.py:371
  20.9 10.5 %all_to_all.11 = f32[32,1,128]{2,1,0:T(1,128)S(1)} all-to-all(f32[32,1,128]{2,1,0:T(1,128)S(1)} %bitcast.24), channel_id=1, replica_groups=mesh['term'=4,'sector'=8] {'term','sector'}, dimensions={0} | all-to-all | bytes 32768 | tf_op jit(solution)/shard_map/all_to_all | solution.py:387
  31.4 0.4 %finish.1 = (bf16[2,128,128]{2,1,0:T(8,128)(2,1)S(1)}, f32[1,128]{1,0:T(1,128)S(1)}) custom-call(f32[32,128]{1,0:T(8,128)S(1)} %bitcast.15, f32[8,2,128,128]{3,2,1,0:T(8,128)S(1)} %get-tuple-element.13.basis_ref), custom_call_target="tpu_custom_call" | custom-call | tf_op jit(solution)/shard_map/finish/pallas_call | solution.py:389
  31.8 0.7 %collective-permute-start.12 = (bf16[2,128,128]{2,1,0:T(8,128)(2,1)S(1)}, bf16[2,128,128]{2,1,0:T(8,128)(2,1)S(1)}, u32[]{:S(2)}, u32[]{:S(2)}) collective-permute-start(bf16[2,128,128]{2,1,0:T(8,128)(2,1)S(1)} %get-tuple-element.14.refs_0_), channel_id=1, source_target_pairs={{24,0},{16,8},{8,16},{0,24},{25,1},{17,9},{9,17},{1,25},{26,2},{18... | collective-permute-start | bytes 196616 | tf_op jit(solution)/shard_map/ppermute | solution.py:306
  32.5 1.4 %collective-permute-start.11 = (bf16[2,128,128]{2,1,0:T(8,128)(2,1)S(1)}, bf16[2,128,128]{2,1,0:T(8,128)(2,1)S(1)}, u32[]{:S(2)}, u32[]{:S(2)}) collective-permute-start(bf16[2,128,128]{2,1,0:T(8,128)(2,1)S(1)} %get-tuple-element.14.refs_0_), channel_id=1, source_target_pairs={{8,0},{0,8},{24,16},{16,24},{9,1},{1,9},{25,17},{17,25},{10,2},{2,... | collective-permute-start | bytes 196616 | tf_op jit(solution)/shard_map/ppermute | solution.py:306
  34.0 1.4 %collective-permute-start.10 = (bf16[2,128,128]{2,1,0:T(8,128)(2,1)S(1)}, bf16[2,128,128]{2,1,0:T(8,128)(2,1)S(1)}, u32[]{:S(2)}, u32[]{:S(2)}) collective-permute-start(bf16[2,128,128]{2,1,0:T(8,128)(2,1)S(1)} %get-tuple-element.14.refs_0_), channel_id=1, source_target_pairs={{16,0},{24,8},{0,16},{8,24},{17,1},{25,9},{1,17},{9,25},{18,2},{26... | collective-permute-start | bytes 196616 | tf_op jit(solution)/shard_map/ppermute | solution.py:306
  35.4 0.5 %slice_bitcast_fusion = f32[3]{0:T(128)} fusion(f32[1,128]{1,0:T(1,128)S(1)} %get-tuple-element.15), kind=kLoop, calls=%fused_computation | loop fusion | bytes 24 | tf_op jit(solution)/shard_map/squeeze | solution.py:409
  35.9 1.5 %collective-permute-done.12.refs_3_ = bf16[2,128,128]{2,1,0:T(8,128)(2,1)S(1)} collective-permute-done((bf16[2,128,128]{2,1,0:T(8,128)(2,1)S(1)}, bf16[2,128,128]{2,1,0:T(8,128)(2,1)S(1)}, u32[]{:S(2)}, u32[]{:S(2)}) %collective-permute-start.12) | collective-permute-done | bytes 65568 | tf_op jit(solution)/shard_map/ppermute | solution.py:306
  37.4 0.8 %collective-permute-done.10.refs_1_ = bf16[2,128,128]{2,1,0:T(8,128)(2,1)S(1)} collective-permute-done((bf16[2,128,128]{2,1,0:T(8,128)(2,1)S(1)}, bf16[2,128,128]{2,1,0:T(8,128)(2,1)S(1)}, u32[]{:S(2)}, u32[]{:S(2)}) %collective-permute-start.10) | collective-permute-done | bytes 65568 | tf_op jit(solution)/shard_map/ppermute | solution.py:306
  38.2 0.7 %assemble.1 = bf16[8,128,128]{2,1,0:T(8,128)(2,1)} custom-call(bf16[2,128,128]{2,1,0:T(8,128)(2,1)S(1)} %get-tuple-element.14.refs_0_, bf16[2,128,128]{2,1,0:T(8,128)(2,1)S(1)} %collective-permute-done.10.refs_1_, bf16[2,128,128]{2,1,0:T(8,128)(2,1)S(1)} %collective-permute-done.11.refs_2_, bf16[2,128,128]{2,1,0:T(8,128)(2,1)S(1)} %collective-permute-done.12.refs_3_), custom_call_target="tpu_custom_call" | custom-call | tf_op jit(solution)/shard_map/assemble/pallas_call | solution.py:400
  (1 shorter events, 0.0 us)
Async XLA Ops:
  0.6 11.9 %collective-permute-start.4 = (bf16[2,128,128]{2,1,0:T(8,128)(2,1)}, bf16[2,128,128]{2,1,0:T(8,128)(2,1)S(1)}, u32[]{:S(2)}, u32[]{:S(2)}) collective-permute-start(bf16[2,128,128]{2,1,0:T(8,128)(2,1)} %bitcast.28), channel_id=1, source_target_pairs={{16,0},{24,8},{0,16},{8,24},{17,1},{25,9},{1,17},{9,25},{18,2},{26... | collective-permute-start | bytes 196616 | tf_op jit(solution)/shard_map/ppermute | solution.py:306
  3.7 10.2 %collective-permute-start.3 = (bf16[2,128,128]{2,1,0:T(8,128)(2,1)}, bf16[2,128,128]{2,1,0:T(8,128)(2,1)S(1)}, u32[]{:S(2)}, u32[]{:S(2)}) collective-permute-start(bf16[2,128,128]{2,1,0:T(8,128)(2,1)} %bitcast.30), channel_id=1, source_target_pairs={{8,2},{9,3},{10,0},{11,1},{12,6},{13,7},{14,4},{15,5},{0,8},{1,9},... | collective-permute-start | bytes 196616 | tf_op jit(solution)/shard_map/ppermute | solution.py:326
  5.2 8.7 %collective-permute-start.2 = (bf16[2,128,128]{2,1,0:T(8,128)(2,1)}, bf16[2,128,128]{2,1,0:T(8,128)(2,1)S(1)}, u32[]{:S(2)}, u32[]{:S(2)}) collective-permute-start(bf16[2,128,128]{2,1,0:T(8,128)(2,1)} %bitcast.31), channel_id=1, source_target_pairs={{24,2},{25,3},{26,0},{27,1},{28,6},{29,7},{30,4},{31,5},{16,8},{17... | collective-permute-start | bytes 196616 | tf_op jit(solution)/shard_map/ppermute | solution.py:326
  8.4 5.9 %collective-permute-start.1 = (bf16[2,128,128]{2,1,0:T(8,128)(2,1)}, bf16[2,128,128]{2,1,0:T(8,128)(2,1)S(1)}, u32[]{:S(2)}, u32[]{:S(2)}) collective-permute-start(bf16[2,128,128]{2,1,0:T(8,128)(2,1)} %bitcast.32), channel_id=1, source_target_pairs={{16,2},{17,3},{18,0},{19,1},{20,6},{21,7},{22,4},{23,5},{24,8},{25... | collective-permute-start | bytes 196616 | tf_op jit(solution)/shard_map/ppermute | solution.py:326
  8.9 6.4 %collective-permute-start = (bf16[2,128,128]{2,1,0:T(8,128)(2,1)}, bf16[2,128,128]{2,1,0:T(8,128)(2,1)S(1)}, u32[]{:S(2)}, u32[]{:S(2)}) collective-permute-start(bf16[2,128,128]{2,1,0:T(8,128)(2,1)} %bitcast.33), channel_id=1, source_target_pairs={{0,2},{1,3},{2,0},{3,1},{4,6},{5,7},{6,4},{7,5},{8,8},{9,9},{10,12... | collective-permute-start | bytes 196616 | tf_op jit(solution)/shard_map/ppermute | solution.py:326
  13.4 5.0 %collective-permute-start.5 = (bf16[4,128,128]{2,1,0:T(8,128)(2,1)S(1)}, bf16[4,128,128]{2,1,0:T(8,128)(2,1)S(1)}, u32[]{:S(2)}, u32[]{:S(2)}) collective-permute-start(bf16[4,128,128]{2,1,0:T(8,128)(2,1)S(1)} %join.1.refs_0_), channel_id=1, source_target_pairs={{8,0},{0,8},{24,16},{16,24},{9,1},{1,9},{25,17},{17,25},{10,2},{2,... | collective-permute-start | bytes 393224 | tf_op jit(solution)/shard_map/ppermute | solution.py:306
  13.9 2.5 %collective-permute-start.9 = (bf16[1,2,128,128]{3,2,1,0:T(8,128)(2,1)S(1)}, bf16[1,2,128,128]{3,2,1,0:T(8,128)(2,1)S(1)}, u32[]{:S(2)}, u32[]{:S(2)}) collective-permute-start(bf16[1,2,128,128]{3,2,1,0:T(8,128)(2,1)S(1)} %bitcast.16), channel_id=1, source_target_pairs={{0,1},{1,0},{2,3},{3,2},{4,5},{5,4},{6,7},{7,6},{8,9},{9,8},{10,11... | collective-permute-start | bytes 196616 | tf_op jit(solution)/shard_map/ppermute | solution.py:328
  13.9 2.5 %collective-permute-start.8 = (bf16[1,2,128,128]{3,2,1,0:T(8,128)(2,1)S(1)}, bf16[1,2,128,128]{3,2,1,0:T(8,128)(2,1)S(1)}, u32[]{:S(2)}, u32[]{:S(2)}) collective-permute-start(bf16[1,2,128,128]{3,2,1,0:T(8,128)(2,1)S(1)} %bitcast.18), channel_id=1, source_target_pairs={{0,1},{1,0},{2,3},{3,2},{4,5},{5,4},{6,7},{7,6},{8,9},{9,8},{10,11... | collective-permute-start | bytes 196616 | tf_op jit(solution)/shard_map/ppermute | solution.py:328
  14.4 2.0 %collective-permute-start.7 = (bf16[1,2,128,128]{3,2,1,0:T(8,128)(2,1)S(1)}, bf16[1,2,128,128]{3,2,1,0:T(8,128)(2,1)S(1)}, u32[]{:S(2)}, u32[]{:S(2)}) collective-permute-start(bf16[1,2,128,128]{3,2,1,0:T(8,128)(2,1)S(1)} %bitcast.20), channel_id=1, source_target_pairs={{0,1},{1,0},{2,3},{3,2},{4,5},{5,4},{6,7},{7,6},{8,9},{9,8},{10,11... | collective-permute-start | bytes 196616 | tf_op jit(solution)/shard_map/ppermute | solution.py:328
  15.3 1.3 %collective-permute-start.6 = (bf16[1,2,128,128]{3,2,1,0:T(8,128)(2,1)S(1)}, bf16[1,2,128,128]{3,2,1,0:T(8,128)(2,1)S(1)}, u32[]{:S(2)}, u32[]{:S(2)}) collective-permute-start(bf16[1,2,128,128]{3,2,1,0:T(8,128)(2,1)S(1)} %bitcast.22), channel_id=1, source_target_pairs={{0,1},{1,0},{2,3},{3,2},{4,5},{5,4},{6,7},{7,6},{8,9},{9,8},{10,11... | collective-permute-start | bytes 196616 | tf_op jit(solution)/shard_map/ppermute | solution.py:328
  31.8 5.5 %collective-permute-start.12 = (bf16[2,128,128]{2,1,0:T(8,128)(2,1)S(1)}, bf16[2,128,128]{2,1,0:T(8,128)(2,1)S(1)}, u32[]{:S(2)}, u32[]{:S(2)}) collective-permute-start(bf16[2,128,128]{2,1,0:T(8,128)(2,1)S(1)} %get-tuple-element.14.refs_0_), channel_id=1, source_target_pairs={{24,0},{16,8},{8,16},{0,24},{25,1},{17,9},{9,17},{1,25},{26,2},{18... | collective-permute-start | bytes 196616 | tf_op jit(solution)/shard_map/ppermute | solution.py:306
  32.5 4.9 %collective-permute-start.11 = (bf16[2,128,128]{2,1,0:T(8,128)(2,1)S(1)}, bf16[2,128,128]{2,1,0:T(8,128)(2,1)S(1)}, u32[]{:S(2)}, u32[]{:S(2)}) collective-permute-start(bf16[2,128,128]{2,1,0:T(8,128)(2,1)S(1)} %get-tuple-element.14.refs_0_), channel_id=1, source_target_pairs={{8,0},{0,8},{24,16},{16,24},{9,1},{1,9},{25,17},{17,25},{10,2},{2,... | collective-permute-start | bytes 196616 | tf_op jit(solution)/shard_map/ppermute | solution.py:306
  34.0 4.3 %collective-permute-start.10 = (bf16[2,128,128]{2,1,0:T(8,128)(2,1)S(1)}, bf16[2,128,128]{2,1,0:T(8,128)(2,1)S(1)}, u32[]{:S(2)}, u32[]{:S(2)}) collective-permute-start(bf16[2,128,128]{2,1,0:T(8,128)(2,1)S(1)} %get-tuple-element.14.refs_0_), channel_id=1, source_target_pairs={{16,0},{24,8},{0,16},{8,24},{17,1},{25,9},{1,17},{9,25},{18,2},{26... | collective-permute-start | bytes 196616 | tf_op jit(solution)/shard_map/ppermute | solution.py:306

commit v8 on v5

--- a/solution.py
+++ b/solution.py
@@ -121,9 +121,9 @@
         pl.loop(0, groups)(body)
 
 
-def prepare_kernel(plan, sizes_hbm, psi_hbm, pre_hbm, *refs):
-    own_refs, refs = refs[: plan.owners], refs[plan.owners :]
-    own_cat, start_ref, inverse_ref, sizes_ref, psi_ref, pre_ref, sems = refs
+def stage_kernel(plan, sizes_hbm, psi_hbm, pre_hbm, left_hbm, *refs):
+    held_refs, refs = refs[:-8], refs[-8:]
+    left_ref, start_ref, inverse_ref, sizes_ref, psi_ref, pre_ref, own_ref, sems = refs
     width = psi_ref.shape[-1]
     row = lax.axis_index("sector")
     core = row % 2
@@ -133,12 +133,17 @@
         pltpu.make_async_copy(sizes_hbm, sizes_ref, sems.at[0]),
         pltpu.make_async_copy(psi_hbm.at[blocks], psi_ref, sems.at[1]),
         pltpu.make_async_copy(pre_hbm.at[blocks], pre_ref, sems.at[2]),
+        pltpu.make_async_copy(left_hbm, own_ref, sems.at[3]),
     ]
     for copy in copies:
         copy.start()
-    each_group(plan.groups, lambda g: stack_right(plan, own_cat.at[g], own_refs, g, psi_ref.shape[-1]))
+    base = own_ref.shape[0]
+    for ref in held_refs:
+        left_ref[base : base + ref.shape[0]] = ref[...]
+        base += ref.shape[0]
     for copy in copies:
         copy.wait()
+    left_ref[: own_ref.shape[0]] = own_ref[...]
     row_ids = lax.broadcasted_iota(jnp.int32, (width, width), 0)
     col_ids = lax.broadcasted_iota(jnp.int32, (width, width), 1)
 
@@ -150,6 +155,11 @@
             inverse_ref[b, g] = jnp.where(valid, 1.0 / pre_ref[block].astype(jnp.float32), 0.0)
 
     each_group(plan.groups, body)
+
+
+def stack_kernel(plan, *refs):
+    own_refs, own_cat = refs[: plan.owners], refs[plan.owners]
+    each_group(plan.groups, lambda g: stack_right(plan, own_cat.at[g], own_refs, g, own_refs[0].shape[-1]))
 
 
 def levels_kernel(plan, pieces, own_cat, start_ref, inverse_ref, *refs):
@@ -242,13 +252,13 @@
         self.groups = self.chips // owners
         self.direct = self.groups == 1 and owners > 1 and owners & (owners - 1) == 0
         self.bits = [1 << b for b in reversed(range(owners.bit_length() - 1))]
-        self.order = (0, 3, 1, 2) if self.direct and owners == 4 else tuple(range(owners))
+        self.order = (0, 2, 3, 1) if self.direct and owners == 4 else tuple(range(owners))
         offsets = [0]
         for bit in self.bits if self.direct else []:
             offsets = offsets + [offset ^ bit for offset in offsets]
         self.places = [self.order.index(offset) for offset in offsets] if self.direct else self.order
         if owners == 4:
-            self.spread = ((0, 2, 1, 3), (1, 3, 0, 2), (2, 0, 3, 1), (3, 1, 2, 0))
+            self.spread = ((1, 0, 3, 2), (0, 2, 1, 3), (2, 3, 0, 1), (3, 1, 2, 0))
         else:
             self.spread = tuple(tuple((q + t) % owners for q in range(owners)) for t in range(owners))
 
@@ -280,14 +290,15 @@
     return lax.ppermute(value, "term", moves)
 
 
-def inputs(plan, left, right):
+def inputs(plan, left, right, stage):
     sectors, owners, groups = plan.sectors, plan.owners, plan.groups
     cores = [(i, i ^ 1) for i in range(sectors)]
     if plan.direct:
-        held = left
-        for bit in plan.bits:
-            lefts = [held, from_owner(plan, held, bit)]
-            held = jnp.concatenate(lefts, axis=0)
+        held = [left]
+        for bit in plan.bits[:-1]:
+            held.append(from_owner(plan, jnp.concatenate(held, axis=0), bit))
+        left, *prepared = stage(left, held[1:])
+        lefts = [left, from_owner(plan, left, plan.bits[-1])]
         own = {}
         for m in plan.order:
             moves = []
@@ -299,7 +310,8 @@
             own[m] = lax.ppermute(right, ("term", "sector"), moves)[None]
         own = [own[m] for m in plan.order]
         swapped = [lax.ppermute(x, "sector", cores) for x in own]
-        return lefts, own, swapped
+        return lefts, own, swapped, prepared
+    left, *prepared = stage(left, [])
     everything = lax.all_gather(right, "sector").reshape((owners, groups, 2) + right.shape)
     by_chip = lax.dynamic_index_in_dim(everything, lax.axis_index("sector") % 2, 2, keepdims=False)
     spread_left = jnp.broadcast_to(left, (owners, 1) + left.shape)
@@ -307,7 +319,7 @@
     swapped = lax.ppermute(got[:, :groups], "sector", cores)
     lefts = [got[t, groups] for t in range(owners)]
     own = [got[t, :groups] for t in range(owners)]
-    return lefts, own, [swapped[t] for t in range(owners)]
+    return lefts, own, [swapped[t] for t in range(owners)], prepared
 
 
 def local(plan, psi, left_env, right_env, precond, block_sizes):
@@ -315,32 +327,45 @@
     devices = owners * sectors
     depth, width = right_env.shape[0], right_env.shape[-1]
     share = 2 * plan.groups
-    lefts, own, swapped = inputs(plan, left_env[:, 0], right_env[:, 0])
-    pieces = len(lefts)
 
     anywhere = pl.BlockSpec(memory_space=pltpu.HBM)
     vmem = pl.BlockSpec(memory_space=pltpu.VMEM)
-    parked = [pltpu.with_memory_space_constraint(x, pltpu.HBM) for x in (block_sizes, psi[0], precond[0])]
     terms, groups = owners * depth, plan.groups
     params = pltpu.CompilerParams(vmem_limit_bytes=32 << 20)
-    prepared = pl.pallas_call(
-        functools.partial(prepare_kernel, plan),
-        out_shape=(
-            jax.ShapeDtypeStruct((groups, terms * width, 2 * width), jnp.bfloat16),
-            jax.ShapeDtypeStruct((2, groups, width, width), jnp.bfloat16),
-            jax.ShapeDtypeStruct((2, groups, width, width), jnp.float32),
-        ),
-        in_specs=[anywhere] * 3 + [vmem] * owners,
-        out_specs=(vmem,) * 3,
-        scratch_shapes=[
-            pltpu.SMEM((sectors,), jnp.int32),
-            pltpu.VMEM((share, width, width), jnp.bfloat16),
-            pltpu.VMEM((share, width, width), jnp.bfloat16),
-            pltpu.SemaphoreType.DMA((3,)),
-        ],
+
+    def stage(left, held):
+        rows = depth + sum(x.shape[0] for x in held)
+        parked = [pltpu.with_memory_space_constraint(x, pltpu.HBM) for x in (block_sizes, psi[0], precond[0], left)]
+        return pl.pallas_call(
+            functools.partial(stage_kernel, plan),
+            out_shape=(
+                jax.ShapeDtypeStruct((rows, width, width), jnp.bfloat16),
+                jax.ShapeDtypeStruct((2, groups, width, width), jnp.bfloat16),
+                jax.ShapeDtypeStruct((2, groups, width, width), jnp.float32),
+            ),
+            in_specs=[anywhere] * 4 + [vmem] * len(held),
+            out_specs=(vmem,) * 3,
+            scratch_shapes=[
+                pltpu.SMEM((sectors,), jnp.int32),
+                pltpu.VMEM((share, width, width), jnp.bfloat16),
+                pltpu.VMEM((share, width, width), jnp.bfloat16),
+                pltpu.VMEM((depth, width, width), jnp.bfloat16),
+                pltpu.SemaphoreType.DMA((4,)),
+            ],
+            compiler_params=params,
+            name="stage",
+        )(*parked, *held)
+
+    lefts, own, swapped, prepared = inputs(plan, left_env[:, 0], right_env[:, 0], stage)
+    pieces = len(lefts)
+    own_cat = pl.pallas_call(
+        functools.partial(stack_kernel, plan),
+        out_shape=jax.ShapeDtypeStruct((groups, terms * width, 2 * width), jnp.bfloat16),
+        in_specs=[vmem] * owners,
+        out_specs=vmem,
         compiler_params=params,
-        name="prepare",
-    )(*parked, *own)
+        name="stack",
+    )(*own)
     gram, basis = pl.pallas_call(
         functools.partial(levels_kernel, plan, pieces),
         out_shape=(
@@ -356,7 +381,7 @@
         ],
         compiler_params=params,
         name="levels",
-    )(*prepared, *lefts, *swapped)
+    )(own_cat, *prepared, *lefts, *swapped)
     gram = lax.all_to_all(gram, ("term", "sector"), 0, 0, tiled=True)
     count = float(sectors * sectors * width * width)
     blocks, energy = pl.pallas_call(

time: 39.5 us -> 39.3 us (level)
  waiting for transfers between devices: 3.18 us -> 6.23 us
  starting transfers between devices: 18.9 us -> 16.5 us
  other arithmetic: 0.85 us -> 0 us
    ppermute x5, starting transfers between devices: 9.13 us -> 7.03 us  [from_owner(): return lax.ppermute(value, 'term', moves)]
    ppermute x5, waiting for transfers between devices: 3.16 us -> 4.33 us  [from_owner(): return lax.ppermute(value, 'term', moves)]
    ppermute x4, waiting for transfers between devices: 0.01 us -> 1.17 us  [inputs(): swapped = [lax.ppermute(x, 'sector', cores) for x in own]]
    concatenate x1 -> x0, other arithmetic: 0.85 us -> none  [inputs(): held = jnp.concatenate(lefts, axis=0)]
    ppermute x4, waiting for transfers between devices: 0.01 us -> 0.73 us  [inputs(): own[m] = lax.ppermute(right, ('term', 'sector'), moves)[None]]
    ppermute x4, starting transfers between devices: 1.02 us -> 0.58 us  [inputs(): swapped = [lax.ppermute(x, 'sector', cores) for x in own]]
    pallas_call x1 -> x2, Pallas kernels: 1.01 us -> 1.08 us  [the longest x1 1.01 us: stage(): pl.pallas_call(functools.partial(stage_kernel, plan), out_shape=(jax.Shap...]
  transfers between devices with their start and end apart: 13 -> 13, of which waited for: 4 -> 7; matrix products, arithmetic and copies ran while one was open for 3% -> 1% of each run, Pallas kernels for 3% -> 3%
where the time goes in v8:
time: 39.3 us; the launch traced here: 39.1 us
  starting transfers between devices  16.5 us (42%)
  blocking collectives  10.5 us (27%)
  waiting for transfers between devices  6.23 us (16%)
  Pallas kernels  4.65 us (12%)
  between operations  0.69 us (2%)
  local copies, waits for them, and re-layouts  0.51 us (1%)
    all_to_all x1, blocking collectives, local(): gram = lax.all_to_all(gram, ('term', 'sector'), 0, 0, tiled=True)  10.5 us
    ppermute x4, starting transfers between devices, inputs(): own[m] = lax.ppermute(right, ('term', 'sector'), moves)[None]  8.87 us
    ppermute x5, starting transfers between devices, from_owner(): return lax.ppermute(value, 'term', moves)  7.03 us
    ppermute x5, waiting for transfers between devices, from_owner(): return lax.ppermute(value, 'term', moves)  4.33 us
    pallas_call x1, Pallas kernels, local(): pl.pallas_call(functools.partial(levels_kernel, plan, pieces), out_shape=...  2.45 us
    ppermute x4, waiting for transfers between devices, inputs(): swapped = [lax.ppermute(x, 'sector', cores) for x in own]  1.17 us
    pallas_call x1, Pallas kernels, stage(): pl.pallas_call(functools.partial(stage_kernel, plan), out_shape=(jax.Shap...  1.01 us
  transfers between devices with their start and end apart: 13, of which 7 were waited for; matrix products, arithmetic and copies ran while one was open for 1% of the time, Pallas kernels for 3%

profile of v8, /device:TPU:0, one launch (start us, length us, event | category | flops | bytes accessed | tf_op | source)
XLA Modules:
  0.0 39.1 jit_solution(4723988750470535355)
XLA Ops:
  0.6 3.0 %collective-permute-start.4 = (bf16[2,128,128]{2,1,0:T(8,128)(2,1)}, bf16[2,128,128]{2,1,0:T(8,128)(2,1)S(1)}, u32[]{:S(2)}, u32[]{:S(2)}) collective-permute-start(bf16[2,128,128]{2,1,0:T(8,128)(2,1)} %bitcast.28), channel_id=1, source_target_pairs={{16,0},{24,8},{0,16},{8,24},{17,1},{25,9},{1,17},{9,25},{18,2},{26... | collective-permute-start | bytes 196616 | tf_op jit(solution)/shard_map/ppermute | solution.py:290
  3.7 1.5 %collective-permute-start.3 = (bf16[2,128,128]{2,1,0:T(8,128)(2,1)}, bf16[2,128,128]{2,1,0:T(8,128)(2,1)S(1)}, u32[]{:S(2)}, u32[]{:S(2)}) collective-permute-start(bf16[2,128,128]{2,1,0:T(8,128)(2,1)} %bitcast.30), channel_id=1, source_target_pairs={{8,2},{9,3},{10,0},{11,1},{12,6},{13,7},{14,4},{15,5},{0,8},{1,9},... | collective-permute-start | bytes 196616 | tf_op jit(solution)/shard_map/ppermute | solution.py:310
  5.2 3.3 %collective-permute-start.2 = (bf16[2,128,128]{2,1,0:T(8,128)(2,1)}, bf16[2,128,128]{2,1,0:T(8,128)(2,1)S(1)}, u32[]{:S(2)}, u32[]{:S(2)}) collective-permute-start(bf16[2,128,128]{2,1,0:T(8,128)(2,1)} %bitcast.31), channel_id=1, source_target_pairs={{24,2},{25,3},{26,0},{27,1},{28,6},{29,7},{30,4},{31,5},{16,8},{17... | collective-permute-start | bytes 196616 | tf_op jit(solution)/shard_map/ppermute | solution.py:310
  8.4 0.5 %collective-permute-start.1 = (bf16[2,128,128]{2,1,0:T(8,128)(2,1)}, bf16[2,128,128]{2,1,0:T(8,128)(2,1)S(1)}, u32[]{:S(2)}, u32[]{:S(2)}) collective-permute-start(bf16[2,128,128]{2,1,0:T(8,128)(2,1)} %bitcast.32), channel_id=1, source_target_pairs={{16,2},{17,3},{18,0},{19,1},{20,6},{21,7},{22,4},{23,5},{24,8},{25... | collective-permute-start | bytes 196616 | tf_op jit(solution)/shard_map/ppermute | solution.py:310
  9.0 3.6 %collective-permute-start = (bf16[2,128,128]{2,1,0:T(8,128)(2,1)}, bf16[2,128,128]{2,1,0:T(8,128)(2,1)S(1)}, u32[]{:S(2)}, u32[]{:S(2)}) collective-permute-start(bf16[2,128,128]{2,1,0:T(8,128)(2,1)} %bitcast.33), channel_id=1, source_target_pairs={{0,2},{1,3},{2,0},{3,1},{4,6},{5,7},{6,4},{7,5},{8,8},{9,9},{10,12... | collective-permute-start | bytes 196616 | tf_op jit(solution)/shard_map/ppermute | solution.py:310
  12.5 0.0 collective-permute-done.4.refs_0_
  12.6 1.0 %stage.1 = (bf16[4,128,128]{2,1,0:T(8,128)(2,1)S(1)}, bf16[2,1,128,128]{3,2,1,0:T(8,128)(2,1)S(1)}, f32[2,1,128,128]{3,2,1,0:T(8,128)S(1)}) custom-call(s32[8]{0:T(128)} %sizes_hbm.1, bf16[8,128,128]{2,1,0:T(8,128)(2,1)} %bitcast.25, bf16[8,128,128]{2,1,0:T(8,128)(2,1)} %bitcast.26, bf16[2,128,128]{2,1,0:T(8,128)(2,1)} %bitcast.29, ...), custom_call_target="tpu_custom_call" | custom-call | tf_op jit(solution)/shard_map/stage/pallas_call | solution.py:339
  13.6 0.4 %collective-permute-start.5 = (bf16[4,128,128]{2,1,0:T(8,128)(2,1)S(1)}, bf16[4,128,128]{2,1,0:T(8,128)(2,1)S(1)}, u32[]{:S(2)}, u32[]{:S(2)}) collective-permute-start(bf16[4,128,128]{2,1,0:T(8,128)(2,1)S(1)} %get-tuple-element.11.refs_0_), channel_id=1, source_target_pairs={{8,0},{0,8},{24,16},{16,24},{9,1},{1,9},{25,17},{17,25},{10,2},{2,... | collective-permute-start | bytes 393224 | tf_op jit(solution)/shard_map/ppermute | solution.py:290
  14.0 0.0 collective-permute-done.3
  14.0 0.0 collective-permute-start.9
  14.0 0.0 collective-permute-done.2
  14.0 0.5 %collective-permute-start.8 = (bf16[1,2,128,128]{3,2,1,0:T(8,128)(2,1)S(1)}, bf16[1,2,128,128]{3,2,1,0:T(8,128)(2,1)S(1)}, u32[]{:S(2)}, u32[]{:S(2)}) collective-permute-start(bf16[1,2,128,128]{3,2,1,0:T(8,128)(2,1)S(1)} %bitcast.18), channel_id=1, source_target_pairs={{0,1},{1,0},{2,3},{3,2},{4,5},{5,4},{6,7},{7,6},{8,9},{9,8},{10,11... | collective-permute-start | bytes 196616 | tf_op jit(solution)/shard_map/ppermute | solution.py:312
  14.5 0.0 collective-permute-done.1
  14.5 0.1 collective-permute-start.7
  14.6 0.7 %collective-permute-done = bf16[2,128,128]{2,1,0:T(8,128)(2,1)S(1)} collective-permute-done((bf16[2,128,128]{2,1,0:T(8,128)(2,1)}, bf16[2,128,128]{2,1,0:T(8,128)(2,1)S(1)}, u32[]{:S(2)}, u32[]{:S(2)}) %collective-permute-start) | collective-permute-done | bytes 65568 | tf_op jit(solution)/shard_map/ppermute | solution.py:310
  15.3 0.0 collective-permute-start.6
  15.3 0.1 stack.1.own_cat
  15.4 0.0 collective-permute-done.8.refs_4_
  15.4 0.4 collective-permute-done.7.refs_3_
  15.8 0.8 %collective-permute-done.6.refs_2_ = bf16[1,2,128,128]{3,2,1,0:T(8,128)(2,1)S(1)} collective-permute-done((bf16[1,2,128,128]{3,2,1,0:T(8,128)(2,1)S(1)}, bf16[1,2,128,128]{3,2,1,0:T(8,128)(2,1)S(1)}, u32[]{:S(2)}, u32[]{:S(2)}) %collective-permute-start.6) | collective-permute-done | bytes 65568 | tf_op jit(solution)/shard_map/ppermute | solution.py:312
  16.6 2.0 %collective-permute-done.5.refs_1_ = bf16[4,128,128]{2,1,0:T(8,128)(2,1)S(1)} collective-permute-done((bf16[4,128,128]{2,1,0:T(8,128)(2,1)S(1)}, bf16[4,128,128]{2,1,0:T(8,128)(2,1)S(1)}, u32[]{:S(2)}, u32[]{:S(2)}) %collective-permute-start.5) | collective-permute-done | bytes 131104 | tf_op jit(solution)/shard_map/ppermute | solution.py:290
  18.6 2.4 %levels.1 = (f32[32,128]{1,0:T(8,128)S(1)}, f32[8,2,128,128]{3,2,1,0:T(8,128)S(1)}) custom-call(bf16[1,1024,256]{2,1,0:T(8,128)(2,1)S(1)} %stack.1.own_cat, bf16[2,1,128,128]{3,2,1,0:T(8,128)(2,1)S(1)} %get-tuple-element.9.start_ref, f32[2,1,128,128]{3,2,1,0:T(8,128)S(1)} %get-tuple-element.10.inverse_ref, ...), custom_call_target="tpu_custom_call" | custom-call | tf_op jit(solution)/shard_map/levels/pallas_call | solution.py:369
  21.1 10.5 %all_to_all.11 = f32[32,1,128]{2,1,0:T(1,128)S(1)} all-to-all(f32[32,1,128]{2,1,0:T(1,128)S(1)} %bitcast.24), channel_id=1, replica_groups=mesh['term'=4,'sector'=8] {'term','sector'}, dimensions={0} | all-to-all | bytes 32768 | tf_op jit(solution)/shard_map/all_to_all | solution.py:385
  31.6 0.4 finish.1
  32.0 0.7 %collective-permute-start.12 = (bf16[2,128,128]{2,1,0:T(8,128)(2,1)S(1)}, bf16[2,128,128]{2,1,0:T(8,128)(2,1)S(1)}, u32[]{:S(2)}, u32[]{:S(2)}) collective-permute-start(bf16[2,128,128]{2,1,0:T(8,128)(2,1)S(1)} %get-tuple-element.14.refs_0_), channel_id=1, source_target_pairs={{24,0},{16,8},{8,16},{0,24},{25,1},{17,9},{9,17},{1,25},{26,2},{18... | collective-permute-start | bytes 196616 | tf_op jit(solution)/shard_map/ppermute | solution.py:290
  32.7 1.4 %collective-permute-start.11 = (bf16[2,128,128]{2,1,0:T(8,128)(2,1)S(1)}, bf16[2,128,128]{2,1,0:T(8,128)(2,1)S(1)}, u32[]{:S(2)}, u32[]{:S(2)}) collective-permute-start(bf16[2,128,128]{2,1,0:T(8,128)(2,1)S(1)} %get-tuple-element.14.refs_0_), channel_id=1, source_target_pairs={{16,0},{24,8},{0,16},{8,24},{17,1},{25,9},{1,17},{9,25},{18,2},{26... | collective-permute-start | bytes 196616 | tf_op jit(solution)/shard_map/ppermute | solution.py:290
  34.1 1.4 %collective-permute-start.10 = (bf16[2,128,128]{2,1,0:T(8,128)(2,1)S(1)}, bf16[2,128,128]{2,1,0:T(8,128)(2,1)S(1)}, u32[]{:S(2)}, u32[]{:S(2)}) collective-permute-start(bf16[2,128,128]{2,1,0:T(8,128)(2,1)S(1)} %get-tuple-element.14.refs_0_), channel_id=1, source_target_pairs={{8,0},{0,8},{24,16},{16,24},{9,1},{1,9},{25,17},{17,25},{10,2},{2,... | collective-permute-start | bytes 196616 | tf_op jit(solution)/shard_map/ppermute | solution.py:290
  35.6 0.5 %slice_bitcast_fusion = f32[3]{0:T(128)} fusion(f32[1,128]{1,0:T(1,128)S(1)} %get-tuple-element.15), kind=kLoop, calls=%fused_computation | loop fusion | bytes 24 | tf_op jit(solution)/shard_map/squeeze | solution.py:407
  36.1 1.5 %collective-permute-done.12.refs_3_ = bf16[2,128,128]{2,1,0:T(8,128)(2,1)S(1)} collective-permute-done((bf16[2,128,128]{2,1,0:T(8,128)(2,1)S(1)}, bf16[2,128,128]{2,1,0:T(8,128)(2,1)S(1)}, u32[]{:S(2)}, u32[]{:S(2)}) %collective-permute-start.12) | collective-permute-done | bytes 65568 | tf_op jit(solution)/shard_map/ppermute | solution.py:290
  37.6 0.1 collective-permute-done.11.refs_2_
  37.6 0.7 %collective-permute-done.10.refs_1_ = bf16[2,128,128]{2,1,0:T(8,128)(2,1)S(1)} collective-permute-done((bf16[2,128,128]{2,1,0:T(8,128)(2,1)S(1)}, bf16[2,128,128]{2,1,0:T(8,128)(2,1)S(1)}, u32[]{:S(2)}, u32[]{:S(2)}) %collective-permute-start.10) | collective-permute-done | bytes 65568 | tf_op jit(solution)/shard_map/ppermute | solution.py:290
  38.4 0.7 %assemble.1 = bf16[8,128,128]{2,1,0:T(8,128)(2,1)} custom-call(bf16[2,128,128]{2,1,0:T(8,128)(2,1)S(1)} %get-tuple-element.14.refs_0_, bf16[2,128,128]{2,1,0:T(8,128)(2,1)S(1)} %collective-permute-done.10.refs_1_, bf16[2,128,128]{2,1,0:T(8,128)(2,1)S(1)} %collective-permute-done.11.refs_2_, bf16[2,128,128]{2,1,0:T(8,128)(2,1)S(1)} %collective-permute-done.12.refs_3_), custom_call_target="tpu_custom_call" | custom-call | tf_op jit(solution)/shard_map/assemble/pallas_call | solution.py:398
  (1 shorter events, 0.0 us)
Async XLA Ops:
  0.6 11.9 %collective-permute-start.4 = (bf16[2,128,128]{2,1,0:T(8,128)(2,1)}, bf16[2,128,128]{2,1,0:T(8,128)(2,1)S(1)}, u32[]{:S(2)}, u32[]{:S(2)}) collective-permute-start(bf16[2,128,128]{2,1,0:T(8,128)(2,1)} %bitcast.28), channel_id=1, source_target_pairs={{16,0},{24,8},{0,16},{8,24},{17,1},{25,9},{1,17},{9,25},{18,2},{26... | collective-permute-start | bytes 196616 | tf_op jit(solution)/shard_map/ppermute | solution.py:290
  3.7 10.4 %collective-permute-start.3 = (bf16[2,128,128]{2,1,0:T(8,128)(2,1)}, bf16[2,128,128]{2,1,0:T(8,128)(2,1)S(1)}, u32[]{:S(2)}, u32[]{:S(2)}) collective-permute-start(bf16[2,128,128]{2,1,0:T(8,128)(2,1)} %bitcast.30), channel_id=1, source_target_pairs={{8,2},{9,3},{10,0},{11,1},{12,6},{13,7},{14,4},{15,5},{0,8},{1,9},... | collective-permute-start | bytes 196616 | tf_op jit(solution)/shard_map/ppermute | solution.py:310
  5.2 8.9 %collective-permute-start.2 = (bf16[2,128,128]{2,1,0:T(8,128)(2,1)}, bf16[2,128,128]{2,1,0:T(8,128)(2,1)S(1)}, u32[]{:S(2)}, u32[]{:S(2)}) collective-permute-start(bf16[2,128,128]{2,1,0:T(8,128)(2,1)} %bitcast.31), channel_id=1, source_target_pairs={{24,2},{25,3},{26,0},{27,1},{28,6},{29,7},{30,4},{31,5},{16,8},{17... | collective-permute-start | bytes 196616 | tf_op jit(solution)/shard_map/ppermute | solution.py:310
  8.4 6.1 %collective-permute-start.1 = (bf16[2,128,128]{2,1,0:T(8,128)(2,1)}, bf16[2,128,128]{2,1,0:T(8,128)(2,1)S(1)}, u32[]{:S(2)}, u32[]{:S(2)}) collective-permute-start(bf16[2,128,128]{2,1,0:T(8,128)(2,1)} %bitcast.32), channel_id=1, source_target_pairs={{16,2},{17,3},{18,0},{19,1},{20,6},{21,7},{22,4},{23,5},{24,8},{25... | collective-permute-start | bytes 196616 | tf_op jit(solution)/shard_map/ppermute | solution.py:310
  9.0 6.4 %collective-permute-start = (bf16[2,128,128]{2,1,0:T(8,128)(2,1)}, bf16[2,128,128]{2,1,0:T(8,128)(2,1)S(1)}, u32[]{:S(2)}, u32[]{:S(2)}) collective-permute-start(bf16[2,128,128]{2,1,0:T(8,128)(2,1)} %bitcast.33), channel_id=1, source_target_pairs={{0,2},{1,3},{2,0},{3,1},{4,6},{5,7},{6,4},{7,5},{8,8},{9,9},{10,12... | collective-permute-start | bytes 196616 | tf_op jit(solution)/shard_map/ppermute | solution.py:310
  13.6 5.0 %collective-permute-start.5 = (bf16[4,128,128]{2,1,0:T(8,128)(2,1)S(1)}, bf16[4,128,128]{2,1,0:T(8,128)(2,1)S(1)}, u32[]{:S(2)}, u32[]{:S(2)}) collective-permute-start(bf16[4,128,128]{2,1,0:T(8,128)(2,1)S(1)} %get-tuple-element.11.refs_0_), channel_id=1, source_target_pairs={{8,0},{0,8},{24,16},{16,24},{9,1},{1,9},{25,17},{17,25},{10,2},{2,... | collective-permute-start | bytes 393224 | tf_op jit(solution)/shard_map/ppermute | solution.py:290
  14.0 1.4 %collective-permute-start.9 = (bf16[1,2,128,128]{3,2,1,0:T(8,128)(2,1)S(1)}, bf16[1,2,128,128]{3,2,1,0:T(8,128)(2,1)S(1)}, u32[]{:S(2)}, u32[]{:S(2)}) collective-permute-start(bf16[1,2,128,128]{3,2,1,0:T(8,128)(2,1)S(1)} %bitcast.16), channel_id=1, source_target_pairs={{0,1},{1,0},{2,3},{3,2},{4,5},{5,4},{6,7},{7,6},{8,9},{9,8},{10,11... | collective-permute-start | bytes 196616 | tf_op jit(solution)/shard_map/ppermute | solution.py:312
  14.0 1.4 %collective-permute-start.8 = (bf16[1,2,128,128]{3,2,1,0:T(8,128)(2,1)S(1)}, bf16[1,2,128,128]{3,2,1,0:T(8,128)(2,1)S(1)}, u32[]{:S(2)}, u32[]{:S(2)}) collective-permute-start(bf16[1,2,128,128]{3,2,1,0:T(8,128)(2,1)S(1)} %bitcast.18), channel_id=1, source_target_pairs={{0,1},{1,0},{2,3},{3,2},{4,5},{5,4},{6,7},{7,6},{8,9},{9,8},{10,11... | collective-permute-start | bytes 196616 | tf_op jit(solution)/shard_map/ppermute | solution.py:312
  14.5 1.3 %collective-permute-start.7 = (bf16[1,2,128,128]{3,2,1,0:T(8,128)(2,1)S(1)}, bf16[1,2,128,128]{3,2,1,0:T(8,128)(2,1)S(1)}, u32[]{:S(2)}, u32[]{:S(2)}) collective-permute-start(bf16[1,2,128,128]{3,2,1,0:T(8,128)(2,1)S(1)} %bitcast.20), channel_id=1, source_target_pairs={{0,1},{1,0},{2,3},{3,2},{4,5},{5,4},{6,7},{7,6},{8,9},{9,8},{10,11... | collective-permute-start | bytes 196616 | tf_op jit(solution)/shard_map/ppermute | solution.py:312
  15.3 1.3 %collective-permute-start.6 = (bf16[1,2,128,128]{3,2,1,0:T(8,128)(2,1)S(1)}, bf16[1,2,128,128]{3,2,1,0:T(8,128)(2,1)S(1)}, u32[]{:S(2)}, u32[]{:S(2)}) collective-permute-start(bf16[1,2,128,128]{3,2,1,0:T(8,128)(2,1)S(1)} %bitcast.22), channel_id=1, source_target_pairs={{0,1},{1,0},{2,3},{3,2},{4,5},{5,4},{6,7},{7,6},{8,9},{9,8},{10,11... | collective-permute-start | bytes 196616 | tf_op jit(solution)/shard_map/ppermute | solution.py:312
  32.0 5.6 %collective-permute-start.12 = (bf16[2,128,128]{2,1,0:T(8,128)(2,1)S(1)}, bf16[2,128,128]{2,1,0:T(8,128)(2,1)S(1)}, u32[]{:S(2)}, u32[]{:S(2)}) collective-permute-start(bf16[2,128,128]{2,1,0:T(8,128)(2,1)S(1)} %get-tuple-element.14.refs_0_), channel_id=1, source_target_pairs={{24,0},{16,8},{8,16},{0,24},{25,1},{17,9},{9,17},{1,25},{26,2},{18... | collective-permute-start | bytes 196616 | tf_op jit(solution)/shard_map/ppermute | solution.py:290
  32.7 5.0 %collective-permute-start.11 = (bf16[2,128,128]{2,1,0:T(8,128)(2,1)S(1)}, bf16[2,128,128]{2,1,0:T(8,128)(2,1)S(1)}, u32[]{:S(2)}, u32[]{:S(2)}) collective-permute-start(bf16[2,128,128]{2,1,0:T(8,128)(2,1)S(1)} %get-tuple-element.14.refs_0_), channel_id=1, source_target_pairs={{16,0},{24,8},{0,16},{8,24},{17,1},{25,9},{1,17},{9,25},{18,2},{26... | collective-permute-start | bytes 196616 | tf_op jit(solution)/shard_map/ppermute | solution.py:290
  34.1 4.3 %collective-permute-start.10 = (bf16[2,128,128]{2,1,0:T(8,128)(2,1)S(1)}, bf16[2,128,128]{2,1,0:T(8,128)(2,1)S(1)}, u32[]{:S(2)}, u32[]{:S(2)}) collective-permute-start(bf16[2,128,128]{2,1,0:T(8,128)(2,1)S(1)} %get-tuple-element.14.refs_0_), channel_id=1, source_target_pairs={{8,0},{0,8},{24,16},{16,24},{9,1},{1,9},{25,17},{17,25},{10,2},{2,... | collective-permute-start | bytes 196616 | tf_op jit(solution)/shard_map/ppermute | solution.py:290

commit v9 on v7

--- a/solution.py
+++ b/solution.py
@@ -267,14 +267,14 @@
         self.groups = self.chips // owners
         self.direct = self.groups == 1 and owners > 1 and owners & (owners - 1) == 0
         self.bits = [1 << b for b in reversed(range(owners.bit_length() - 1))]
-        self.order = (0, 2, 3, 1) if self.direct and owners == 4 else tuple(range(owners))
+        self.order = (0, 3, 1, 2) if self.direct and owners == 4 else tuple(range(owners))
         self.last = (0, 2, 1, 3) if owners == 4 else tuple(range(owners))
         offsets = [0]
         for bit in self.bits if self.direct else []:
             offsets = offsets + [offset ^ bit for offset in offsets]
         self.places = [self.order.index(offset) for offset in offsets] if self.direct else self.order
         if owners == 4:
-            self.spread = ((1, 0, 3, 2), (0, 2, 1, 3), (2, 3, 0, 1), (3, 1, 2, 0))
+            self.spread = ((2, 3, 1, 0), (0, 1, 3, 2), (3, 2, 0, 1), (1, 0, 2, 3))
         else:
             self.spread = tuple(tuple((q + t) % owners for q in range(owners)) for t in range(owners))
 

time: 39.2 us -> 39.3 us (level)
  blocking collectives: 10.5 us -> 9.73 us
  starting transfers between devices: 16.5 us -> 17 us
  waiting for transfers between devices: 5.27 us -> 5.69 us
    ppermute x4, waiting for transfers between devices: 0.89 us -> 2.39 us  [inputs(): own[m] = lax.ppermute(right, ('term', 'sector'), moves)[None]]
    ppermute x5, waiting for transfers between devices: 4.18 us -> 3.09 us  [from_owner(): return lax.ppermute(value, 'term', moves)]
    ppermute x4, starting transfers between devices: 8.87 us -> 9.77 us  [inputs(): own[m] = lax.ppermute(right, ('term', 'sector'), moves)[None]]
    all_to_all x1, blocking collectives: 10.5 us -> 9.73 us  [local(): gram = lax.all_to_all(gram, ('term', 'sector'), 0, 0, tiled=True)]
  transfers between devices with their start and end apart: 13 -> 13, of which waited for: 5 -> 6; matrix products, arithmetic and copies ran while one was open for 1% -> 1% of each run, Pallas kernels for 5% -> 5%
where the time goes in v9:
time: 39.3 us; the launch traced here: 39 us
  starting transfers between devices  17 us (43%)
  blocking collectives  9.73 us (25%)
  waiting for transfers between devices  5.69 us (14%)
  Pallas kernels  5.43 us (14%)
  between operations  0.73 us (2%)
  local copies, waits for them, and re-layouts  0.51 us (1%)
    ppermute x4, starting transfers between devices, inputs(): own[m] = lax.ppermute(right, ('term', 'sector'), moves)[None]  9.77 us
    all_to_all x1, blocking collectives, local(): gram = lax.all_to_all(gram, ('term', 'sector'), 0, 0, tiled=True)  9.73 us
    ppermute x5, starting transfers between devices, from_owner(): return lax.ppermute(value, 'term', moves)  6.66 us
    ppermute x5, waiting for transfers between devices, from_owner(): return lax.ppermute(value, 'term', moves)  3.09 us
    pallas_call x1, Pallas kernels, local(): pl.pallas_call(functools.partial(levels_kernel, plan, pieces), out_shape=...  2.45 us
    ppermute x4, waiting for transfers between devices, inputs(): own[m] = lax.ppermute(right, ('term', 'sector'), moves)[None]  2.39 us
    pallas_call x1, Pallas kernels, local(): pl.pallas_call(functools.partial(prepare_kernel, plan), out_shape=(jax.Sh...  1.01 us
    pallas_call x1, Pallas kernels, join(): pl.pallas_call(join_kernel, out_shape=jax.ShapeDtypeStruct((rows,) + own....  0.85 us
  transfers between devices with their start and end apart: 13, of which 6 were waited for; matrix products, arithmetic and copies ran while one was open for 1% of the time, Pallas kernels for 5%

profile of v9, /device:TPU:0, one launch (start us, length us, event | category | flops | bytes accessed | tf_op | source)
XLA Modules:
  0.0 39.0 jit_solution(7141076899681456573)
XLA Ops:
  0.6 3.0 %collective-permute-start.4 = (bf16[2,128,128]{2,1,0:T(8,128)(2,1)}, bf16[2,128,128]{2,1,0:T(8,128)(2,1)S(1)}, u32[]{:S(2)}, u32[]{:S(2)}) collective-permute-start(bf16[2,128,128]{2,1,0:T(8,128)(2,1)} %bitcast.28), channel_id=1, source_target_pairs={{16,0},{24,8},{0,16},{8,24},{17,1},{25,9},{1,17},{9,25},{18,2},{26... | collective-permute-start | bytes 196616 | tf_op jit(solution)/shard_map/ppermute | solution.py:306
  3.7 3.5 %collective-permute-start.3 = (bf16[2,128,128]{2,1,0:T(8,128)(2,1)}, bf16[2,128,128]{2,1,0:T(8,128)(2,1)S(1)}, u32[]{:S(2)}, u32[]{:S(2)}) collective-permute-start(bf16[2,128,128]{2,1,0:T(8,128)(2,1)} %bitcast.30), channel_id=1, source_target_pairs={{16,4},{17,5},{18,6},{19,7},{20,2},{21,3},{22,0},{23,1},{24,8},{25... | collective-permute-start | bytes 196616 | tf_op jit(solution)/shard_map/ppermute | solution.py:326
  7.2 0.0 collective-permute-start.2
  7.2 1.9 %collective-permute-start.1 = (bf16[2,128,128]{2,1,0:T(8,128)(2,1)}, bf16[2,128,128]{2,1,0:T(8,128)(2,1)S(1)}, u32[]{:S(2)}, u32[]{:S(2)}) collective-permute-start(bf16[2,128,128]{2,1,0:T(8,128)(2,1)} %bitcast.32), channel_id=1, source_target_pairs={{24,4},{25,5},{26,6},{27,7},{28,2},{29,3},{30,0},{31,1},{16,8},{17... | collective-permute-start | bytes 196616 | tf_op jit(solution)/shard_map/ppermute | solution.py:326
  9.1 4.4 %collective-permute-start = (bf16[2,128,128]{2,1,0:T(8,128)(2,1)}, bf16[2,128,128]{2,1,0:T(8,128)(2,1)S(1)}, u32[]{:S(2)}, u32[]{:S(2)}) collective-permute-start(bf16[2,128,128]{2,1,0:T(8,128)(2,1)} %bitcast.33), channel_id=1, source_target_pairs={{0,4},{1,5},{2,6},{3,7},{4,2},{5,3},{6,0},{7,1},{8,8},{9,9},{10,10... | collective-permute-start | bytes 196616 | tf_op jit(solution)/shard_map/ppermute | solution.py:326
  13.4 0.0 collective-permute-done.4.refs_0_
  13.5 0.8 %join.1.refs_0_ = bf16[4,128,128]{2,1,0:T(8,128)(2,1)S(1)} custom-call(bf16[2,128,128]{2,1,0:T(8,128)(2,1)} %bitcast.29, bf16[2,128,128]{2,1,0:T(8,128)(2,1)S(1)} %collective-permute-done.4.refs_0_), custom_call_target="tpu_custom_call" | custom-call | tf_op jit(solution)/shard_map/join/pallas_call | solution.py:169
  14.3 0.1 collective-permute-start.5
  14.4 0.0 collective-permute-done.3
  14.4 0.1 collective-permute-start.9
  14.5 0.0 collective-permute-done.2
  14.5 0.5 %collective-permute-start.8 = (bf16[1,2,128,128]{3,2,1,0:T(8,128)(2,1)S(1)}, bf16[1,2,128,128]{3,2,1,0:T(8,128)(2,1)S(1)}, u32[]{:S(2)}, u32[]{:S(2)}) collective-permute-start(bf16[1,2,128,128]{3,2,1,0:T(8,128)(2,1)S(1)} %bitcast.18), channel_id=1, source_target_pairs={{0,1},{1,0},{2,3},{3,2},{4,5},{5,4},{6,7},{7,6},{8,9},{9,8},{10,11... | collective-permute-start | bytes 196616 | tf_op jit(solution)/shard_map/ppermute | solution.py:328
  15.0 0.4 %collective-permute-done.1 = bf16[2,128,128]{2,1,0:T(8,128)(2,1)S(1)} collective-permute-done((bf16[2,128,128]{2,1,0:T(8,128)(2,1)}, bf16[2,128,128]{2,1,0:T(8,128)(2,1)S(1)}, u32[]{:S(2)}, u32[]{:S(2)}) %collective-permute-start.1) | collective-permute-done | bytes 65568 | tf_op jit(solution)/shard_map/ppermute | solution.py:326
  15.4 0.0 collective-permute-start.7
  15.4 1.9 %collective-permute-done = bf16[2,128,128]{2,1,0:T(8,128)(2,1)S(1)} collective-permute-done((bf16[2,128,128]{2,1,0:T(8,128)(2,1)}, bf16[2,128,128]{2,1,0:T(8,128)(2,1)S(1)}, u32[]{:S(2)}, u32[]{:S(2)}) %collective-permute-start) | collective-permute-done | bytes 65568 | tf_op jit(solution)/shard_map/ppermute | solution.py:326
  17.3 0.0 collective-permute-start.6
  17.3 1.0 %prepare.1 = (bf16[1,1024,256]{2,1,0:T(8,128)(2,1)S(1)}, bf16[2,1,128,128]{3,2,1,0:T(8,128)(2,1)S(1)}, f32[2,1,128,128]{3,2,1,0:T(8,128)S(1)}) custom-call(s32[8]{0:T(128)} %sizes_hbm.1, bf16[8,128,128]{2,1,0:T(8,128)(2,1)} %bitcast.26, bf16[8,128,128]{2,1,0:T(8,128)(2,1)} %bitcast.27, bf16[1,2,128,128]{3,2,1,0:T(8,128)(2,1)S(1)} %bitcast.23, ...), custom_call_target="tpu_custom_call" | custom-call | tf_op jit(solution)/shard_map/prepare/pallas_call | solution.py:353
  18.4 0.0 collective-permute-done.9.refs_5_
  18.4 0.0 collective-permute-done.7.refs_3_
  18.4 0.2 collective-permute-done.6.refs_2_
  18.6 0.8 %collective-permute-done.5.refs_1_ = bf16[4,128,128]{2,1,0:T(8,128)(2,1)S(1)} collective-permute-done((bf16[4,128,128]{2,1,0:T(8,128)(2,1)S(1)}, bf16[4,128,128]{2,1,0:T(8,128)(2,1)S(1)}, u32[]{:S(2)}, u32[]{:S(2)}) %collective-permute-start.5) | collective-permute-done | bytes 131104 | tf_op jit(solution)/shard_map/ppermute | solution.py:306
  19.3 2.4 %levels.1 = (f32[32,128]{1,0:T(8,128)S(1)}, f32[8,2,128,128]{3,2,1,0:T(8,128)S(1)}) custom-call(bf16[1,1024,256]{2,1,0:T(8,128)(2,1)S(1)} %get-tuple-element.9.own_cat, bf16[2,1,128,128]{3,2,1,0:T(8,128)(2,1)S(1)} %get-tuple-element.10.start_ref, f32[2,1,128,128]{3,2,1,0:T(8,128)S(1)} %get-tuple-element.11.inverse_ref, ...), custom_call_target="tpu_custom_call" | custom-call | tf_op jit(solution)/shard_map/levels/pallas_call | solution.py:371
  21.8 9.7 %all_to_all.11 = f32[32,1,128]{2,1,0:T(1,128)S(1)} all-to-all(f32[32,1,128]{2,1,0:T(1,128)S(1)} %bitcast.24), channel_id=1, replica_groups=mesh['term'=4,'sector'=8] {'term','sector'}, dimensions={0} | all-to-all | bytes 32768 | tf_op jit(solution)/shard_map/all_to_all | solution.py:387
  31.5 0.4 %finish.1 = (bf16[2,128,128]{2,1,0:T(8,128)(2,1)S(1)}, f32[1,128]{1,0:T(1,128)S(1)}) custom-call(f32[32,128]{1,0:T(8,128)S(1)} %bitcast.15, f32[8,2,128,128]{3,2,1,0:T(8,128)S(1)} %get-tuple-element.13.basis_ref), custom_call_target="tpu_custom_call" | custom-call | tf_op jit(solution)/shard_map/finish/pallas_call | solution.py:389
  31.9 0.7 %collective-permute-start.12 = (bf16[2,128,128]{2,1,0:T(8,128)(2,1)S(1)}, bf16[2,128,128]{2,1,0:T(8,128)(2,1)S(1)}, u32[]{:S(2)}, u32[]{:S(2)}) collective-permute-start(bf16[2,128,128]{2,1,0:T(8,128)(2,1)S(1)} %get-tuple-element.14.refs_0_), channel_id=1, source_target_pairs={{24,0},{16,8},{8,16},{0,24},{25,1},{17,9},{9,17},{1,25},{26,2},{18... | collective-permute-start | bytes 196616 | tf_op jit(solution)/shard_map/ppermute | solution.py:306
  32.6 1.4 %collective-permute-start.11 = (bf16[2,128,128]{2,1,0:T(8,128)(2,1)S(1)}, bf16[2,128,128]{2,1,0:T(8,128)(2,1)S(1)}, u32[]{:S(2)}, u32[]{:S(2)}) collective-permute-start(bf16[2,128,128]{2,1,0:T(8,128)(2,1)S(1)} %get-tuple-element.14.refs_0_), channel_id=1, source_target_pairs={{8,0},{0,8},{24,16},{16,24},{9,1},{1,9},{25,17},{17,25},{10,2},{2,... | collective-permute-start | bytes 196616 | tf_op jit(solution)/shard_map/ppermute | solution.py:306
  34.0 1.4 %collective-permute-start.10 = (bf16[2,128,128]{2,1,0:T(8,128)(2,1)S(1)}, bf16[2,128,128]{2,1,0:T(8,128)(2,1)S(1)}, u32[]{:S(2)}, u32[]{:S(2)}) collective-permute-start(bf16[2,128,128]{2,1,0:T(8,128)(2,1)S(1)} %get-tuple-element.14.refs_0_), channel_id=1, source_target_pairs={{16,0},{24,8},{0,16},{8,24},{17,1},{25,9},{1,17},{9,25},{18,2},{26... | collective-permute-start | bytes 196616 | tf_op jit(solution)/shard_map/ppermute | solution.py:306
  35.5 0.5 %slice_bitcast_fusion = f32[3]{0:T(128)} fusion(f32[1,128]{1,0:T(1,128)S(1)} %get-tuple-element.15), kind=kLoop, calls=%fused_computation | loop fusion | bytes 24 | tf_op jit(solution)/shard_map/squeeze | solution.py:409
  36.0 1.5 %collective-permute-done.12.refs_3_ = bf16[2,128,128]{2,1,0:T(8,128)(2,1)S(1)} collective-permute-done((bf16[2,128,128]{2,1,0:T(8,128)(2,1)S(1)}, bf16[2,128,128]{2,1,0:T(8,128)(2,1)S(1)}, u32[]{:S(2)}, u32[]{:S(2)}) %collective-permute-start.12) | collective-permute-done | bytes 65568 | tf_op jit(solution)/shard_map/ppermute | solution.py:306
  37.5 0.0 collective-permute-done.11.refs_2_
  37.5 0.8 %collective-permute-done.10.refs_1_ = bf16[2,128,128]{2,1,0:T(8,128)(2,1)S(1)} collective-permute-done((bf16[2,128,128]{2,1,0:T(8,128)(2,1)S(1)}, bf16[2,128,128]{2,1,0:T(8,128)(2,1)S(1)}, u32[]{:S(2)}, u32[]{:S(2)}) %collective-permute-start.10) | collective-permute-done | bytes 65568 | tf_op jit(solution)/shard_map/ppermute | solution.py:306
  38.3 0.7 %assemble.1 = bf16[8,128,128]{2,1,0:T(8,128)(2,1)} custom-call(bf16[2,128,128]{2,1,0:T(8,128)(2,1)S(1)} %get-tuple-element.14.refs_0_, bf16[2,128,128]{2,1,0:T(8,128)(2,1)S(1)} %collective-permute-done.10.refs_1_, bf16[2,128,128]{2,1,0:T(8,128)(2,1)S(1)} %collective-permute-done.11.refs_2_, bf16[2,128,128]{2,1,0:T(8,128)(2,1)S(1)} %collective-permute-done.12.refs_3_), custom_call_target="tpu_custom_call" | custom-call | tf_op jit(solution)/shard_map/assemble/pallas_call | solution.py:400
  (1 shorter events, 0.0 us)
Async XLA Ops:
  0.6 12.8 %collective-permute-start.4 = (bf16[2,128,128]{2,1,0:T(8,128)(2,1)}, bf16[2,128,128]{2,1,0:T(8,128)(2,1)S(1)}, u32[]{:S(2)}, u32[]{:S(2)}) collective-permute-start(bf16[2,128,128]{2,1,0:T(8,128)(2,1)} %bitcast.28), channel_id=1, source_target_pairs={{16,0},{24,8},{0,16},{8,24},{17,1},{25,9},{1,17},{9,25},{18,2},{26... | collective-permute-start | bytes 196616 | tf_op jit(solution)/shard_map/ppermute | solution.py:306
  3.7 10.7 %collective-permute-start.3 = (bf16[2,128,128]{2,1,0:T(8,128)(2,1)}, bf16[2,128,128]{2,1,0:T(8,128)(2,1)S(1)}, u32[]{:S(2)}, u32[]{:S(2)}) collective-permute-start(bf16[2,128,128]{2,1,0:T(8,128)(2,1)} %bitcast.30), channel_id=1, source_target_pairs={{16,4},{17,5},{18,6},{19,7},{20,2},{21,3},{22,0},{23,1},{24,8},{25... | collective-permute-start | bytes 196616 | tf_op jit(solution)/shard_map/ppermute | solution.py:326
  7.2 7.3 %collective-permute-start.2 = (bf16[2,128,128]{2,1,0:T(8,128)(2,1)}, bf16[2,128,128]{2,1,0:T(8,128)(2,1)S(1)}, u32[]{:S(2)}, u32[]{:S(2)}) collective-permute-start(bf16[2,128,128]{2,1,0:T(8,128)(2,1)} %bitcast.31), channel_id=1, source_target_pairs={{8,4},{9,5},{10,6},{11,7},{12,2},{13,3},{14,0},{15,1},{0,8},{1,9},... | collective-permute-start | bytes 196616 | tf_op jit(solution)/shard_map/ppermute | solution.py:326
  7.2 8.2 %collective-permute-start.1 = (bf16[2,128,128]{2,1,0:T(8,128)(2,1)}, bf16[2,128,128]{2,1,0:T(8,128)(2,1)S(1)}, u32[]{:S(2)}, u32[]{:S(2)}) collective-permute-start(bf16[2,128,128]{2,1,0:T(8,128)(2,1)} %bitcast.32), channel_id=1, source_target_pairs={{24,4},{25,5},{26,6},{27,7},{28,2},{29,3},{30,0},{31,1},{16,8},{17... | collective-permute-start | bytes 196616 | tf_op jit(solution)/shard_map/ppermute | solution.py:326
  9.1 8.3 %collective-permute-start = (bf16[2,128,128]{2,1,0:T(8,128)(2,1)}, bf16[2,128,128]{2,1,0:T(8,128)(2,1)S(1)}, u32[]{:S(2)}, u32[]{:S(2)}) collective-permute-start(bf16[2,128,128]{2,1,0:T(8,128)(2,1)} %bitcast.33), channel_id=1, source_target_pairs={{0,4},{1,5},{2,6},{3,7},{4,2},{5,3},{6,0},{7,1},{8,8},{9,9},{10,10... | collective-permute-start | bytes 196616 | tf_op jit(solution)/shard_map/ppermute | solution.py:326
  14.3 5.0 %collective-permute-start.5 = (bf16[4,128,128]{2,1,0:T(8,128)(2,1)S(1)}, bf16[4,128,128]{2,1,0:T(8,128)(2,1)S(1)}, u32[]{:S(2)}, u32[]{:S(2)}) collective-permute-start(bf16[4,128,128]{2,1,0:T(8,128)(2,1)S(1)} %join.1.refs_0_), channel_id=1, source_target_pairs={{8,0},{0,8},{24,16},{16,24},{9,1},{1,9},{25,17},{17,25},{10,2},{2,... | collective-permute-start | bytes 393224 | tf_op jit(solution)/shard_map/ppermute | solution.py:306
  14.4 4.0 %collective-permute-start.9 = (bf16[1,2,128,128]{3,2,1,0:T(8,128)(2,1)S(1)}, bf16[1,2,128,128]{3,2,1,0:T(8,128)(2,1)S(1)}, u32[]{:S(2)}, u32[]{:S(2)}) collective-permute-start(bf16[1,2,128,128]{3,2,1,0:T(8,128)(2,1)S(1)} %bitcast.16), channel_id=1, source_target_pairs={{0,1},{1,0},{2,3},{3,2},{4,5},{5,4},{6,7},{7,6},{8,9},{9,8},{10,11... | collective-permute-start | bytes 196616 | tf_op jit(solution)/shard_map/ppermute | solution.py:328
  14.5 3.8 %collective-permute-start.8 = (bf16[1,2,128,128]{3,2,1,0:T(8,128)(2,1)S(1)}, bf16[1,2,128,128]{3,2,1,0:T(8,128)(2,1)S(1)}, u32[]{:S(2)}, u32[]{:S(2)}) collective-permute-start(bf16[1,2,128,128]{3,2,1,0:T(8,128)(2,1)S(1)} %bitcast.18), channel_id=1, source_target_pairs={{0,1},{1,0},{2,3},{3,2},{4,5},{5,4},{6,7},{7,6},{8,9},{9,8},{10,11... | collective-permute-start | bytes 196616 | tf_op jit(solution)/shard_map/ppermute | solution.py:328
  15.4 3.0 %collective-permute-start.7 = (bf16[1,2,128,128]{3,2,1,0:T(8,128)(2,1)S(1)}, bf16[1,2,128,128]{3,2,1,0:T(8,128)(2,1)S(1)}, u32[]{:S(2)}, u32[]{:S(2)}) collective-permute-start(bf16[1,2,128,128]{3,2,1,0:T(8,128)(2,1)S(1)} %bitcast.20), channel_id=1, source_target_pairs={{0,1},{1,0},{2,3},{3,2},{4,5},{5,4},{6,7},{7,6},{8,9},{9,8},{10,11... | collective-permute-start | bytes 196616 | tf_op jit(solution)/shard_map/ppermute | solution.py:328
  17.3 1.3 %collective-permute-start.6 = (bf16[1,2,128,128]{3,2,1,0:T(8,128)(2,1)S(1)}, bf16[1,2,128,128]{3,2,1,0:T(8,128)(2,1)S(1)}, u32[]{:S(2)}, u32[]{:S(2)}) collective-permute-start(bf16[1,2,128,128]{3,2,1,0:T(8,128)(2,1)S(1)} %bitcast.22), channel_id=1, source_target_pairs={{0,1},{1,0},{2,3},{3,2},{4,5},{5,4},{6,7},{7,6},{8,9},{9,8},{10,11... | collective-permute-start | bytes 196616 | tf_op jit(solution)/shard_map/ppermute | solution.py:328
  31.9 5.5 %collective-permute-start.12 = (bf16[2,128,128]{2,1,0:T(8,128)(2,1)S(1)}, bf16[2,128,128]{2,1,0:T(8,128)(2,1)S(1)}, u32[]{:S(2)}, u32[]{:S(2)}) collective-permute-start(bf16[2,128,128]{2,1,0:T(8,128)(2,1)S(1)} %get-tuple-element.14.refs_0_), channel_id=1, source_target_pairs={{24,0},{16,8},{8,16},{0,24},{25,1},{17,9},{9,17},{1,25},{26,2},{18... | collective-permute-start | bytes 196616 | tf_op jit(solution)/shard_map/ppermute | solution.py:306
  32.6 4.9 %collective-permute-start.11 = (bf16[2,128,128]{2,1,0:T(8,128)(2,1)S(1)}, bf16[2,128,128]{2,1,0:T(8,128)(2,1)S(1)}, u32[]{:S(2)}, u32[]{:S(2)}) collective-permute-start(bf16[2,128,128]{2,1,0:T(8,128)(2,1)S(1)} %get-tuple-element.14.refs_0_), channel_id=1, source_target_pairs={{8,0},{0,8},{24,16},{16,24},{9,1},{1,9},{25,17},{17,25},{10,2},{2,... | collective-permute-start | bytes 196616 | tf_op jit(solution)/shard_map/ppermute | solution.py:306
  34.0 4.3 %collective-permute-start.10 = (bf16[2,128,128]{2,1,0:T(8,128)(2,1)S(1)}, bf16[2,128,128]{2,1,0:T(8,128)(2,1)S(1)}, u32[]{:S(2)}, u32[]{:S(2)}) collective-permute-start(bf16[2,128,128]{2,1,0:T(8,128)(2,1)S(1)} %get-tuple-element.14.refs_0_), channel_id=1, source_target_pairs={{16,0},{24,8},{0,16},{8,24},{17,1},{25,9},{1,17},{9,25},{18,2},{26... | collective-permute-start | bytes 196616 | tf_op jit(solution)/shard_map/ppermute | solution.py:306
